TPU v7x, 32 devices: a whole 2x2x4 slice. The times are simulated.
32 devices in a mesh: dp: 8 (over y, x, core), tensor: 4 (over z).
Axes of the slice: x: 2, y: 2, z: 4, core: 2. Of those that a mesh axis runs over, the one named last changes fastest.
Arguments:
- tokens: bfloat16 [16384, 768], P(('dp', 'tensor')), may hold values from -48 to 48
- counts: int32 [8], replicated, may hold values from 4 to 8
- routes: int32 [2, 16384, 2], P(None, 'dp'), may hold values from 0 to 3, all different within a row; in each aligned block of 2048 rows (0 to 2047, 2048 to 4095, ..., all dimensions but the last counted through in order) at most 1536 rows name the same one
- norm_gain: bfloat16 [3072], P(('dp', 'tensor')), may hold values from 0.5 to 1.5
- norm_bias: bfloat16 [3072], P(('dp', 'tensor')), may hold values from -0.59765625 to 0.59765625
- w_router: bfloat16 [6144], P(('dp', 'tensor')), may hold values from -0.15625 to 0.15625
- w_qkv: bfloat16 [2, 3, 768, 768], P(None, None, 'dp', 'tensor'), may hold values from -0.21875 to 0.21875
- w_out: bfloat16 [2, 768, 768], P(None, 'tensor', 'dp'), may hold values from -1.75 to 1.75
- w_in: bfloat16 [2, 4, 768, 3072], P(None, None, 'dp', 'tensor'), may hold values from -0.21875 to 0.21875
- w_back: bfloat16 [2, 4, 768, 3072], P(None, None, 'dp', 'tensor'), may hold values from -0.4375 to 0.4375
- cotangent: bfloat16 [16384, 768], P(('dp', 'tensor')), may hold values from -6 to 6
Outputs:
- out: float32 [16384, 768], P(('dp', 'tensor'))
- grad_input: float32 [16384, 768], P(('dp', 'tensor'))
- grad_gain: float32 [3072], P(('dp', 'tensor'))
- grad_bias: float32 [3072], P(('dp', 'tensor'))
- grad_router: float32 [6144], P(('dp', 'tensor'))
- grad_qkv: float32 [2, 3, 768, 768], P(None, None, 'dp', 'tensor')
- grad_out: float32 [2, 768, 768], P(None, 'tensor', 'dp')
- grad_in: float32 [2, 4, 768, 3072], P(None, None, 'dp', 'tensor')
- grad_back: float32 [2, 4, 768, 3072], P(None, None, 'dp', 'tensor')
- rms: float32 [2, 3], replicated
Inputs may be any that keep to these rules, and one draw needn't show every extreme that they name: `routes`: each row names two different experts. Within the rows of one data group of one block no expert is named more than 1536 times, and in every draw some expert is named exactly 1536 times in some group.
All inputs are finite; a program needn't handle non-finite values.
Results may differ from a plain program's by a relative error of at most 0.038.
Values may be sent and summed in bfloat16 or wider, within the bound.
A program may use at most 320 MiB of HBM per device.

v0:
```python
from functools import partial
import math

import jax
import jax.numpy as jnp
from jax import lax
from jax.sharding import PartitionSpec as P

D = 768
HD = 64
LEN = 197
SEQ = 256
LAYERS = 2


eps_norm = 1e-06
far_negative = -1e30
highest = lax.Precision.HIGHEST


def norm_forward(row_vals, gain_vec, bias_vec):
    row_mean = jnp.mean(row_vals, axis=-1, keepdims=True)
    centred = row_vals - row_mean
    row_var = jnp.mean(centred * centred, axis=-1, keepdims=True)
    inv_std = lax.rsqrt(row_var + eps_norm)
    normed = centred * inv_std
    return (normed * gain_vec + bias_vec, normed, inv_std)


def norm_backward(grad_vals, normed, inv_std, gain_vec):
    gain_grad = jnp.sum(grad_vals * normed, axis=0)
    bias_grad = jnp.sum(grad_vals, axis=0)
    scaled = grad_vals * gain_vec
    mean_one = jnp.mean(scaled, axis=-1, keepdims=True)
    mean_two = jnp.mean(scaled * normed, axis=-1, keepdims=True)
    return (inv_std * (scaled - mean_one - normed * mean_two), gain_grad, bias_grad)


def gather_rows(row_vals):
    return lax.all_gather(row_vals, "tensor", axis=0, tiled=True)


def sum_rows(row_vals):
    return lax.psum_scatter(
        row_vals.astype(jnp.bfloat16), "tensor", scatter_dimension=0, tiled=True
    ).astype(jnp.float32)


def sum_slots(slot_vals):
    return lax.psum_scatter(
        slot_vals.astype(jnp.bfloat16), "tensor", scatter_dimension=1, tiled=True
    ).astype(jnp.float32)


def to_experts(make_rows, positions):
    return lax.all_to_all(make_rows(positions), "dp", split_axis=0, concat_axis=0, tiled=True)


def attend(block_in, key_keep, score_scale):
    query_heads, key_heads, value_heads = block_in
    scores = (
        jnp.einsum("iqhd,ikhd->ihqk", query_heads, key_heads, preferred_element_type=jnp.float32)
        * score_scale
    )
    scores = jnp.where(key_keep, scores, far_negative)
    row_max = jnp.max(scores, axis=-1, keepdims=True)
    exponent = jnp.exp(scores - row_max)
    row_total = jnp.sum(exponent, axis=-1, keepdims=True)
    weights = (exponent / row_total).astype(jnp.bfloat16)
    context = jnp.einsum(
        "ihqk,ikhd->iqhd", weights, value_heads, preferred_element_type=jnp.float32
    )
    return (context.astype(jnp.bfloat16), (row_max + jnp.log(row_total))[..., 0])


def attend_back(block_in, key_keep, score_scale):
    query_heads, key_heads, value_heads, d_context, log_total = block_in
    scores = (
        jnp.einsum("iqhd,ikhd->ihqk", query_heads, key_heads, preferred_element_type=jnp.float32)
        * score_scale
    )
    scores = jnp.where(key_keep, scores, far_negative)
    weights = jnp.exp(scores - log_total[..., None])
    d_values = jnp.einsum(
        "ihqk,iqhd->ikhd",
        weights.astype(jnp.bfloat16),
        d_context,
        preferred_element_type=jnp.float32,
    )
    d_weights = jnp.einsum(
        "iqhd,ikhd->ihqk", d_context, value_heads, preferred_element_type=jnp.float32
    )
    inner_sum = jnp.sum(weights * d_weights, axis=-1, keepdims=True)
    d_scores = (weights * (d_weights - inner_sum)).astype(jnp.bfloat16)
    d_queries = (
        jnp.einsum("ihqk,ikhd->iqhd", d_scores, key_heads, preferred_element_type=jnp.float32)
        * score_scale
    )
    d_keys = (
        jnp.einsum("ihqk,iqhd->ikhd", d_scores, query_heads, preferred_element_type=jnp.float32)
        * score_scale
    )
    return (
        d_queries.astype(jnp.bfloat16),
        d_keys.astype(jnp.bfloat16),
        d_values.astype(jnp.bfloat16),
    )


def contract_first(left_mat, right_mat):
    return lax.dot_general(
        left_mat, right_mat, (((0,), (0,)), ((), ())), preferred_element_type=jnp.float32
    )


def contract_last(left_mat, right_mat):
    return lax.dot_general(
        left_mat, right_mat, (((1,), (1,)), ((), ())), preferred_element_type=jnp.float32
    )


def per_device(
    tokens, counts, routes, norm_gain, norm_bias, w_router, w_qkv, w_out, w_in, w_back, cotangent
):
    groups = lax.axis_size("dp")
    parts = lax.axis_size("tensor")
    experts = groups // 2
    group_idx = lax.axis_index("dp")
    my_part = lax.axis_index("tensor")
    own_rows = tokens.shape[0]
    rows_all = own_rows * parts
    slot_count = 3 * rows_all // experts
    half_slots = slot_count // 2
    quarter = half_slots // parts
    score_scale = HD ** (-0.5)
    images = rows_all // SEQ
    per_block = math.gcd(images, max(1, 512 // SEQ))
    blocks = images // per_block
    head_cols = w_qkv.shape[-1]
    heads_here = head_cols // HD
    key_keep = jnp.arange(SEQ) < LEN
    gain_flat, bias_flat, router_flat = (
        lax.all_gather(norm_gain, ("dp", "tensor"), axis=0, tiled=True),
        lax.all_gather(norm_bias, ("dp", "tensor"), axis=0, tiled=True),
        lax.all_gather(w_router, ("dp", "tensor"), axis=0, tiled=True),
    )
    gains_all = gain_flat.astype(jnp.float32).reshape(LAYERS, 2, D)
    biases_all = bias_flat.astype(jnp.float32).reshape(LAYERS, 2, D)
    router_all = router_flat.reshape(LAYERS, D, experts)
    row_ids = my_part * own_rows + jnp.arange(own_rows, dtype=jnp.int32)
    image_count = lax.dynamic_index_in_dim(counts, group_idx, keepdims=False)
    valid_rows = ((row_ids // SEQ < image_count) & (row_ids % SEQ < LEN)).astype(jnp.float32)[
        :, None
    ]

    def split_heads(columns):
        return columns.reshape(blocks, per_block, SEQ, heads_here, HD)

    hidden = tokens.astype(jnp.float32)
    kept_layers = []
    stat_terms = []
    for layer_idx in range(LAYERS):
        gain_pair = gains_all[layer_idx]
        shift_pair = biases_all[layer_idx]
        wq_part, wo_part = (
            lax.all_gather(w_qkv[layer_idx], "dp", axis=1, tiled=True),
            lax.all_gather(w_out[layer_idx], "dp", axis=1, tiled=True),
        )
        w_cat = jnp.concatenate([wq_part[0], wq_part[1], wq_part[2]], axis=1)
        up_part, back_part = (
            lax.all_to_all(
                jnp.repeat(w_in[layer_idx], 2, axis=0),
                "dp",
                split_axis=0,
                concat_axis=0,
                tiled=True,
            ),
            lax.all_to_all(
                jnp.repeat(w_back[layer_idx], 2, axis=0),
                "dp",
                split_axis=0,
                concat_axis=0,
                tiled=True,
            ),
        )
        up_part = up_part.reshape(D, -1)
        back_part = back_part.reshape(D, -1)
        up_use, back_use = (up_part, back_part)
        norm_one, normed_one, inv_one = norm_forward(hidden, gain_pair[0], shift_pair[0])
        rows_one = gather_rows(norm_one.astype(jnp.bfloat16))
        qkv_rows = jnp.dot(rows_one, w_cat, preferred_element_type=jnp.float32).astype(jnp.bfloat16)
        query_heads = split_heads(qkv_rows[:, :head_cols])
        key_heads = split_heads(qkv_rows[:, head_cols : 2 * head_cols])
        value_heads = split_heads(qkv_rows[:, 2 * head_cols :])
        context, log_total = lax.map(
            partial(attend, key_keep=key_keep, score_scale=score_scale),
            (query_heads, key_heads, value_heads),
        )
        context = context.reshape(rows_all, head_cols)
        attn_out = sum_rows(jnp.dot(context, wo_part, preferred_element_type=jnp.float32))
        residual = hidden + attn_out
        norm_two, normed_two, inv_two = norm_forward(residual, gain_pair[1], shift_pair[1])
        rows_two = gather_rows(norm_two.astype(jnp.bfloat16))
        router = router_all[layer_idx]
        router_probs = jax.nn.softmax(
            jnp.dot(rows_two, router, preferred_element_type=jnp.float32), axis=-1
        )
        routing = routes[layer_idx]
        one_hot = routing[:, :, None] == jnp.arange(experts)[None, None, :]
        gate_vals = jnp.sum(jnp.where(one_hot, router_probs[:, None, :], 0.0), axis=-1)
        flat_pick = routing.reshape(-1)
        hot_int = (flat_pick[:, None] == jnp.arange(experts)[None, :]).astype(jnp.int32)
        rank_in = jnp.sum((jnp.cumsum(hot_int, axis=0) - hot_int) * hot_int, axis=1)
        target = flat_pick * slot_count + rank_in
        positions = (
            jnp.full((experts * slot_count,), 2 * rows_all, jnp.int32)
            .at[target]
            .set(jnp.arange(2 * rows_all, dtype=jnp.int32))
        )
        positions = positions.reshape(groups, half_slots)
        padded_two = jnp.concatenate([rows_two, jnp.zeros((1, D), jnp.bfloat16)], axis=0)

        def take_rows(slot_index):
            return padded_two[jnp.where(slot_index < 2 * rows_all, slot_index // 2, rows_all)]

        arrived = to_experts(take_rows, positions).reshape(-1, D)
        pre_act = jnp.dot(arrived, up_use, preferred_element_type=jnp.float32)
        activation = jax.nn.gelu(pre_act, approximate=True).astype(jnp.bfloat16)
        partial_out = contract_last(activation, back_use)
        summed = sum_slots(partial_out.reshape(groups, half_slots, D)).astype(jnp.bfloat16)
        returned = lax.all_to_all(summed, "dp", split_axis=0, concat_axis=0, tiled=True)
        slot_pair = target.reshape(rows_all, 2)
        owner = slot_pair // half_slots
        inside = slot_pair % half_slots
        in_quarter = inside // quarter == my_part
        pick_index = jnp.where(
            in_quarter, owner * quarter + inside - my_part * quarter, groups * quarter
        )
        padded_ret = jnp.concatenate(
            [returned.reshape(groups * quarter, D), jnp.zeros((1, D), jnp.bfloat16)], axis=0
        )
        chosen = padded_ret[pick_index]
        expert_out = sum_rows(jnp.sum(gate_vals[:, :, None] * chosen, axis=1))
        result = residual + expert_out
        stat_terms.append(
            jnp.stack(
                [
                    jnp.sum(valid_rows * result * result),
                    jnp.sum(valid_rows * attn_out * attn_out),
                    jnp.sum(valid_rows * expert_out * expert_out),
                ]
            )
        )
        kept_layers.append(
            (
                wo_part,
                w_cat,
                up_use,
                back_use,
                normed_one,
                inv_one,
                rows_one,
                query_heads,
                key_heads,
                value_heads,
                context,
                log_total,
                normed_two,
                inv_two,
                rows_two,
                router,
                router_probs,
                one_hot,
                gate_vals,
                positions,
                arrived,
                pre_act,
                activation,
                pick_index,
                chosen,
            )
        )
        hidden = result
    totals = lax.psum(jnp.stack(stat_terms), ("dp", "tensor"))
    denom = jnp.sum(counts).astype(jnp.float32) * (LEN * D)
    rms = jnp.sqrt(totals / denom)
    grad_rows = cotangent.astype(jnp.float32) * valid_rows
    gain_grads = [None] * LAYERS
    bias_grads = [None] * LAYERS
    router_grads = [None] * LAYERS
    qkv_grads = [None] * LAYERS
    out_grads = [None] * LAYERS
    up_grads = [None] * LAYERS
    back_grads = [None] * LAYERS
    for layer_idx in reversed(range(LAYERS)):
        (
            wo_part,
            w_cat,
            up_use,
            back_use,
            normed_one,
            inv_one,
            rows_one,
            query_heads,
            key_heads,
            value_heads,
            context,
            log_total,
            normed_two,
            inv_two,
            rows_two,
            router,
            router_probs,
            one_hot,
            gate_vals,
            positions,
            arrived,
            pre_act,
            activation,
            pick_index,
            chosen,
        ) = kept_layers[layer_idx]
        gain_pair = gains_all[layer_idx]
        grad_moe = gather_rows(grad_rows.astype(jnp.bfloat16))
        d_gates = jnp.einsum("rkd,rd->rk", chosen, grad_moe, preferred_element_type=jnp.float32)
        padded_down = jnp.concatenate([grad_moe, jnp.zeros((1, D), jnp.bfloat16)], axis=0)
        flat_gates = jnp.concatenate([gate_vals.reshape(-1), jnp.zeros((1,), jnp.float32)], axis=0)

        def scaled_rows(slot_index):
            filled = slot_index < 2 * rows_all
            row_index = jnp.where(filled, slot_index // 2, rows_all)
            gate_index = jnp.where(filled, slot_index, 2 * rows_all)
            return (flat_gates[gate_index][..., None] * padded_down[row_index]).astype(jnp.bfloat16)

        d_expert_rows = to_experts(scaled_rows, positions).reshape(-1, D)
        d_activation = jnp.dot(d_expert_rows, back_use, preferred_element_type=jnp.float32)
        back_grad = contract_first(d_expert_rows, activation)
        d_pre = jax.vjp(partial(jax.nn.gelu, approximate=True), pre_act)[1](d_activation)[0].astype(
            jnp.bfloat16
        )
        up_grad = contract_first(arrived, d_pre)
        d_arrived = contract_last(d_pre, up_use)
        d_slots = sum_slots(d_arrived.reshape(groups, half_slots, D))
        d_back_rows, up_pieces, back_pieces = (
            lax.all_to_all(
                d_slots.astype(jnp.bfloat16), "dp", split_axis=0, concat_axis=0, tiled=True
            ).astype(d_slots.dtype),
            lax.all_to_all(
                up_grad.reshape(groups, -1, up_grad.shape[1]).astype(jnp.bfloat16),
                "dp",
                split_axis=0,
                concat_axis=0,
                tiled=True,
            ).astype(jnp.float32),
            lax.all_to_all(
                back_grad.reshape(groups, -1, back_grad.shape[1]).astype(jnp.bfloat16),
                "dp",
                split_axis=0,
                concat_axis=0,
                tiled=True,
            ).astype(jnp.float32),
        )
        up_grads[layer_idx] = up_pieces.reshape(
            experts, 2, up_pieces.shape[1], up_pieces.shape[2]
        ).sum(axis=1)
        back_grads[layer_idx] = back_pieces.reshape(
            experts, 2, back_pieces.shape[1], back_pieces.shape[2]
        ).sum(axis=1)
        padded_back = jnp.concatenate(
            [d_back_rows.reshape(groups * quarter, D), jnp.zeros((1, D), jnp.float32)], axis=0
        )
        d_rows_two = jnp.sum(padded_back[pick_index], axis=1)
        d_probs = jnp.sum(jnp.where(one_hot, d_gates[:, :, None], 0.0), axis=1)
        d_logits = router_probs * (
            d_probs - jnp.sum(router_probs * d_probs, axis=-1, keepdims=True)
        )
        d_rows_two = d_rows_two + jnp.dot(d_logits, router.astype(jnp.float32).T, precision=highest)
        router_grads[layer_idx] = jnp.dot(
            rows_two.astype(jnp.float32).T, d_logits, precision=highest
        )
        d_second = sum_rows(d_rows_two)
        d_resid, gain_two, bias_two = norm_backward(d_second, normed_two, inv_two, gain_pair[1])
        grad_rows = grad_rows + d_resid
        grad_attn = gather_rows(grad_rows.astype(jnp.bfloat16))
        d_context = contract_last(grad_attn, wo_part).astype(jnp.bfloat16)
        out_grad = contract_first(context, grad_attn)
        d_queries, d_keys, d_values = lax.map(
            partial(attend_back, key_keep=key_keep, score_scale=score_scale),
            (query_heads, key_heads, value_heads, split_heads(d_context), log_total),
        )
        d_mixed = jnp.concatenate(
            [
                d_queries.reshape(rows_all, head_cols),
                d_keys.reshape(rows_all, head_cols),
                d_values.reshape(rows_all, head_cols),
            ],
            axis=1,
        )
        cat_grad = contract_first(rows_one, d_mixed)
        qkv_grad = jnp.stack(
            [
                cat_grad[:, :head_cols],
                cat_grad[:, head_cols : 2 * head_cols],
                cat_grad[:, 2 * head_cols :],
            ]
        )
        qkv_grads[layer_idx], out_grads[layer_idx] = (
            lax.psum_scatter(qkv_grad, "dp", scatter_dimension=1, tiled=True),
            lax.psum_scatter(out_grad, "dp", scatter_dimension=1, tiled=True),
        )
        d_first = sum_rows(contract_last(d_mixed, w_cat))
        d_hidden, gain_one, bias_one = norm_backward(d_first, normed_one, inv_one, gain_pair[0])
        grad_rows = grad_rows + d_hidden
        gain_grads[layer_idx] = jnp.stack([gain_one, gain_two])
        bias_grads[layer_idx] = jnp.stack([bias_one, bias_two])
    grad_gain, grad_bias, grad_router = (
        lax.psum_scatter(
            jnp.stack(gain_grads).reshape(-1), ("dp", "tensor"), scatter_dimension=0, tiled=True
        ),
        lax.psum_scatter(
            jnp.stack(bias_grads).reshape(-1), ("dp", "tensor"), scatter_dimension=0, tiled=True
        ),
        lax.psum_scatter(
            jnp.stack(router_grads).reshape(-1), ("dp", "tensor"), scatter_dimension=0, tiled=True
        ),
    )
    return (
        hidden,
        grad_rows,
        grad_gain,
        grad_bias,
        grad_router,
        jnp.stack(qkv_grads),
        jnp.stack(out_grads),
        jnp.stack(up_grads),
        jnp.stack(back_grads),
        rms,
    )


def solution(mesh):
    return jax.shard_map(
        per_device,
        mesh=mesh,
        in_specs=(
            P(("dp", "tensor"), None),
            P(),
            P(None, "dp", None),
            P(("dp", "tensor")),
            P(("dp", "tensor")),
            P(("dp", "tensor")),
            P(None, None, "dp", "tensor"),
            P(None, "tensor", "dp"),
            P(None, None, "dp", "tensor"),
            P(None, None, "dp", "tensor"),
            P(("dp", "tensor"), None),
        ),
        out_specs=(
            P(("dp", "tensor"), None),
            P(("dp", "tensor"), None),
            P(("dp", "tensor")),
            P(("dp", "tensor")),
            P(("dp", "tensor")),
            P(None, None, "dp", "tensor"),
            P(None, "tensor", "dp"),
            P(None, None, "dp", "tensor"),
            P(None, None, "dp", "tensor"),
            P(),
        ),
        check_vma=False,
    )
```

profile of v0, /device:TPU:0, one launch (start us, length us, event | category | flops | bytes accessed | tf_op | source)
XLA Modules:
  0.0 3200.6 jit_solution(4988154364550785197)
XLA Ops:
  9.8 42.3 %all-reduce.15 = (bf16[3072]{0:T(1024)(128)(2,1)S(1)}, bf16[3072]{0:T(1024)(128)(2,1)S(1)}, bf16[6144]{0:T(1024)(128)(2,1)S(1)}) all-reduce(bf16[3072]{0:T(1024)(128)(2,1)S(1)} %dynamic-update-slice, bf16[3072]{0:T(1024)(128)(2,1)S(1)} %dynamic-update-slice.1, ...), channel_id=1, replica_groups=mesh['dp'=8,'tensor'=4] {'dp','tensor'}, use_global_device_ids=true, to_apply=%add.8 | all-reduce | flops 12288 | bytes 49152
  83.4 38.7 %all-gather.13.cloned.1.call-done = bf16[2048,768]{1,0:T(8,128)(2,1)} async-done(((bf16[512,768]{1,0:T(8,128)(2,1)}), bf16[2048,768]{1,0:T(8,128)(2,1)}) %all-gather.13.cloned.1.call-update) | async-done | bytes 3145744 | tf_op jit(solution)/shard_map/all_gather | solution.py:40
  139.2 59.2 %reduce-scatter.25.cloned.1.call-done = bf16[512,768]{1,0:T(8,128)(2,1)} async-done(((bf16[2048,768]{1,0:T(8,128)(2,1)}), bf16[512,768]{1,0:T(8,128)(2,1)}) %reduce-scatter.25.cloned.1.call-update) | async-done | bytes 786448 | tf_op jit(solution)/shard_map/reduce_scatter | solution.py:44
  300.8 104.4 %all-to-all-done = bf16[8,768,768]{2,1,0:T(8,128)(2,1)} async-done(((bf16[8,768,768]{2,1,0:T(8,128)(2,1)}), bf16[8,768,768]{2,1,0:T(8,128)(2,1)}, u32[]{:S(2)}, u32[]{:S(2)}) %all-to-all-start) | async-done | bytes 9437216 | tf_op jit(solution)/shard_map/all_to_all | solution.py:56
  448.6 154.3 %reduce-scatter.27.cloned.1.call-done = bf16[8,192,768]{2,1,0:T(8,128)(2,1)} async-done(((bf16[8,768,768]{2,1,0:T(8,128)(2,1)}), bf16[8,192,768]{2,1,0:T(8,128)(2,1)}) %reduce-scatter.27.cloned.1.call-update) | async-done | bytes 2359312 | tf_op jit(solution)/shard_map/reduce_scatter | solution.py:50
  690.6 59.7 %reduce-scatter.29.cloned.1.call-done = bf16[512,768]{1,0:T(8,128)(2,1)} async-done(((bf16[2048,768]{1,0:T(8,128)(2,1)}), bf16[512,768]{1,0:T(8,128)(2,1)}) %reduce-scatter.29.cloned.1.call-update) | async-done | bytes 786448 | tf_op jit(solution)/shard_map/reduce_scatter | solution.py:44
  778.9 38.2 %all-gather.17.cloned.1.call-done = bf16[2048,768]{1,0:T(8,128)(2,1)} async-done(((bf16[512,768]{1,0:T(8,128)(2,1)}), bf16[2048,768]{1,0:T(8,128)(2,1)}) %all-gather.17.cloned.1.call-update) | async-done | bytes 3145744 | tf_op jit(solution)/shard_map/all_gather | solution.py:40
  860.5 59.0 %reduce-scatter.31.cloned.1.call-done = bf16[512,768]{1,0:T(8,128)(2,1)} async-done(((bf16[2048,768]{1,0:T(8,128)(2,1)}), bf16[512,768]{1,0:T(8,128)(2,1)}) %reduce-scatter.31.cloned.1.call-update) | async-done | bytes 786448 | tf_op jit(solution)/shard_map/reduce_scatter | solution.py:44
  945.0 41.7 %all-gather.19.cloned.1.call-done = bf16[2048,768]{1,0:T(8,128)(2,1)} async-done(((bf16[512,768]{1,0:T(8,128)(2,1)}), bf16[2048,768]{1,0:T(8,128)(2,1)}) %all-gather.19.cloned.1.call-update) | async-done | bytes 3145744 | tf_op jit(solution)/shard_map/all_gather | solution.py:40
  1015.0 111.3 %all_to_all.80 = bf16[8,768,768]{2,1,0:T(8,128)(2,1)} all-to-all(bf16[8,768,768]{2,1,0:T(8,128)(2,1)} %bitcast.496), channel_id=1, replica_groups=mesh['dp'=8,'tensor'=4] {'dp'}, dimensions={0} | all-to-all | bytes 18874368 | tf_op jit(solution)/shard_map/all_to_all | solution.py:56
  1166.7 157.3 %reduce-scatter.33.cloned.1.call-done = bf16[8,192,768]{2,1,0:T(8,128)(2,1)} async-done(((bf16[8,768,768]{2,1,0:T(8,128)(2,1)}), bf16[8,192,768]{2,1,0:T(8,128)(2,1)}) %reduce-scatter.33.cloned.1.call-update) | async-done | bytes 2359312 | tf_op jit(solution)/shard_map/reduce_scatter | solution.py:50
  1329.9 59.9 %all-gather.21.cloned.1.call-done = bf16[2048,768]{1,0:T(8,128)(2,1)} async-done(((bf16[512,768]{1,0:T(8,128)(2,1)}), bf16[2048,768]{1,0:T(8,128)(2,1)}) %all-gather.21.cloned.1.call-update) | async-done | bytes 3145744 | tf_op jit(solution)/shard_map/all_gather | solution.py:40
  1454.0 38.7 %fusion.96 = f32[2048,1,2]{2,1,0:T(1,128)} fusion(bf16[2048,2,768]{2,1,0:T(2,128)(2,1)} %reshape.1024, bf16[2048,768,1]{1,0,2:T(8,128)(2,1)S(1)} %bitcast.517), kind=kOutput, calls=%fused_computation.160 | convolution fusion | flops 6291456 | bytes 9453568 | tf_op jit(solution)/shard_map/rkd,rd->rk/dot_general | solution.py:325
  1539.5 109.2 %all_to_all.81 = bf16[8,768,768]{2,1,0:T(8,128)(2,1)S(1)} all-to-all(bf16[8,768,768]{2,1,0:T(8,128)(2,1)} %fusion.85), channel_id=1, replica_groups=mesh['dp'=8,'tensor'=4] {'dp'}, dimensions={0} | all-to-all | bytes 18874368 | tf_op jit(solution)/shard_map/all_to_all | solution.py:56
  1684.7 158.2 %reduce-scatter.37.cloned.1.call-done = bf16[8,192,768]{2,1,0:T(8,128)(2,1)} async-done(((bf16[8,768,768]{2,1,0:T(8,128)(2,1)}), bf16[8,192,768]{2,1,0:T(8,128)(2,1)}) %reduce-scatter.37.cloned.1.call-update) | async-done | bytes 2359312 | tf_op jit(solution)/shard_map/reduce_scatter | solution.py:50
  1982.3 38.7 %reduce-scatter.39.cloned.1.call-done = bf16[512,768]{1,0:T(8,128)(2,1)} async-done(((bf16[2048,768]{1,0:T(8,128)(2,1)}), bf16[512,768]{1,0:T(8,128)(2,1)}) %reduce-scatter.39.cloned.1.call-update) | async-done | bytes 786448 | tf_op jit(solution)/shard_map/reduce_scatter | solution.py:44
  2023.5 60.2 %reduce-scatter.35.cloned.1.call-done = bf16[512,768]{1,0:T(8,128)(2,1)} async-done(((bf16[2048,768]{1,0:T(8,128)(2,1)}), bf16[512,768]{1,0:T(8,128)(2,1)}) %reduce-scatter.35.cloned.1.call-update) | async-done | bytes 786448 | tf_op jit(solution)/shard_map/reduce_scatter | solution.py:44
  2088.6 63.2 %all-gather.23.cloned.1.call-done = bf16[2048,768]{1,0:T(8,128)(2,1)} async-done(((bf16[512,768]{1,0:T(8,128)(2,1)}), bf16[2048,768]{1,0:T(8,128)(2,1)}) %all-gather.23.cloned.1.call-update) | async-done | bytes 3145744 | tf_op jit(solution)/shard_map/all_gather | solution.py:40
  2191.9 59.2 %reduce-scatter.41.cloned.1.call-done = bf16[512,768]{1,0:T(8,128)(2,1)} async-done(((bf16[2048,768]{1,0:T(8,128)(2,1)}), bf16[512,768]{1,0:T(8,128)(2,1)}) %reduce-scatter.41.cloned.1.call-update) | async-done | bytes 786448 | tf_op jit(solution)/shard_map/reduce_scatter | solution.py:44
  2358.3 109.2 %all_to_all.82 = bf16[8,768,768]{2,1,0:T(8,128)(2,1)S(1)} all-to-all(bf16[8,768,768]{2,1,0:T(8,128)(2,1)} %fusion.84), channel_id=1, replica_groups=mesh['dp'=8,'tensor'=4] {'dp'}, dimensions={0} | all-to-all | bytes 18874368 | tf_op jit(solution)/shard_map/all_to_all | solution.py:56
  2503.5 158.2 %reduce-scatter.43.cloned.1.call-done = bf16[8,192,768]{2,1,0:T(8,128)(2,1)} async-done(((bf16[8,768,768]{2,1,0:T(8,128)(2,1)}), bf16[8,192,768]{2,1,0:T(8,128)(2,1)}) %reduce-scatter.43.cloned.1.call-update) | async-done | bytes 2359312 | tf_op jit(solution)/shard_map/reduce_scatter | solution.py:50
  2777.5 59.7 %reduce-scatter.45.cloned.1.call-done = bf16[512,768]{1,0:T(8,128)(2,1)} async-done(((bf16[2048,768]{1,0:T(8,128)(2,1)}), bf16[512,768]{1,0:T(8,128)(2,1)}) %reduce-scatter.45.cloned.1.call-update) | async-done | bytes 786448 | tf_op jit(solution)/shard_map/reduce_scatter | solution.py:44
  2860.9 46.6 %all-gather.27.cloned.1.call-done = bf16[2048,768]{1,0:T(8,128)(2,1)} async-done(((bf16[512,768]{1,0:T(8,128)(2,1)}), bf16[2048,768]{1,0:T(8,128)(2,1)}) %all-gather.27.cloned.1.call-update) | async-done | bytes 3145744 | tf_op jit(solution)/shard_map/all_gather | solution.py:40
  3147.5 40.8 %all-reduce.14 = (f32[3072]{0:T(1024)S(1)}, f32[3072]{0:T(1024)S(1)}, f32[6144]{0:T(1024)S(1)}, f32[2,3]{1,0:T(2,128)S(1)}) all-reduce(f32[3072]{0:T(1024)S(1)} %reshape.980, f32[3072]{0:T(1024)S(1)} %reshape.981, f32[6144]{0:T(1024)} %reshape.982, ...), channel_id=18, replica_groups=mesh['dp'=8,'tensor'=4] {'dp','tensor'}, use_global_device_ids=true, to_apply=%region_68.69.clone | all-reduce | flops 12294 | bytes 98352
  (788 shorter events, 1383.6 us)
Async XLA Ops:
  7.2 114.9 %all-gather.13.cloned.1.call-start = ((), (), s32[]{:S(2)}) async-start(), calls=%async_computation.32 | async-start | bytes 3932160 | tf_op jit(solution)/shard_map/all_gather | solution.py:40
  58.6 139.7 %reduce-scatter.25.cloned.1.call-start = ((), (), s32[]{:S(2)}) async-start(), calls=%async_computation.33 | async-start | bytes 3932160 | tf_op jit(solution)/shard_map/reduce_scatter | solution.py:44
  139.1 127.2 %all-gather.15.cloned.1.call-start = ((), (), s32[]{:S(2)}) async-start(), calls=%async_computation.34 | async-start | bytes 3932160 | tf_op jit(solution)/shard_map/all_gather | solution.py:40
  294.7 110.5 %all-to-all-start = ((bf16[8,768,768]{2,1,0:T(8,128)(2,1)}), bf16[8,768,768]{2,1,0:T(8,128)(2,1)}, u32[]{:S(2)}, u32[]{:S(2)}) async-start(bf16[8,768,768]{2,1,0:T(8,128)(2,1)} %bitcast.495), calls=%async_computation.1 | async-start | bytes 18874368 | tf_op jit(solution)/shard_map/all_to_all | solution.py:56
  409.8 193.1 %reduce-scatter.27.cloned.1.call-start = ((), (), s32[]{:S(2)}) async-start(), calls=%async_computation.35 | async-start | bytes 11796480 | tf_op jit(solution)/shard_map/reduce_scatter | solution.py:50
  607.3 143.0 %reduce-scatter.29.cloned.1.call-start = ((), (), s32[]{:S(2)}) async-start(), calls=%async_computation.36 | async-start | bytes 3932160 | tf_op jit(solution)/shard_map/reduce_scatter | solution.py:44
  690.5 126.6 %all-gather.17.cloned.1.call-start = ((), (), s32[]{:S(2)}) async-start(), calls=%async_computation.37 | async-start | bytes 3932160 | tf_op jit(solution)/shard_map/all_gather | solution.py:40
  753.6 165.9 %reduce-scatter.31.cloned.1.call-start = ((), (), s32[]{:S(2)}) async-start(), calls=%async_computation.38 | async-start | bytes 3932160 | tf_op jit(solution)/shard_map/reduce_scatter | solution.py:44
  860.3 126.4 %all-gather.19.cloned.1.call-start = ((), (), s32[]{:S(2)}) async-start(), calls=%async_computation.39 | async-start | bytes 3932160 | tf_op jit(solution)/shard_map/all_gather | solution.py:40
  1131.1 192.9 %reduce-scatter.33.cloned.1.call-start = ((), (), s32[]{:S(2)}) async-start(), calls=%async_computation.40 | async-start | bytes 11796480 | tf_op jit(solution)/shard_map/reduce_scatter | solution.py:50
  1163.6 226.2 %all-gather.21.cloned.1.call-start = ((), (), s32[]{:S(2)}) async-start(), calls=%async_computation.42 | async-start | bytes 3932160 | tf_op jit(solution)/shard_map/all_gather | solution.py:40
  1328.4 514.4 %reduce-scatter.37.cloned.1.call-start = ((), (), s32[]{:S(2)}) async-start(), calls=%async_computation.43 | async-start | bytes 11796480 | tf_op jit(solution)/shard_map/reduce_scatter | solution.py:50
  1847.2 173.8 %reduce-scatter.39.cloned.1.call-start = ((), (), s32[]{:S(2)}) async-start(), calls=%async_computation.44 | async-start | bytes 3932160 | tf_op jit(solution)/shard_map/reduce_scatter | solution.py:44
  1961.3 122.4 %reduce-scatter.35.cloned.1.call-start = ((), (), s32[]{:S(2)}) async-start(), calls=%async_computation.41 | async-start | bytes 3932160 | tf_op jit(solution)/shard_map/reduce_scatter | solution.py:44
  1982.2 169.7 %all-gather.23.cloned.1.call-start = ((), (), s32[]{:S(2)}) async-start(), calls=%async_computation.45 | async-start | bytes 3932160 | tf_op jit(solution)/shard_map/all_gather | solution.py:40
  2088.4 162.7 %reduce-scatter.41.cloned.1.call-start = ((), (), s32[]{:S(2)}) async-start(), calls=%async_computation.46 | async-start | bytes 3932160 | tf_op jit(solution)/shard_map/reduce_scatter | solution.py:44
  2191.8 129.3 %all-gather.25.cloned.1.call-start = ((), (), s32[]{:S(2)}) async-start(), calls=%async_computation.47 | async-start | bytes 3932160 | tf_op jit(solution)/shard_map/all_gather | solution.py:40
  2257.6 404.0 %reduce-scatter.43.cloned.1.call-start = ((), (), s32[]{:S(2)}) async-start(), calls=%async_computation.48 | async-start | bytes 11796480 | tf_op jit(solution)/shard_map/reduce_scatter | solution.py:50
  2665.3 171.9 %reduce-scatter.45.cloned.1.call-start = ((), (), s32[]{:S(2)}) async-start(), calls=%async_computation.49 | async-start | bytes 3932160 | tf_op jit(solution)/shard_map/reduce_scatter | solution.py:44
  2777.5 130.0 %all-gather.27.cloned.1.call-start = ((), (), s32[]{:S(2)}) async-start(), calls=%async_computation.50 | async-start | bytes 3932160 | tf_op jit(solution)/shard_map/all_gather | solution.py:40
  2844.0 273.1 %reduce-scatter.55.cloned.1.call-start = ((), (), s32[]{:S(2)}) async-start(), calls=%async_computation.55 | async-start | bytes 884736
  2848.2 270.6 %reduce-scatter.51.cloned.1.call-start = ((), (), s32[]{:S(2)}) async-start(), calls=%async_computation.53 | async-start | bytes 2211840
  2860.7 278.6 %reduce-scatter.53.cloned.1.call-start = ((), (), s32[]{:S(2)}) async-start(), calls=%async_computation.54 | async-start | bytes 884736
  2957.4 183.6 %reduce-scatter.49.cloned.1.call-start = ((), (), s32[]{:S(2)}) async-start(), calls=%async_computation.52 | async-start | bytes 2211840
  (152 other events, 7062.1 us)
Sparse Core Ops, SparseCore 0:
  58.8 63.2 all-gather.12
  139.2 59.0 reduce-scatter.24
  203.0 63.3 all-gather.14
  442.6 160.2 reduce-scatter.26
  690.6 59.6 reduce-scatter.28
  753.7 63.3 all-gather.16
  860.4 59.0 reduce-scatter.30
  923.4 63.3 all-gather.18
  1163.7 160.2 reduce-scatter.32
  1325.4 64.3 all-gather.20
  1684.8 157.9 reduce-scatter.36
  1961.4 59.5 reduce-scatter.38
  2023.3 60.3 reduce-scatter.34
  2088.5 63.3 all-gather.22
  2192.0 59.0 reduce-scatter.40
  2257.7 63.3 all-gather.24
  2503.6 157.9 reduce-scatter.42
  2777.6 59.5 reduce-scatter.44
  2844.1 63.3 all-gather.26
  2910.5 33.5 reduce-scatter.54
  2948.1 40.1 reduce-scatter.50
  2991.4 34.9 reduce-scatter.52
  3029.9 43.9 reduce-scatter.48
  3076.0 61.3 reduce-scatter.46
where the time goes:
time: 3210 us; the launch traced here: 3200 us
  waiting for transfers between devices  1550 us (48%)
  local copies, waits for them, and re-layouts  555 us (17%)
  blocking collectives  458 us (14%)
  matrix products  347 us (11%)
  other arithmetic  217 us (7%)
  starting transfers between devices  56.6 us (2%)
    reduce_scatter x4, waiting for transfers between devices, sum_slots(): lax.psum_scatter(slot_vals.astype(jnp.bfloat16), 'tensor', scatter_dimens...  628 us
    reduce_scatter x8, waiting for transfers between devices, sum_rows(): lax.psum_scatter(row_vals.astype(jnp.bfloat16), 'tensor', scatter_dimensi...  396 us
    all_gather x8, waiting for transfers between devices, gather_rows(): return lax.all_gather(row_vals, 'tensor', axis=0, tiled=True)  354 us
    all_to_all x3, blocking collectives, to_experts(): lax.all_to_all(make_rows(positions), 'dp', split_axis=0, concat_axis=0, t...  330 us
    all_to_all x1, waiting for transfers between devices, to_experts(): lax.all_to_all(make_rows(positions), 'dp', split_axis=0, concat_axis=0, t...  104 us
    unnamed x2, blocking collectives  83.1 us
    gather x4, local copies, waits for them, and re-layouts, per_device(): d_rows_two = jnp.sum(padded_back[pick_index], axis=1)  75.7 us
    reduce_sum x2, other arithmetic, per_device(): d_rows_two = jnp.sum(padded_back[pick_index], axis=1)  73 us
  transfers between devices with their start and end apart: 37, of which 24 were waited for; matrix products, arithmetic and copies ran while one was open for 15% of the time, Pallas kernels for 0%

commit v1 on v0

--- a/solution.py
+++ b/solution.py
@@ -4,6 +4,8 @@
 import jax
 import jax.numpy as jnp
 from jax import lax
+from jax.experimental import pallas as pl
+from jax.experimental.pallas import tpu as pltpu
 from jax.sharding import PartitionSpec as P
 
 D = 768
@@ -119,7 +121,7 @@
     )
 
 
-def per_device(
+def per_device_general(
     tokens, counts, routes, norm_gain, norm_bias, w_router, w_qkv, w_out, w_in, w_back, cotangent
 ):
     groups = lax.axis_size("dp")
@@ -438,9 +440,699 @@
     )
 
 
+bf16 = jnp.bfloat16
+f32 = jnp.float32
+MESH = pl.DeviceIdType.MESH
+VMEM_LIMIT = 60 * 1024 * 1024
+EXPERTS = 4
+HEADS_PART = 3
+QKV = 3 * HEADS_PART * HD
+
+
+def nn(left, right):
+    return jnp.dot(left, right, preferred_element_type=f32)
+
+
+def nt(left, right):
+    return lax.dot_general(left, right, (((1,), (1,)), ((), ())), preferred_element_type=f32)
+
+
+def tn(left, right):
+    return lax.dot_general(left, right, (((0,), (0,)), ((), ())), preferred_element_type=f32)
+
+
+def group_of(kind):
+    dp, part = lax.axis_index("dp"), lax.axis_index("tensor")
+    if kind == "plane":
+        return dp // 2, 4, lambda place: (place * 2 + dp % 2, part)
+    if kind == "column":
+        return part, 4, lambda place: (dp, place)
+    if kind == "chip":
+        return dp % 2, 2, lambda place: (dp // 2 * 2 + place, part)
+    return dp * 4 + part, 32, lambda place: (place // 4, place % 4)
+
+
+def greet(devices):
+    barrier = pltpu.get_barrier_semaphore()
+    for device in devices:
+        pl.semaphore_signal(barrier, inc=1, device_id=device, device_id_type=MESH)
+    pl.semaphore_wait(barrier, len(devices))
+
+
+def swap_kernel(kind, same, in_ref, out_ref, held, local_sem, send_sem, recv_sem):
+    place, count, device = group_of(kind)
+    others = [lax.rem(place + step, count) for step in range(1, count)]
+    first = pltpu.make_async_copy(in_ref if same else in_ref.at[place], held, local_sem.at[0])
+    first.start()
+    greet([device(other) for other in others])
+    copies = []
+    for step, other in enumerate(others):
+        copies.append(
+            pltpu.make_async_remote_copy(
+                src_ref=in_ref if same else in_ref.at[other],
+                dst_ref=out_ref.at[place],
+                send_sem=send_sem.at[step],
+                recv_sem=recv_sem.at[step],
+                device_id=device(other),
+                device_id_type=MESH,
+            )
+        )
+        copies[-1].start()
+    first.wait()
+    second = pltpu.make_async_copy(held, out_ref.at[place], local_sem.at[1])
+    second.start()
+    second.wait()
+    for copy in copies:
+        copy.wait()
+
+
+def swap(array, kind, same, collective_id):
+    count = {"plane": 4, "column": 4, "chip": 2, "all": 32}[kind]
+    block = array.shape if same else array.shape[1:]
+    any_spec = pl.BlockSpec(memory_space=pl.ANY)
+    return pl.pallas_call(
+        partial(swap_kernel, kind, same),
+        out_shape=jax.ShapeDtypeStruct((count,) + block, array.dtype),
+        in_specs=[any_spec],
+        out_specs=any_spec,
+        scratch_shapes=[
+            pltpu.VMEM(block, array.dtype),
+            pltpu.SemaphoreType.DMA((2,)),
+            pltpu.SemaphoreType.DMA((count - 1,)),
+            pltpu.SemaphoreType.DMA((count - 1,)),
+        ],
+        compiler_params=pltpu.CompilerParams(
+            collective_id=collective_id, has_side_effects=True, vmem_limit_bytes=VMEM_LIMIT
+        ),
+        name=f"swap_{kind}_{collective_id}",
+    )(array)
+
+
+def spread_kernel(
+    block_ref, small_ref, out_ref, small_out, local_sem, za_send, za_recv, yx_send, yx_recv, cc_send, cc_recv
+):
+    dp, part = lax.axis_index("dp"), lax.axis_index("tensor")
+    place, core = dp // 2, dp % 2
+    partner = (place * 2 + 1 - core, part)
+    columns = [lax.rem(part + step, 4) for step in range(1, 4)]
+    planes = [lax.rem(place + step, 4) for step in range(1, 4)]
+    own = pltpu.make_async_copy(block_ref, out_ref.at[:, part, dp], local_sem.at[0])
+    own_small = pltpu.make_async_copy(small_ref, small_out.at[part, dp], local_sem.at[1])
+    own.start()
+    own_small.start()
+    greet(
+        [(dp, other) for other in columns]
+        + [(other * 2 + core, part) for other in planes]
+        + [partner]
+    )
+
+    def send(src, dst, send_sem, recv_sem, device):
+        copy = pltpu.make_async_remote_copy(
+            src_ref=src, dst_ref=dst, send_sem=send_sem, recv_sem=recv_sem,
+            device_id=device, device_id_type=MESH,
+        )
+        copy.start()
+        return copy
+
+    pairs = ((block_ref, out_ref), (small_ref, small_out))
+
+    def slot(which, part_at, dp_at):
+        return out_ref.at[:, part_at, dp_at] if which == 0 else small_out.at[part_at, dp_at]
+
+    first = [
+        [
+            send(pairs[which][0], slot(which, part, dp), za_send.at[which, step], za_recv.at[which, step], (dp, other))
+            for which in range(2)
+        ]
+        for step, other in enumerate(columns)
+    ]
+    own.wait()
+    own_small.wait()
+    second = [[], [], [], []]
+    third = []
+    for turn in range(4):
+        part_at = lax.rem(part + 4 - turn, 4)
+        if turn:
+            for copy in first[turn - 1]:
+                copy.wait()
+        for step, other in enumerate(planes):
+            for which in range(2):
+                second[turn].append(
+                    send(
+                        slot(which, part_at, dp), slot(which, part_at, dp),
+                        yx_send.at[turn, which, step], yx_recv.at[turn, which, step],
+                        (other * 2 + core, part),
+                    )
+                )
+        for which in range(2):
+            third.append(
+                send(
+                    slot(which, part_at, dp), slot(which, part_at, dp),
+                    cc_send.at[turn, which, 0], cc_recv.at[turn, which, 0], partner,
+                )
+            )
+    for turn in range(4):
+        part_at = lax.rem(part + 4 - turn, 4)
+        for step in range(3):
+            for which in range(2):
+                second[turn][step * 2 + which].wait()
+                dp_at = lax.rem(place + 3 - step, 4) * 2 + core
+                third.append(
+                    send(
+                        slot(which, part_at, dp_at), slot(which, part_at, dp_at),
+                        cc_send.at[turn, which, step + 1], cc_recv.at[turn, which, step + 1], partner,
+                    )
+                )
+    for copy in third:
+        copy.wait()
+
+
+def spread(block, small):
+    any_spec = pl.BlockSpec(memory_space=pl.ANY)
+    vmem_spec = pl.BlockSpec(memory_space=pltpu.VMEM)
+    dma = pltpu.SemaphoreType.DMA
+    return pl.pallas_call(
+        spread_kernel,
+        out_shape=(
+            jax.ShapeDtypeStruct((block.shape[0], 4, 8) + block.shape[1:], block.dtype),
+            jax.ShapeDtypeStruct((4, 8) + small.shape, small.dtype),
+        ),
+        in_specs=[vmem_spec, vmem_spec],
+        out_specs=(any_spec, any_spec),
+        scratch_shapes=[
+            dma((2,)), dma((2, 3)), dma((2, 3)), dma((4, 2, 3)), dma((4, 2, 3)), dma((4, 2, 4)), dma((4, 2, 4)),
+        ],
+        compiler_params=pltpu.CompilerParams(
+            collective_id=1, has_side_effects=True, vmem_limit_bytes=VMEM_LIMIT
+        ),
+        name="spread",
+    )(block, small)
+
+
+def join_kernel(in_ref, out_ref, held, local_sem, send_sem, recv_sem):
+    dp, part = lax.axis_index("dp"), lax.axis_index("tensor")
+    core = dp % 2
+    partner = (dp // 2 * 2 + 1 - core, part)
+    loads = [
+        pltpu.make_async_copy(in_ref.at[:, which], held.at[which], local_sem.at[0, which])
+        for which in range(2)
+    ]
+    for load in loads:
+        load.start()
+    greet([partner])
+    copies = [
+        pltpu.make_async_remote_copy(
+            src_ref=in_ref.at[:, which],
+            dst_ref=out_ref.at[which, :, core],
+            send_sem=send_sem.at[which],
+            recv_sem=recv_sem.at[which],
+            device_id=partner,
+            device_id_type=MESH,
+        )
+        for which in range(2)
+    ]
+    for copy in copies:
+        copy.start()
+    stores = [
+        pltpu.make_async_copy(held.at[which], out_ref.at[which, :, core], local_sem.at[1, which])
+        for which in range(2)
+    ]
+    for which in range(2):
+        loads[which].wait()
+        stores[which].start()
+    for copy in stores + copies:
+        copy.wait()
+
+
+def join(pieces):
+    any_spec = pl.BlockSpec(memory_space=pl.ANY)
+    dma = pltpu.SemaphoreType.DMA
+    count, _, rows, width = pieces.shape
+    return pl.pallas_call(
+        join_kernel,
+        out_shape=jax.ShapeDtypeStruct((2, count, 2, rows, width), pieces.dtype),
+        in_specs=[any_spec],
+        out_specs=any_spec,
+        scratch_shapes=[
+            pltpu.VMEM((2, count, rows, width), pieces.dtype), dma((2, 2)), dma((2,)), dma((2,)),
+        ],
+        compiler_params=pltpu.CompilerParams(
+            collective_id=2, has_side_effects=True, vmem_limit_bytes=VMEM_LIMIT
+        ),
+        name="join",
+    )(pieces)
+
+
+def standard(rows):
+    centred = rows - jnp.mean(rows, axis=-1, keepdims=True)
+    inv_std = lax.rsqrt(jnp.mean(centred * centred, axis=-1, keepdims=True) + eps_norm)
+    return centred * inv_std, inv_std
+
+
+def lane_put(table, lane, column):
+    lanes = lax.broadcasted_iota(jnp.int32, table.shape, 1)
+    return jnp.where(lanes == lane, column, table)
+
+
+def masked_scores(query, key):
+    scores = nt(query, key) * (HD ** (-0.5))
+    slots = lax.broadcasted_iota(jnp.int32, scores.shape, 1)
+    return jnp.where(slots < LEN, scores, far_negative)
+
+
+def attend_kernel(
+    hidden_ref, weight_ref, vec_ref, router_ref,
+    resid_ref, second_ref, saved_ref, table_ref, logs_ref, first_sc, attn_sc,
+):
+    turn = pl.program_id(0)
+    images = hidden_ref.shape[0] // SEQ
+
+    @pl.when(turn == 0)
+    def _():
+        normed, _ = standard(hidden_ref[...].astype(f32))
+        first_sc[...] = (normed * vec_ref[0:1] + vec_ref[1:2]).astype(bf16)
+        attn_sc[...] = jnp.zeros_like(attn_sc)
+
+    for image in range(images):
+        rows = pl.ds(image * SEQ, SEQ)
+        mixed = nn(first_sc[rows, :], weight_ref[0, :, :QKV]).astype(bf16)
+        logs = jnp.zeros((SEQ, 128), f32)
+        contexts = []
+        for head in range(HEADS_PART):
+            query, key, value = [
+                mixed[:, (kind * HEADS_PART + head) * HD : (kind * HEADS_PART + head + 1) * HD]
+                for kind in range(3)
+            ]
+            scores = masked_scores(query, key)
+            top = jnp.max(scores, axis=-1, keepdims=True)
+            grown = jnp.exp(scores - top)
+            total = jnp.sum(grown, axis=-1, keepdims=True)
+            weights = (grown / total).astype(bf16)
+            contexts.append(nn(weights, value).astype(bf16))
+            logs = lane_put(logs, head, top + jnp.log(total))
+        context = jnp.concatenate(contexts, axis=1)
+        saved_ref[0, rows, :] = jnp.concatenate([mixed, context], axis=1)
+        logs_ref[0, rows, :] = logs
+        attn_sc[rows, :] += nt(context, weight_ref[0, :, QKV:])
+
+    @pl.when(turn == pl.num_programs(0) - 1)
+    def _():
+        attn = attn_sc[...]
+        resid = hidden_ref[...].astype(f32) + attn
+        resid_ref[...] = resid
+        normed, _ = standard(resid)
+        second = (normed * vec_ref[2:3] + vec_ref[3:4]).astype(bf16)
+        second_ref[...] = second
+        logits = nn(second, router_ref[...])
+        lanes = lax.broadcasted_iota(jnp.int32, logits.shape, 1)
+        logits = jnp.where(lanes < EXPERTS, logits, far_negative)
+        grown = jnp.exp(logits - jnp.max(logits, axis=-1, keepdims=True))
+        probs = grown / jnp.sum(grown, axis=-1, keepdims=True)
+        table_ref[...] = lane_put(probs, EXPERTS, jnp.sum(attn * attn, axis=-1, keepdims=True))
+
+
+def attend_rows(hidden, weights, vecs, router):
+    rows = hidden.shape[0]
+    whole = lambda shape: pl.BlockSpec(shape, lambda turn: (0,) * len(shape))
+    by_part = lambda shape: pl.BlockSpec((1,) + shape, lambda turn: (turn, 0, 0))
+    return pl.pallas_call(
+        attend_kernel,
+        grid=(4,),
+        in_specs=[whole((rows, D)), by_part((D, D)), whole((8, D)), whole((D, 128))],
+        out_specs=(
+            whole((rows, D)), whole((rows, D)), by_part((rows, D)), whole((rows, 128)), by_part((rows, 128)),
+        ),
+        out_shape=(
+            jax.ShapeDtypeStruct((rows, D), f32),
+            jax.ShapeDtypeStruct((rows, D), bf16),
+            jax.ShapeDtypeStruct((4, rows, D), bf16),
+            jax.ShapeDtypeStruct((rows, 128), f32),
+            jax.ShapeDtypeStruct((4, rows, 128), f32),
+        ),
+        scratch_shapes=[pltpu.VMEM((rows, D), bf16), pltpu.VMEM((rows, D), f32)],
+        compiler_params=pltpu.CompilerParams(vmem_limit_bytes=VMEM_LIMIT),
+        name="attend_rows",
+    )(hidden, weights, vecs, router)
+
+
+def norm_pull(grad, normed, inv_std, gain):
+    scaled = grad * gain
+    one = jnp.mean(scaled, axis=-1, keepdims=True)
+    two = jnp.mean(scaled * normed, axis=-1, keepdims=True)
+    return inv_std * (scaled - one - normed * two)
+
+
+def attend_pull_kernel(
+    grad_ref, moved_ref, hidden_ref, resid_ref, saved_ref, table_ref, logs_ref, dprob_ref,
+    weight_ref, vec_ref, router_ref,
+    out_ref, wgrad_ref, small_ref, rgrad_ref,
+    first_sc, grad_sc, low_sc, back_sc,
+):
+    turn = pl.program_id(0)
+    rows_all = grad_ref.shape[0]
+    images = rows_all // SEQ
+    scale = HD ** (-0.5)
+
+    @pl.when(turn == 0)
+    def _():
+        normed, inv_std = standard(resid_ref[...])
+        second = (normed * vec_ref[2:3] + vec_ref[3:4]).astype(bf16)
+        lanes = lax.broadcasted_iota(jnp.int32, (rows_all, 128), 1)
+        probs = jnp.where(lanes < EXPERTS, table_ref[...], 0.0)
+        dprobs = dprob_ref[...]
+        dlogit = probs * (dprobs - jnp.sum(probs * dprobs, axis=-1, keepdims=True))
+        high = dlogit.astype(bf16)
+        low = (dlogit - high.astype(f32)).astype(bf16)
+        rgrad_ref[...] = tn(second, high) + tn(second, low)
+        dsecond = nt(high, router_ref[...]) + nt(low, router_ref[...])
+        for expert in range(EXPERTS):
+            dsecond = dsecond + moved_ref[expert].astype(f32)
+        small_ref[2:3] = jnp.sum(dsecond * normed, axis=0, keepdims=True)
+        small_ref[3:4] = jnp.sum(dsecond, axis=0, keepdims=True)
+        grad = grad_ref[...] + norm_pull(dsecond, normed, inv_std, vec_ref[2:3])
+        grad_sc[...] = grad
+        low_sc[...] = grad.astype(bf16)
+        normed, _ = standard(hidden_ref[...].astype(f32))
+        first_sc[...] = (normed * vec_ref[0:1] + vec_ref[1:2]).astype(bf16)
+        back_sc[...] = jnp.zeros_like(back_sc)
+
+    mixed_grads = []
+    for image in range(images):
+        rows = pl.ds(image * SEQ, SEQ)
+        saved = saved_ref[0, rows, :]
+        dcontext = nn(low_sc[rows, :], weight_ref[0, :, QKV:]).astype(bf16)
+        pieces = [[], [], []]
+        for head in range(HEADS_PART):
+            query, key, value = [
+                saved[:, (kind * HEADS_PART + head) * HD : (kind * HEADS_PART + head + 1) * HD]
+                for kind in range(3)
+            ]
+            dhead = dcontext[:, head * HD : (head + 1) * HD]
+            weights = jnp.exp(masked_scores(query, key) - logs_ref[0, rows, head : head + 1])
+            dvalue = tn(weights.astype(bf16), dhead)
+            dweights = nt(dhead, value)
+            inner = jnp.sum(weights * dweights, axis=-1, keepdims=True)
+            dscores = (weights * (dweights - inner)).astype(bf16)
+            pieces[0].append((nn(dscores, key) * scale).astype(bf16))
+            pieces[1].append((tn(dscores, query) * scale).astype(bf16))
+            pieces[2].append(dvalue.astype(bf16))
+        mixed = jnp.concatenate(pieces[0] + pieces[1] + pieces[2], axis=1)
+        back_sc[rows, :] += nt(mixed, weight_ref[0, :, :QKV])
+        mixed_grads.append(mixed)
+    mixed = jnp.concatenate(mixed_grads, axis=0)
+    wgrad_ref[0, :, :QKV] = tn(first_sc[...], mixed).astype(bf16)
+    wgrad_ref[0, :, QKV:] = tn(low_sc[...], saved_ref[0, :, QKV:]).astype(bf16)
+
+    @pl.when(turn == pl.num_programs(0) - 1)
+    def _():
+        dfirst = back_sc[...]
+        normed, inv_std = standard(hidden_ref[...].astype(f32))
+        small_ref[0:1] = jnp.sum(dfirst * normed, axis=0, keepdims=True)
+        small_ref[1:2] = jnp.sum(dfirst, axis=0, keepdims=True)
+        small_ref[4:8] = jnp.zeros((4, D), f32)
+        out_ref[...] = grad_sc[...] + norm_pull(dfirst, normed, inv_std, vec_ref[0:1])
+
+
+def attend_pull(grad, moved, hidden, resid, saved, table, logs, dprob, weights, vecs, router):
+    rows = grad.shape[0]
+    whole = lambda shape: pl.BlockSpec(shape, lambda turn: (0,) * len(shape))
+    by_part = lambda shape: pl.BlockSpec((1,) + shape, lambda turn: (turn, 0, 0))
+    return pl.pallas_call(
+        attend_pull_kernel,
+        grid=(4,),
+        in_specs=[
+            whole((rows, D)), whole((EXPERTS, rows, D)), whole((rows, D)), whole((rows, D)),
+            by_part((rows, D)), whole((rows, 128)), by_part((rows, 128)), whole((rows, 128)),
+            by_part((D, D)), whole((8, D)), whole((D, 128)),
+        ],
+        out_specs=(whole((rows, D)), by_part((D, D)), whole((8, D)), whole((D, 128))),
+        out_shape=(
+            jax.ShapeDtypeStruct((rows, D), f32),
+            jax.ShapeDtypeStruct((4, D, D), bf16),
+            jax.ShapeDtypeStruct((8, D), f32),
+            jax.ShapeDtypeStruct((D, 128), f32),
+        ),
+        scratch_shapes=[
+            pltpu.VMEM((rows, D), bf16), pltpu.VMEM((rows, D), f32),
+            pltpu.VMEM((rows, D), bf16), pltpu.VMEM((rows, D), f32),
+        ],
+        compiler_params=pltpu.CompilerParams(vmem_limit_bytes=VMEM_LIMIT),
+        name="attend_pull",
+    )(grad, moved, hidden, resid, saved, table, logs, dprob, weights, vecs, router)
+
+
+GELU_C = math.sqrt(2.0 / math.pi)
+GELU_K = 0.044715
+
+
+def gelu_pair(pre):
+    square = pre * pre
+    bent = jnp.tanh(GELU_C * pre * (1.0 + GELU_K * square))
+    half = 0.5 * (1.0 + bent)
+    slope = half + (0.5 * GELU_C) * pre * (1.0 - bent * bent) * (1.0 + (3.0 * GELU_K) * square)
+    return pre * half, slope
+
+
+TILE = 256
+
+
+def expert_kernel(rows_ref, weight_ref, out_ref, act_ref, slope_ref, sum_sc):
+    turn = pl.program_id(1)
+    for at in range(0, rows_ref.shape[1], TILE):
+        tile = pl.ds(at, TILE)
+        act, slope = gelu_pair(nn(rows_ref[0, tile, :], weight_ref[0, turn]))
+        act = act.astype(bf16)
+        act_ref[0, tile, :] = act
+        slope_ref[0, tile, :] = slope.astype(bf16)
+        part = nt(act, weight_ref[1, turn])
+        sum_sc[tile, :] = jnp.where(turn == 0, part, sum_sc[tile, :] + part)
+
+    @pl.when(turn == pl.num_programs(1) - 1)
+    def _():
+        out_ref[0] = sum_sc[...].astype(bf16)
+
+
+def expert_rows(rows, weights):
+    groups, count, _ = rows.shape
+    return pl.pallas_call(
+        expert_kernel,
+        grid=(groups, 4),
+        in_specs=[
+            pl.BlockSpec((1, count, D), lambda at, turn: (at, 0, 0)),
+            pl.BlockSpec((2, 4, D, D), lambda at, turn: (0, 0, 0, 0), pipeline_mode=pl.Buffered(1)),
+        ],
+        out_specs=(
+            pl.BlockSpec((1, count, D), lambda at, turn: (at, 0, 0)),
+            pl.BlockSpec((1, count, D), lambda at, turn: (turn, at, 0)),
+            pl.BlockSpec((1, count, D), lambda at, turn: (turn, at, 0)),
+        ),
+        out_shape=(
+            jax.ShapeDtypeStruct((groups, count, D), bf16),
+            jax.ShapeDtypeStruct((4, groups * count, D), bf16),
+            jax.ShapeDtypeStruct((4, groups * count, D), bf16),
+        ),
+        scratch_shapes=[pltpu.VMEM((count, D), f32)],
+        compiler_params=pltpu.CompilerParams(vmem_limit_bytes=VMEM_LIMIT),
+        name="expert_rows",
+    )(rows, weights)
+
+
+def expert_pull_kernel(rows_ref, grad_ref, act_ref, slope_ref, weight_ref, out_ref, wgrad_ref, sum_sc, pre_sc):
+    step = pl.program_id(0)
+    groups, count, _ = rows_ref.shape
+    last = groups * 4
+
+    @pl.when(step < last)
+    def _():
+        at, turn = step // 4, step % 4
+        for place in range(0, count, TILE):
+            tile = pl.ds(place, TILE)
+            dact = nn(grad_ref[at, tile, :], weight_ref[1, turn])
+            dpre = (slope_ref[0, tile, :].astype(f32) * dact).astype(bf16)
+            pre_sc[turn, pl.ds(at * count + place, TILE), :] = dpre
+            part = nt(dpre, weight_ref[0, turn])
+            sum_sc[tile, :] = jnp.where(turn == 0, part, sum_sc[tile, :] + part)
+
+        @pl.when(turn == 3)
+        def _():
+            out_ref[0] = sum_sc[...].astype(bf16)
+
+    @pl.when(step >= last)
+    def _():
+        turn = step - last
+        rows = rows_ref[...].reshape(groups * count, D)
+        grads = grad_ref[...].reshape(groups * count, D)
+        wgrad_ref[0, 0] = tn(rows, pre_sc[turn]).astype(bf16)
+        wgrad_ref[1, 0] = tn(grads, act_ref[0]).astype(bf16)
+
+
+def expert_pull(rows, grads, act, slope, weights):
+    groups, count, _ = rows.shape
+    last = groups * 4
+    early = lambda step: jnp.minimum(step, last - 1)
+    late = lambda step: jnp.maximum(step - last, 0)
+    whole = lambda shape: pl.BlockSpec(
+        shape, lambda step: (0,) * len(shape), pipeline_mode=pl.Buffered(1)
+    )
+    return pl.pallas_call(
+        expert_pull_kernel,
+        grid=(last + 4,),
+        in_specs=[
+            whole((groups, count, D)),
+            whole((groups, count, D)),
+            pl.BlockSpec((1, groups * count, D), lambda step: (late(step), 0, 0)),
+            pl.BlockSpec((1, count, D), lambda step: (early(step) % 4, early(step) // 4, 0)),
+            whole((2, 4, D, D)),
+        ],
+        out_specs=(
+            pl.BlockSpec((1, count, D), lambda step: (early(step) // 4, 0, 0)),
+            pl.BlockSpec((2, 1, D, D), lambda step: (0, late(step), 0, 0)),
+        ),
+        out_shape=(
+            jax.ShapeDtypeStruct((groups, count, D), bf16),
+            jax.ShapeDtypeStruct((2, 4, D, D), bf16),
+        ),
+        scratch_shapes=[
+            pltpu.VMEM((count, D), f32),
+            pltpu.VMEM((4, groups * count, D), bf16),
+        ],
+        compiler_params=pltpu.CompilerParams(vmem_limit_bytes=VMEM_LIMIT),
+        name="expert_pull",
+    )(rows, grads, act, slope, weights)
+
+
+def add_up(pieces, own):
+    return sum(pieces[at].astype(f32) for at in range(pieces.shape[0])).astype(own)
+
+
+def per_device(
+    tokens, counts, routes, norm_gain, norm_bias, w_router, w_qkv, w_out, w_in, w_back, cotangent
+):
+    dp, part = lax.axis_index("dp"), lax.axis_index("tensor")
+    core = dp % 2
+    own_rows = tokens.shape[0]
+    slices = D // 8
+    row_ids = part * own_rows + jnp.arange(own_rows, dtype=jnp.int32)
+    image_count = lax.dynamic_index_in_dim(counts, dp, keepdims=False)
+    valid = ((row_ids // SEQ < image_count) & (row_ids % SEQ < LEN)).astype(f32)[:, None]
+    my_routes = lax.dynamic_slice_in_dim(routes, part * own_rows, own_rows, axis=1)
+    chosen = (my_routes[:, :, :, None] == jnp.arange(EXPERTS)).any(axis=2)
+
+    pieces = []
+    for layer in range(LAYERS):
+        packed = jnp.stack([w_in[layer], w_back[layer]], axis=1)
+        arrived = swap(packed, "plane", False, 3)
+        pieces.append(lax.all_gather(arrived, "tensor", axis=0, tiled=True))
+
+    mixed_in = jnp.transpose(w_qkv, (0, 2, 1, 3)).reshape(LAYERS, slices, QKV)
+    attn_block = jnp.concatenate([mixed_in, jnp.transpose(w_out, (0, 2, 1))], axis=2)
+    small = jnp.concatenate([norm_gain, norm_bias, w_router])
+    small = jnp.pad(small, (0, 2048 - small.shape[0])).reshape(16, 128)
+    attn_all, small_all = spread(attn_block, small)
+    attn_all = attn_all.reshape(LAYERS, 4, D, D)
+    flat = jnp.transpose(small_all.reshape(4, 8, 2048), (1, 0, 2)).reshape(32, 2048)
+    vec_count = LAYERS * 2 * D // 32
+    gains = flat[:, :vec_count].reshape(LAYERS, 2, D).astype(f32)
+    biases = flat[:, vec_count : 2 * vec_count].reshape(LAYERS, 2, D).astype(f32)
+    routers = flat[:, 2 * vec_count : 2 * vec_count + LAYERS * D * EXPERTS // 32]
+    routers = jnp.pad(routers.reshape(LAYERS, D, EXPERTS), ((0, 0), (0, 0), (0, 128 - EXPERTS)))
+    vecs = jnp.pad(
+        jnp.stack([gains[:, 0], biases[:, 0], gains[:, 1], biases[:, 1]], axis=1), ((0, 0), (0, 4), (0, 0))
+    )
+
+    hidden = tokens
+    kept = []
+    stats = []
+    for layer in range(LAYERS):
+        resid, second, saved, table, logs = attend_rows(hidden, attn_all[layer], vecs[layer], routers[layer])
+        rows = swap(second, "plane", True, 4)
+        weights = join(pieces[layer]).reshape(2, 4, D, D)
+        made, act, slope = expert_rows(rows, weights)
+        back = swap(made, "plane", False, 5)
+        gates = jnp.where(chosen[layer], table[:, :EXPERTS], 0.0)
+        moe = sum(gates[:, e : e + 1] * back[e].astype(f32) for e in range(EXPERTS))
+        result = resid + moe
+        stats.append(
+            jnp.stack(
+                [
+                    jnp.sum(valid * result * result),
+                    jnp.sum(valid[:, 0] * table[:, EXPERTS]),
+                    jnp.sum(valid * moe * moe),
+                ]
+            )
+        )
+        kept.append((hidden, resid, saved, table, logs, rows, weights, act, slope, back, gates))
+        hidden = result
+
+    grad = cotangent.astype(f32) * valid
+    attn_grads, expert_grads, small_grads, router_grads = [], [], [], []
+    for layer in reversed(range(LAYERS)):
+        before, resid, saved, table, logs, rows, weights, act, slope, back, gates = kept[layer]
+        low = grad.astype(bf16)
+        dgate = [jnp.sum(back[e].astype(f32) * low.astype(f32), axis=-1) for e in range(EXPERTS)]
+        dprob = jnp.where(chosen[layer], jnp.stack(dgate, axis=1), 0.0)
+        dprob = jnp.pad(dprob, ((0, 0), (0, 128 - EXPERTS)))
+        sent = jnp.stack([(gates[:, e : e + 1] * low.astype(f32)).astype(bf16) for e in range(EXPERTS)])
+        arrived = swap(sent, "plane", False, 5)
+        drows, wgrad = expert_pull(rows, arrived, act, slope, weights)
+        moved = swap(drows, "plane", False, 5)
+        wgrad = wgrad.reshape(2, 4, 4, 2, slices, D)
+        halves = jnp.transpose(wgrad, (3, 1, 2, 0, 4, 5))
+        halves = add_up(swap(halves, "chip", False, 6), bf16)
+        summed = lax.psum_scatter(halves, "tensor", scatter_dimension=0, tiled=False)
+        expert_grads.append(summed)
+        grad, attn_wgrad, small_grad, router_grad = attend_pull(
+            grad, moved, before, resid, saved, table, logs, dprob, attn_all[layer], vecs[layer], routers[layer]
+        )
+        attn_wgrad = jnp.transpose(attn_wgrad.reshape(4, 4, 2, slices, D), (2, 1, 0, 3, 4))
+        attn_wgrad = add_up(swap(attn_wgrad, "chip", False, 7), bf16)
+        attn_wgrad = add_up(swap(attn_wgrad, "plane", False, 8), bf16)
+        attn_wgrad = add_up(swap(attn_wgrad, "column", False, 9), f32)
+        attn_grads.append(attn_wgrad)
+        small_grads.append(small_grad[:4])
+        router_grads.append(router_grad[:, :EXPERTS])
+    owned = [swap(each, "plane", False, 10) for each in expert_grads]
+    for listed in (attn_grads, owned, small_grads, router_grads):
+        listed.reverse()
+
+    vec_grads = jnp.stack(small_grads).reshape(LAYERS, 2, 2, D)
+    packed = jnp.concatenate(
+        [
+            vec_grads[:, :, 0].reshape(32, -1),
+            vec_grads[:, :, 1].reshape(32, -1),
+            jnp.stack(router_grads).reshape(32, -1),
+            jnp.broadcast_to(jnp.stack(stats).reshape(1, -1), (32, 3 * LAYERS)),
+        ],
+        axis=1,
+    )
+    packed = jnp.pad(packed, ((0, 0), (0, 1024 - packed.shape[1]))).reshape(32, 8, 128)
+    total = jnp.sum(swap(packed, "all", False, 11), axis=0).reshape(-1)
+    share = LAYERS * 2 * D // 32
+    router_share = LAYERS * D * EXPERTS // 32
+    at = 2 * share + router_share
+    denom = jnp.sum(counts).astype(f32) * (LEN * D)
+    rms = jnp.sqrt(total[at : at + 3 * LAYERS].reshape(LAYERS, 3) / denom)
+    attn_grad = jnp.stack(attn_grads)
+    qkv_grad = jnp.transpose(attn_grad[:, :, :QKV].reshape(LAYERS, slices, 3, QKV // 3), (0, 2, 1, 3))
+    out_grad = jnp.transpose(attn_grad[:, :, QKV:], (0, 2, 1))
+    expert_grad = jnp.stack(owned).astype(f32)
+    return (
+        hidden,
+        grad,
+        total[:share],
+        total[share : 2 * share],
+        total[2 * share : at],
+        qkv_grad,
+        out_grad,
+        expert_grad[:, :, 0],
+        expert_grad[:, :, 1],
+        rms,
+    )
+
+
 def solution(mesh):
     return jax.shard_map(
-        per_device,
+        per_device if mesh.shape["dp"] == 8 else per_device_general,
         mesh=mesh,
         in_specs=(
             P(("dp", "tensor"), None),

time: 3210 us -> 1020 us (0.32)
  waiting for transfers between devices: 1550 us -> 0.13 us
  Pallas kernels: 0 us -> 879 us
  local copies, waits for them, and re-layouts: 555 us -> 54.1 us
  blocking collectives: 458 us -> 0 us
  matrix products: 347 us -> 0 us
  other arithmetic: 217 us -> 61.5 us
  starting transfers between devices: 56.6 us -> 0.16 us
    reduce_scatter x12 -> x2, waiting for transfers between devices: 1020 us -> 0.02 us  [per_device(): lax.psum_scatter(halves, 'tensor', scatter_dimension=0, tiled=False)]
    pallas_call x0 -> x32, Pallas kernels: none -> 879 us  [the longest x21 517 us: swap(): pl.pallas_call(partial(swap_kernel, kind, same), out_shape=jax.ShapeDtype...]
    all_gather x8 -> x2, waiting for transfers between devices: 354 us -> 0.04 us  [per_device(): pieces.append(lax.all_gather(arrived, 'tensor', axis=0, tiled=True))]
    dot_general x86 -> x0, matrix products: 339 us -> none  [the longest x8 69.1 us: contract_last(): lax.dot_general(left_mat, right_mat, (((1,), (1,)), ((), ())), preferred_...]
    all_to_all x3 -> x0, blocking collectives: 330 us -> none  [to_experts(): lax.all_to_all(make_rows(positions), 'dp', split_axis=0, concat_axis=0, t...]
    gather x16 -> x0, local copies, waits for them, and re-layouts: 312 us -> none  [the longest x4 75.7 us: per_device(): d_rows_two = jnp.sum(padded_back[pick_index], axis=1)]
    all_to_all x13 -> x0, waiting for transfers between devices: 171 us -> none  [the longest x1 104 us: to_experts(): lax.all_to_all(make_rows(positions), 'dp', split_axis=0, concat_axis=0, t...]
    reduce_sum x38 -> x6, other arithmetic: 143 us -> 12.1 us  [the longest x2 7.99 us: per_device(): jnp.sum(back[e].astype(f32) * low.astype(f32), axis=-1)]
  transfers between devices with their start and end apart: 37 -> 4, of which waited for: 24 -> 0; matrix products, arithmetic and copies ran while one was open for 15% -> 8% of each run, Pallas kernels for 0% -> 65%
where the time goes in v1:
time: 1020 us; the launch traced here: 1010 us
  Pallas kernels  879 us (86%)
  other arithmetic  61.5 us (6%)
  local copies, waits for them, and re-layouts  54.1 us (5%)
  between operations  15.7 us (2%)
    pallas_call x21, Pallas kernels, swap(): pl.pallas_call(partial(swap_kernel, kind, same), out_shape=jax.ShapeDtype...  517 us
    pallas_call x2, Pallas kernels, expert_pull(): pl.pallas_call(expert_pull_kernel, grid=(last + 4,), in_specs=[whole((gro...  110 us
    pallas_call x2, Pallas kernels, expert_rows(): pl.pallas_call(expert_kernel, grid=(groups, 4), in_specs=[pl.BlockSpec((1...  75 us
    pallas_call x1, Pallas kernels, spread(): pl.pallas_call(spread_kernel, out_shape=(jax.ShapeDtypeStruct((block.shap...  69.5 us
    pallas_call x2, Pallas kernels, attend_pull(): pl.pallas_call(attend_pull_kernel, grid=(4,), in_specs=[whole((rows, D)),...  61.6 us
    pallas_call x2, Pallas kernels, attend_rows(): pl.pallas_call(attend_kernel, grid=(4,), in_specs=[whole((rows, D)), by_p...  29.4 us
    convert_element_type x4, other arithmetic, add_up(): sum((pieces[at].astype(f32) for at in range(pieces.shape[0]))).astype(own)  24.3 us
  transfers between devices with their start and end apart: 4, of which 0 were waited for; matrix products, arithmetic and copies ran while one was open for 8% of the time, Pallas kernels for 65%

profile of v1, /device:TPU:0, one launch (start us, length us, event | category | flops | bytes accessed | tf_op | source)
XLA Modules:
  0.0 1010.7 jit_solution(13128678102235205442)
XLA Ops:
  10.1 18.0 %swap_plane_3.2 = bf16[4,2,96,768]{3,2,1,0:T(8,128)(2,1)} custom-call(bf16[4,2,96,768]{3,2,1,0:T(8,128)(2,1)} %pad_maximum_fusion.2.in_ref), custom_call_target="tpu_custom_call" | custom-call | tf_op jit(solution)/shard_map/swap_plane_3/pallas_call | solution.py:513
  29.3 16.5 %swap_plane_3.3 = bf16[4,2,96,768]{3,2,1,0:T(8,128)(2,1)} custom-call(bf16[4,2,96,768]{3,2,1,0:T(8,128)(2,1)} %pad_maximum_fusion.3.in_ref), custom_call_target="tpu_custom_call" | custom-call | tf_op jit(solution)/shard_map/swap_plane_3/pallas_call | solution.py:513
  48.0 69.5 %spread.1 = (bf16[2,4,8,96,768]{4,3,2,1,0:T(8,128)(2,1)}, bf16[4,8,16,128]{3,2,1,0:T(8,128)(2,1)}) custom-call(bf16[2,96,768]{2,1,0:T(8,128)(2,1)} %pad_maximum_fusion.5.block_ref, bf16[16,128]{1,0:T(8,128)(2,1)} %fusion.50.small_ref), custom_call_target="tpu_custom_call" | custom-call | tf_op jit(solution)/shard_map/spread/pallas_call | solution.py:614
  129.0 14.7 %attend_rows.2 = (f32[512,768]{1,0:T(8,128)}, bf16[512,768]{1,0:T(8,128)(2,1)}, bf16[4,512,768]{2,1,0:T(8,128)(2,1)}, f32[512,128]{1,0:T(8,128)}, f32[4,512,128]{2,1,0:T(8,128)}) custom-call(bf16[512,768]{1,0:T(8,128)(2,1)} %hidden_ref.3, bf16[4,768,768]{2,1,0:T(8,128)(2,1)} %bitcast.168, f32[8,768]{1,0:T(8,128)} %get-tuple-element.158.vec_ref, ...), custom_call_target="tpu_custom_call" | custom-call | tf_op jit(solution)/shard_map/attend_rows/pallas_call | solution.py:758
  143.7 38.5 %swap_plane_4.2.rows_ref = bf16[4,512,768]{2,1,0:T(8,128)(2,1)} custom-call(bf16[512,768]{1,0:T(8,128)(2,1)} %get-tuple-element.44.in_ref), custom_call_target="tpu_custom_call" | custom-call | tf_op jit(solution)/shard_map/swap_plane_4/pallas_call | solution.py:513
  193.0 37.3 %expert_rows.2 = (bf16[4,512,768]{2,1,0:T(8,128)(2,1)}, bf16[4,2048,768]{2,1,0:T(8,128)(2,1)}, bf16[4,2048,768]{2,1,0:T(8,128)(2,1)}) custom-call(bf16[4,512,768]{2,1,0:T(8,128)(2,1)} %swap_plane_4.2.rows_ref, bf16[2,4,768,768]{3,2,1,0:T(8,128)(2,1)} %bitcast.162), custom_call_target="tpu_custom_call" | custom-call | tf_op jit(solution)/shard_map/expert_rows/pallas_call | solution.py:917
  230.3 37.8 %swap_plane_5.6 = bf16[4,512,768]{2,1,0:T(8,128)(2,1)} custom-call(bf16[4,512,768]{2,1,0:T(8,128)(2,1)} %get-tuple-element.45.in_ref), custom_call_target="tpu_custom_call" | custom-call | tf_op jit(solution)/shard_map/swap_plane_5/pallas_call | solution.py:513
  286.4 37.6 %swap_plane_4.3.rows_ref = bf16[4,512,768]{2,1,0:T(8,128)(2,1)} custom-call(bf16[512,768]{1,0:T(8,128)(2,1)} %get-tuple-element.48.in_ref), custom_call_target="tpu_custom_call" | custom-call | tf_op jit(solution)/shard_map/swap_plane_4/pallas_call | solution.py:513
  332.4 37.7 %expert_rows.3 = (bf16[4,512,768]{2,1,0:T(8,128)(2,1)}, bf16[4,2048,768]{2,1,0:T(8,128)(2,1)}, bf16[4,2048,768]{2,1,0:T(8,128)(2,1)}) custom-call(bf16[4,512,768]{2,1,0:T(8,128)(2,1)} %swap_plane_4.3.rows_ref, bf16[2,4,768,768]{3,2,1,0:T(8,128)(2,1)} %bitcast.164), custom_call_target="tpu_custom_call" | custom-call | tf_op jit(solution)/shard_map/expert_rows/pallas_call | solution.py:917
  370.1 37.1 %swap_plane_5.7 = bf16[4,512,768]{2,1,0:T(8,128)(2,1)} custom-call(bf16[4,512,768]{2,1,0:T(8,128)(2,1)} %get-tuple-element.49.in_ref), custom_call_target="tpu_custom_call" | custom-call | tf_op jit(solution)/shard_map/swap_plane_5/pallas_call | solution.py:513
  416.3 37.5 %swap_plane_5.8.grad_ref = bf16[4,512,768]{2,1,0:T(8,128)(2,1)} custom-call(bf16[4,512,768]{2,1,0:T(8,128)(2,1)} %pad_maximum_fusion.in_ref), custom_call_target="tpu_custom_call" | custom-call | tf_op jit(solution)/shard_map/swap_plane_5/pallas_call | solution.py:513
  453.8 55.2 %expert_pull.2 = (bf16[4,512,768]{2,1,0:T(8,128)(2,1)}, bf16[2,4,768,768]{3,2,1,0:T(8,128)(2,1)}) custom-call(bf16[4,512,768]{2,1,0:T(8,128)(2,1)} %swap_plane_4.3.rows_ref, bf16[4,512,768]{2,1,0:T(8,128)(2,1)} %swap_plane_5.8.grad_ref, bf16[4,2048,768]{2,1,0:T(8,128)(2,1)} %get-tuple-element.50.act_ref, bf16[4,2048,768]{2,1,0:T(8,128)(2,1)} %get-tuple-element.51.slope_ref, ...), custom_call_target="tpu_custom_call" | custom-call | tf_op jit(solution)/shard_map/expert_pull/pallas_call | solution.py:977
  533.1 37.1 %swap_plane_5.9.moved_ref = bf16[4,512,768]{2,1,0:T(8,128)(2,1)} custom-call(bf16[4,512,768]{2,1,0:T(8,128)(2,1)} %get-tuple-element.52.in_ref), custom_call_target="tpu_custom_call" | custom-call | tf_op jit(solution)/shard_map/swap_plane_5/pallas_call | solution.py:513
  571.2 30.8 %attend_pull.2 = (f32[512,768]{1,0:T(8,128)}, bf16[4,768,768]{2,1,0:T(8,128)(2,1)}, f32[8,768]{1,0:T(8,128)}, f32[768,128]{1,0:T(8,128)}) custom-call(f32[512,768]{1,0:T(8,128)} %get-tuple-element.148.grad_ref, bf16[4,512,768]{2,1,0:T(8,128)(2,1)} %swap_plane_5.9.moved_ref, f32[512,768]{1,0:T(8,128)} %get-tuple-element.134.hidden_ref, ...), custom_call_target="tpu_custom_call" | custom-call | tf_op jit(solution)/shard_map/attend_pull/pallas_call | solution.py:860
  606.4 37.6 %swap_plane_5.10.grad_ref = bf16[4,512,768]{2,1,0:T(8,128)(2,1)} custom-call(bf16[4,512,768]{2,1,0:T(8,128)(2,1)} %pad_maximum_fusion.1.in_ref), custom_call_target="tpu_custom_call" | custom-call | tf_op jit(solution)/shard_map/swap_plane_5/pallas_call | solution.py:513
  644.0 55.3 %expert_pull.3 = (bf16[4,512,768]{2,1,0:T(8,128)(2,1)}, bf16[2,4,768,768]{3,2,1,0:T(8,128)(2,1)}) custom-call(bf16[4,512,768]{2,1,0:T(8,128)(2,1)} %swap_plane_4.2.rows_ref, bf16[4,512,768]{2,1,0:T(8,128)(2,1)} %swap_plane_5.10.grad_ref, bf16[4,2048,768]{2,1,0:T(8,128)(2,1)} %get-tuple-element.56.act_ref, bf16[4,2048,768]{2,1,0:T(8,128)(2,1)} %get-tuple-element.57.slope_ref, ...), custom_call_target="tpu_custom_call" | custom-call | tf_op jit(solution)/shard_map/expert_pull/pallas_call | solution.py:977
  726.2 37.0 %swap_plane_5.11.moved_ref = bf16[4,512,768]{2,1,0:T(8,128)(2,1)} custom-call(bf16[4,512,768]{2,1,0:T(8,128)(2,1)} %get-tuple-element.58.in_ref), custom_call_target="tpu_custom_call" | custom-call | tf_op jit(solution)/shard_map/swap_plane_5/pallas_call | solution.py:513
  764.1 30.8 %attend_pull.3 = (f32[512,768]{1,0:T(8,128)}, bf16[4,768,768]{2,1,0:T(8,128)(2,1)}, f32[8,768]{1,0:T(8,128)}, f32[768,128]{1,0:T(8,128)}) custom-call(f32[512,768]{1,0:T(8,128)} %get-tuple-element.55.grad_ref, bf16[4,512,768]{2,1,0:T(8,128)(2,1)} %swap_plane_5.11.moved_ref, bf16[512,768]{1,0:T(8,128)(2,1)} %hidden_ref.3, ...), custom_call_target="tpu_custom_call" | custom-call | tf_op jit(solution)/shard_map/attend_pull/pallas_call | solution.py:860
  803.3 35.3 %swap_all_11.1 = f32[32,8,128]{2,1,0:T(8,128)} custom-call(f32[32,8,128]{2,1,0:T(8,128)} %bitcast.185), custom_call_target="tpu_custom_call" | custom-call | tf_op jit(solution)/shard_map/swap_all_11/pallas_call | solution.py:513
  854.5 29.2 %swap_plane_8.2 = bf16[4,4,96,768]{3,2,1,0:T(8,128)(2,1)} custom-call(bf16[4,4,96,768]{3,2,1,0:T(8,128)(2,1)} %fusion.2.in_ref), custom_call_target="tpu_custom_call" | custom-call | tf_op jit(solution)/shard_map/swap_plane_8/pallas_call | solution.py:513
  915.1 29.3 %swap_plane_8.3 = bf16[4,4,96,768]{3,2,1,0:T(8,128)(2,1)} custom-call(bf16[4,4,96,768]{3,2,1,0:T(8,128)(2,1)} %fusion.3.in_ref), custom_call_target="tpu_custom_call" | custom-call | tf_op jit(solution)/shard_map/swap_plane_8/pallas_call | solution.py:513
  947.2 15.2 %swap_column_9.3 = bf16[4,96,768]{2,1,0:T(8,128)(2,1)} custom-call(bf16[4,96,768]{2,1,0:T(8,128)(2,1)} %fusion.39.in_ref), custom_call_target="tpu_custom_call" | custom-call | tf_op jit(solution)/shard_map/swap_column_9/pallas_call | solution.py:513
  967.3 15.7 %swap_plane_10.3 = bf16[4,2,96,768]{3,2,1,0:T(8,128)(2,1)} custom-call(bf16[4,2,96,768]{3,2,1,0:T(8,128)(2,1)} %bitcast.181), custom_call_target="tpu_custom_call" | custom-call | tf_op jit(solution)/shard_map/swap_plane_10/pallas_call | solution.py:513
  983.0 16.5 %swap_plane_10.2 = bf16[4,2,96,768]{3,2,1,0:T(8,128)(2,1)} custom-call(bf16[4,2,96,768]{3,2,1,0:T(8,128)(2,1)} %bitcast.182), custom_call_target="tpu_custom_call" | custom-call | tf_op jit(solution)/shard_map/swap_plane_10/pallas_call | solution.py:513
  (156 shorter events, 187.9 us)
Async XLA Ops:
  7.2 175.1 %copy-start = (s32[2,2048,2]{1,2,0:T(2,128)S(1)}, s32[2,2048,2]{1,2,0:T(2,128)}, u32[]{:S(2)}) copy-start(s32[2,2048,2]{1,2,0:T(2,128)} %param.13) | copy-start | bytes 98308
  7.2 177.4 %all-gather.3.cloned.1.call-start = ((), (), s32[]{:S(2)}) async-start(), calls=%async_computation.2 | async-start | bytes 5898240 | tf_op jit(solution)/shard_map/all_gather | solution.py:1025
  28.1 295.9 %all-gather.5.cloned.1.call-start = ((), (), s32[]{:S(2)}) async-start(), calls=%async_computation.3 | async-start | bytes 5898240 | tf_op jit(solution)/shard_map/all_gather | solution.py:1025
  29.3 16.7 %copy-start.13 = (bf16[2,192,96]{2,1,0:T(8,128)(2,1)S(1)}, bf16[2,192,96]{2,1,0:T(8,128)(2,1)}, u32[]{:S(2)}) copy-start(bf16[2,192,96]{2,1,0:T(8,128)(2,1)} %param.18) | copy-start | bytes 221188
  29.3 16.8 %copy-start.12 = (bf16[2,3,96,192]{3,2,1,0:T(8,128)(2,1)S(1)}, bf16[2,3,96,192]{3,2,1,0:T(8,128)(2,1)}, u32[]{:S(2)}) copy-start(bf16[2,3,96,192]{3,2,1,0:T(8,128)(2,1)} %param.17) | copy-start | bytes 663556
  45.8 0.7 copy-start.16
  45.8 0.7 copy-start.17
  45.9 0.7 copy-start.18
  45.9 921.4 %reduce-scatter.5.cloned.1.call-start = ((), (), s32[]{:S(2)}) async-start(), calls=%async_computation.5 | async-start | bytes 5898240 | tf_op jit(solution)/shard_map/reduce_scatter | solution.py:1082
  143.7 39.0 %copy-start.19 = (s32[8]{0:T(128)S(1)}, s32[8]{0:T(128)}, u32[]{:S(2)}) copy-start(s32[8]{0:T(128)} %param.12) | copy-start | bytes 100
  143.7 40.2 %copy-start.7 = (f32[512,128]{1,0:T(8,128)S(1)}, f32[512,128]{1,0:T(8,128)}, u32[]{:S(2)}) copy-start(f32[512,128]{1,0:T(8,128)} %get-tuple-element.43.table_ref) | copy-start | bytes 786436
  230.3 37.8 %copy-start.5 = (f32[512,768]{1,0:T(8,128)S(1)}, f32[512,768]{1,0:T(8,128)}, u32[]{:S(2)}) copy-start(f32[512,768]{1,0:T(8,128)} %get-tuple-element.42.resid_ref) | copy-start | bytes 4718596
  370.1 37.1 %copy-start.8 = (f32[512,128]{1,0:T(8,128)S(1)}, f32[512,128]{1,0:T(8,128)}, u32[]{:S(2)}) copy-start(f32[512,128]{1,0:T(8,128)} %get-tuple-element.47.table_ref) | copy-start | bytes 786436
  370.1 37.7 %copy-start.4 = (f32[512,768]{1,0:T(8,128)S(1)}, f32[512,768]{1,0:T(8,128)}, u32[]{:S(2)}) copy-start(f32[512,768]{1,0:T(8,128)} %get-tuple-element.46.resid_ref) | copy-start | bytes 4718596
  407.2 1.4 copy-start.3
  533.1 449.9 %reduce-scatter.3.cloned.1.call-start = ((), (), s32[]{:S(2)}) async-start(), calls=%async_computation.4 | async-start | bytes 5898240 | tf_op jit(solution)/shard_map/reduce_scatter | solution.py:1082
  571.2 30.8 %copy-start.2 = (bf16[4,512,768]{2,1,0:T(8,128)(2,1)S(1)}, bf16[4,512,768]{2,1,0:T(8,128)(2,1)}, u32[]{:S(2)}) copy-start(bf16[4,512,768]{2,1,0:T(8,128)(2,1)} %swap_plane_5.6) | copy-start | bytes 9437188
  764.1 30.8 %copy-start.11 = (f32[768,128]{1,0:T(8,128)S(1)}, f32[768,128]{1,0:T(8,128)}, u32[]{:S(2)}) copy-start(f32[768,128]{1,0:T(8,128)} %get-tuple-element.65) | copy-start | bytes 1179652
  795.0 1.5 copy-start.15
  795.0 1.5 copy-start.14
  795.0 1.9 copy-start.9
  944.4 18.0 %copy-start.10 = (bf16[4,96,768]{2,1,0:T(8,128)(2,1)S(1)}, bf16[4,96,768]{2,1,0:T(8,128)(2,1)}, u32[]{:S(2)}) copy-start(bf16[4,96,768]{2,1,0:T(8,128)(2,1)} %swap_column_9.2) | copy-start | bytes 1769476
  982.9 16.6 %copy-start.6 = (bf16[4,2,96,768]{3,2,1,0:T(8,128)(2,1)S(1)}, bf16[4,2,96,768]{3,2,1,0:T(8,128)(2,1)}, u32[]{:S(2)}) copy-start(bf16[4,2,96,768]{3,2,1,0:T(8,128)(2,1)} %swap_plane_10.3) | copy-start | bytes 3538948
  1001.1 2.6 copy-start.1
Sparse Core Ops, SparseCore 0:
  28.2 115.7 all-gather.2
  145.6 87.7 all-gather.4
  533.2 110.5 reduce-scatter.4
  723.5 110.5 reduce-scatter.2

commit v2 on v1

--- a/solution.py
+++ b/solution.py
@@ -443,7 +443,7 @@
 bf16 = jnp.bfloat16
 f32 = jnp.float32
 MESH = pl.DeviceIdType.MESH
-VMEM_LIMIT = 60 * 1024 * 1024
+VMEM_LIMIT = 63 * 1024 * 1024
 EXPERTS = 4
 HEADS_PART = 3
 QKV = 3 * HEADS_PART * HD
@@ -528,159 +528,196 @@
     )(array)
 
 
+def relatives():
+    dp, part = lax.axis_index("dp"), lax.axis_index("tensor")
+    place, core = dp // 2, dp % 2
+    row, col = place // 2, place % 2
+    near = (row * 2 + 1 - col, (1 - row) * 2 + col, (1 - row) * 2 + 1 - col)
+    return place, core, part, [None] + [(at * 2 + core, part) for at in near], (place * 2 + 1 - core, part)
+
+
+def push(src, dst, send_sem, recv_sem, device):
+    return pltpu.make_async_remote_copy(
+        src_ref=src, dst_ref=dst, send_sem=send_sem, recv_sem=recv_sem, device_id=device, device_id_type=MESH
+    )
+
+
+def comm_params(collective_id):
+    return pltpu.CompilerParams(
+        collective_id=collective_id, has_side_effects=True, vmem_limit_bytes=VMEM_LIMIT
+    )
+
+
+ANY_SPEC = pl.BlockSpec(memory_space=pl.ANY)
+DMA = pltpu.SemaphoreType.DMA
+
+
 def spread_kernel(
     block_ref, small_ref, out_ref, small_out, local_sem, za_send, za_recv, yx_send, yx_recv, cc_send, cc_recv
 ):
-    dp, part = lax.axis_index("dp"), lax.axis_index("tensor")
-    place, core = dp // 2, dp % 2
-    partner = (place * 2 + 1 - core, part)
+    place, core, part, near, partner = relatives()
+    dp = place * 2 + core
     columns = [lax.rem(part + step, 4) for step in range(1, 4)]
-    planes = [lax.rem(place + step, 4) for step in range(1, 4)]
-    own = pltpu.make_async_copy(block_ref, out_ref.at[:, part, dp], local_sem.at[0])
-    own_small = pltpu.make_async_copy(small_ref, small_out.at[part, dp], local_sem.at[1])
-    own.start()
-    own_small.start()
-    greet(
-        [(dp, other) for other in columns]
-        + [(other * 2 + core, part) for other in planes]
-        + [partner]
-    )
-
-    def send(src, dst, send_sem, recv_sem, device):
-        copy = pltpu.make_async_remote_copy(
-            src_ref=src, dst_ref=dst, send_sem=send_sem, recv_sem=recv_sem,
-            device_id=device, device_id_type=MESH,
-        )
+    pairs = ((block_ref, out_ref), (small_ref, small_out))
+    locals_ = [
+        pltpu.make_async_copy(src, dst.at[dp, part], local_sem.at[which])
+        for which, (src, dst) in enumerate(pairs)
+    ]
+    for copy in locals_:
         copy.start()
-        return copy
-
-    pairs = ((block_ref, out_ref), (small_ref, small_out))
-
-    def slot(which, part_at, dp_at):
-        return out_ref.at[:, part_at, dp_at] if which == 0 else small_out.at[part_at, dp_at]
-
+    greet([(dp, other) for other in columns] + near[1:] + [partner])
     first = [
         [
-            send(pairs[which][0], slot(which, part, dp), za_send.at[which, step], za_recv.at[which, step], (dp, other))
-            for which in range(2)
+            push(src, dst.at[dp, part], za_send.at[which, step], za_recv.at[which, step], (dp, other))
+            for which, (src, dst) in enumerate(pairs)
         ]
         for step, other in enumerate(columns)
     ]
-    own.wait()
-    own_small.wait()
+    for listed in first:
+        for copy in listed:
+            copy.start()
+    for copy in locals_:
+        copy.wait()
     second = [[], [], [], []]
     third = []
+
+    def start(listed, copy):
+        copy.start()
+        listed.append(copy)
+
     for turn in range(4):
         part_at = lax.rem(part + 4 - turn, 4)
         if turn:
             for copy in first[turn - 1]:
                 copy.wait()
-        for step, other in enumerate(planes):
-            for which in range(2):
-                second[turn].append(
-                    send(
-                        slot(which, part_at, dp), slot(which, part_at, dp),
-                        yx_send.at[turn, which, step], yx_recv.at[turn, which, step],
-                        (other * 2 + core, part),
-                    )
+        for which, (_, dst) in enumerate(pairs):
+            spot = dst.at[dp, part_at]
+            for step in range(3):
+                start(
+                    second[turn],
+                    push(spot, spot, yx_send.at[turn, which, step], yx_recv.at[turn, which, step], near[step + 1]),
                 )
-        for which in range(2):
-            third.append(
-                send(
-                    slot(which, part_at, dp), slot(which, part_at, dp),
-                    cc_send.at[turn, which, 0], cc_recv.at[turn, which, 0], partner,
-                )
-            )
+            start(third, push(spot, spot, cc_send.at[turn, which, 0], cc_recv.at[turn, which, 0], partner))
     for turn in range(4):
         part_at = lax.rem(part + 4 - turn, 4)
-        for step in range(3):
-            for which in range(2):
-                second[turn][step * 2 + which].wait()
-                dp_at = lax.rem(place + 3 - step, 4) * 2 + core
-                third.append(
-                    send(
-                        slot(which, part_at, dp_at), slot(which, part_at, dp_at),
-                        cc_send.at[turn, which, step + 1], cc_recv.at[turn, which, step + 1], partner,
-                    )
+        for which, (_, dst) in enumerate(pairs):
+            for step in range(3):
+                second[turn][which * 3 + step].wait()
+                spot = dst.at[near[step + 1][0], part_at]
+                start(
+                    third,
+                    push(spot, spot, cc_send.at[turn, which, step + 1], cc_recv.at[turn, which, step + 1], partner),
                 )
     for copy in third:
         copy.wait()
 
 
 def spread(block, small):
-    any_spec = pl.BlockSpec(memory_space=pl.ANY)
     vmem_spec = pl.BlockSpec(memory_space=pltpu.VMEM)
-    dma = pltpu.SemaphoreType.DMA
     return pl.pallas_call(
         spread_kernel,
         out_shape=(
-            jax.ShapeDtypeStruct((block.shape[0], 4, 8) + block.shape[1:], block.dtype),
-            jax.ShapeDtypeStruct((4, 8) + small.shape, small.dtype),
+            jax.ShapeDtypeStruct((8, 4) + block.shape, block.dtype),
+            jax.ShapeDtypeStruct((8, 4) + small.shape, small.dtype),
         ),
         in_specs=[vmem_spec, vmem_spec],
-        out_specs=(any_spec, any_spec),
+        out_specs=(ANY_SPEC, ANY_SPEC),
         scratch_shapes=[
-            dma((2,)), dma((2, 3)), dma((2, 3)), dma((4, 2, 3)), dma((4, 2, 3)), dma((4, 2, 4)), dma((4, 2, 4)),
+            DMA((2,)), DMA((2, 3)), DMA((2, 3)), DMA((4, 2, 3)), DMA((4, 2, 3)), DMA((4, 2, 4)), DMA((4, 2, 4)),
         ],
-        compiler_params=pltpu.CompilerParams(
-            collective_id=1, has_side_effects=True, vmem_limit_bytes=VMEM_LIMIT
-        ),
+        compiler_params=comm_params(1),
         name="spread",
     )(block, small)
 
 
-def join_kernel(in_ref, out_ref, held, local_sem, send_sem, recv_sem):
-    dp, part = lax.axis_index("dp"), lax.axis_index("tensor")
-    core = dp % 2
-    partner = (dp // 2 * 2 + 1 - core, part)
-    loads = [
-        pltpu.make_async_copy(in_ref.at[:, which], held.at[which], local_sem.at[0, which])
-        for which in range(2)
-    ]
-    for load in loads:
-        load.start()
-    greet([partner])
-    copies = [
-        pltpu.make_async_remote_copy(
-            src_ref=in_ref.at[:, which],
-            dst_ref=out_ref.at[which, :, core],
-            send_sem=send_sem.at[which],
-            recv_sem=recv_sem.at[which],
-            device_id=partner,
-            device_id_type=MESH,
-        )
-        for which in range(2)
-    ]
-    for copy in copies:
-        copy.start()
-    stores = [
-        pltpu.make_async_copy(held.at[which], out_ref.at[which, :, core], local_sem.at[1, which])
-        for which in range(2)
-    ]
-    for which in range(2):
-        loads[which].wait()
-        stores[which].start()
-    for copy in stores + copies:
-        copy.wait()
-
-
-def join(pieces):
-    any_spec = pl.BlockSpec(memory_space=pl.ANY)
-    dma = pltpu.SemaphoreType.DMA
-    count, _, rows, width = pieces.shape
+def gather_sums_kernel(
+    large_ref, small_ref, large_out, small_out,
+    own_a, own_b, chip_a, chip_b, sum_a, sum_b, near_a, near_b, col_a, col_b, part_a, part_b,
+    local_sem, chip_send, chip_recv, near_send, near_recv, col_send, col_recv,
+):
+    place, core, part, near, partner = relatives()
+    dp = place * 2 + core
+    columns = [lax.rem(part + step, 4) for step in range(1, 4)]
+    spots = [place] + [near[step][0] // 2 for step in range(1, 4)]
+    order = (3, 1, 2, 0)
+    sets = (
+        (large_ref, own_a, chip_a, sum_a, near_a, col_a, part_a),
+        (small_ref, own_b, chip_b, sum_b, near_b, col_b, part_b),
+    )
+    loads = {}
+    for step in order:
+        for which, (src, own, *_) in enumerate(sets):
+            loads[which, step] = pltpu.make_async_copy(
+                src.at[spots[step], core], own.at[step], local_sem.at[which, step]
+            )
+            loads[which, step].start()
+    greet([(dp, other) for other in columns] + near[1:] + [partner])
+    chips, nears, cols = {}, {}, {}
+    for step in order:
+        for which, (src, own, chip, *_) in enumerate(sets):
+            chips[which, step] = push(
+                src.at[spots[step], 1 - core], chip.at[step],
+                chip_send.at[which, step], chip_recv.at[which, step], partner,
+            )
+            chips[which, step].start()
+    for step in order:
+        for which, (src, own, chip, total, arrived, *_) in enumerate(sets):
+            loads[which, step].wait()
+            chips[which, step].wait()
+            total[step] = (own[step].astype(f32) + chip[step].astype(f32)).astype(total.dtype)
+            if step:
+                nears[which, step] = push(
+                    total.at[step], arrived.at[step - 1],
+                    near_send.at[which, step - 1], near_recv.at[which, step - 1], near[step],
+                )
+                nears[which, step].start()
+    for which, (src, own, chip, total, arrived, column, partial_sum) in enumerate(sets):
+        for step in order[:3]:
+            nears[which, step].wait()
+        partial_sum[...] = (
+            total[0].astype(f32)
+            + arrived[0].astype(f32)
+            + arrived[1].astype(f32)
+            + arrived[2].astype(f32)
+        ).astype(partial_sum.dtype)
+        for step, other in enumerate(columns):
+            cols[which, step] = push(
+                partial_sum.at[other], column.at[step],
+                col_send.at[which, step], col_recv.at[which, step], (dp, other),
+            )
+            cols[which, step].start()
+    for which, out in enumerate((large_out, small_out)):
+        _, _, _, _, _, column, partial_sum = sets[which]
+        for step in range(3):
+            cols[which, step].wait()
+        out[...] = (
+            partial_sum[part].astype(f32)
+            + column[0].astype(f32)
+            + column[1].astype(f32)
+            + column[2].astype(f32)
+        )
+
+
+def gather_sums(large, small):
+    blocks = (large.shape[2:], small.shape[2:])
+    kinds = (large.dtype, small.dtype)
+    two = lambda lead: [pltpu.VMEM(lead(block), kind) for block, kind in zip(blocks, kinds)]
+    vmem_spec = pl.BlockSpec(memory_space=pltpu.VMEM)
     return pl.pallas_call(
-        join_kernel,
-        out_shape=jax.ShapeDtypeStruct((2, count, 2, rows, width), pieces.dtype),
-        in_specs=[any_spec],
-        out_specs=any_spec,
-        scratch_shapes=[
-            pltpu.VMEM((2, count, rows, width), pieces.dtype), dma((2, 2)), dma((2,)), dma((2,)),
-        ],
-        compiler_params=pltpu.CompilerParams(
-            collective_id=2, has_side_effects=True, vmem_limit_bytes=VMEM_LIMIT
-        ),
-        name="join",
-    )(pieces)
+        gather_sums_kernel,
+        out_shape=tuple(jax.ShapeDtypeStruct(block[1:], f32) for block in blocks),
+        in_specs=[ANY_SPEC, ANY_SPEC],
+        out_specs=(vmem_spec, vmem_spec),
+        scratch_shapes=two(lambda block: (4,) + block)
+        + two(lambda block: (4,) + block)
+        + two(lambda block: (4,) + block)
+        + two(lambda block: (3,) + block)
+        + two(lambda block: (3,) + block[1:])
+        + two(lambda block: block)
+        + [DMA((2, 4)), DMA((2, 4)), DMA((2, 4)), DMA((2, 3)), DMA((2, 3)), DMA((2, 3)), DMA((2, 3))],
+        compiler_params=comm_params(2),
+        name="gather_sums",
+    )(large, small)
 
 
 def standard(rows):
@@ -698,6 +735,9 @@
     scores = nt(query, key) * (HD ** (-0.5))
     slots = lax.broadcasted_iota(jnp.int32, scores.shape, 1)
     return jnp.where(slots < LEN, scores, far_negative)
+
+
+WEIGHT_SPEC = pl.BlockSpec((8, 1, D // 8, D), lambda turn: (0, turn, 0, 0))
 
 
 def attend_kernel(
@@ -706,6 +746,7 @@
 ):
     turn = pl.program_id(0)
     images = hidden_ref.shape[0] // SEQ
+    weight = weight_ref[:, 0].reshape(D, D)
 
     @pl.when(turn == 0)
     def _():
@@ -715,7 +756,7 @@
 
     for image in range(images):
         rows = pl.ds(image * SEQ, SEQ)
-        mixed = nn(first_sc[rows, :], weight_ref[0, :, :QKV]).astype(bf16)
+        mixed = nn(first_sc[rows, :], weight[:, :QKV]).astype(bf16)
         logs = jnp.zeros((SEQ, 128), f32)
         contexts = []
         for head in range(HEADS_PART):
@@ -733,7 +774,7 @@
         context = jnp.concatenate(contexts, axis=1)
         saved_ref[0, rows, :] = jnp.concatenate([mixed, context], axis=1)
         logs_ref[0, rows, :] = logs
-        attn_sc[rows, :] += nt(context, weight_ref[0, :, QKV:])
+        attn_sc[rows, :] += nt(context, weight[:, QKV:])
 
     @pl.when(turn == pl.num_programs(0) - 1)
     def _():
@@ -758,7 +799,7 @@
     return pl.pallas_call(
         attend_kernel,
         grid=(4,),
-        in_specs=[whole((rows, D)), by_part((D, D)), whole((8, D)), whole((D, 128))],
+        in_specs=[whole((rows, D)), WEIGHT_SPEC, whole((8, D)), whole((D, 128))],
         out_specs=(
             whole((rows, D)), whole((rows, D)), by_part((rows, D)), whole((rows, 128)), by_part((rows, 128)),
         ),
@@ -791,6 +832,7 @@
     turn = pl.program_id(0)
     rows_all = grad_ref.shape[0]
     images = rows_all // SEQ
+    weight = weight_ref[:, 0].reshape(D, D)
     scale = HD ** (-0.5)
 
     @pl.when(turn == 0)
@@ -820,7 +862,7 @@
     for image in range(images):
         rows = pl.ds(image * SEQ, SEQ)
         saved = saved_ref[0, rows, :]
-        dcontext = nn(low_sc[rows, :], weight_ref[0, :, QKV:]).astype(bf16)
+        dcontext = nn(low_sc[rows, :], weight[:, QKV:]).astype(bf16)
         pieces = [[], [], []]
         for head in range(HEADS_PART):
             query, key, value = [
@@ -837,11 +879,11 @@
             pieces[1].append((tn(dscores, query) * scale).astype(bf16))
             pieces[2].append(dvalue.astype(bf16))
         mixed = jnp.concatenate(pieces[0] + pieces[1] + pieces[2], axis=1)
-        back_sc[rows, :] += nt(mixed, weight_ref[0, :, :QKV])
+        back_sc[rows, :] += nt(mixed, weight[:, :QKV])
         mixed_grads.append(mixed)
     mixed = jnp.concatenate(mixed_grads, axis=0)
-    wgrad_ref[0, :, :QKV] = tn(first_sc[...], mixed).astype(bf16)
-    wgrad_ref[0, :, QKV:] = tn(low_sc[...], saved_ref[0, :, QKV:]).astype(bf16)
+    wgrad = jnp.concatenate([tn(first_sc[...], mixed), tn(low_sc[...], saved_ref[0, :, QKV:])], axis=1)
+    wgrad_ref[:, 0] = wgrad.astype(bf16).reshape(8, D // 8, D)
 
     @pl.when(turn == pl.num_programs(0) - 1)
     def _():
@@ -863,12 +905,12 @@
         in_specs=[
             whole((rows, D)), whole((EXPERTS, rows, D)), whole((rows, D)), whole((rows, D)),
             by_part((rows, D)), whole((rows, 128)), by_part((rows, 128)), whole((rows, 128)),
-            by_part((D, D)), whole((8, D)), whole((D, 128)),
+            WEIGHT_SPEC, whole((8, D)), whole((D, 128)),
         ],
-        out_specs=(whole((rows, D)), by_part((D, D)), whole((8, D)), whole((D, 128))),
+        out_specs=(whole((rows, D)), WEIGHT_SPEC, whole((8, D)), whole((D, 128))),
         out_shape=(
             jax.ShapeDtypeStruct((rows, D), f32),
-            jax.ShapeDtypeStruct((4, D, D), bf16),
+            jax.ShapeDtypeStruct((8, 4, D // 8, D), bf16),
             jax.ShapeDtypeStruct((8, D), f32),
             jax.ShapeDtypeStruct((D, 128), f32),
         ),
@@ -896,141 +938,344 @@
 TILE = 256
 
 
-def expert_kernel(rows_ref, weight_ref, out_ref, act_ref, slope_ref, sum_sc):
-    turn = pl.program_id(1)
-    for at in range(0, rows_ref.shape[1], TILE):
-        tile = pl.ds(at, TILE)
-        act, slope = gelu_pair(nn(rows_ref[0, tile, :], weight_ref[0, turn]))
-        act = act.astype(bf16)
-        act_ref[0, tile, :] = act
-        slope_ref[0, tile, :] = slope.astype(bf16)
-        part = nt(act, weight_ref[1, turn])
-        sum_sc[tile, :] = jnp.where(turn == 0, part, sum_sc[tile, :] + part)
-
-    @pl.when(turn == pl.num_programs(1) - 1)
-    def _():
-        out_ref[0] = sum_sc[...].astype(bf16)
-
-
-def expert_rows(rows, weights):
-    groups, count, _ = rows.shape
+def weight_of(held, which, turn):
+    return held[which, pl.ds(turn * 4, 4)].reshape(D, D)
+
+
+def expert_kernel(
+    second_ref, pieces_ref, rows_out, back_out, weights_out, act_out, slope_out,
+    held, weights, made, acts, slopes, total,
+    load_sem, join_send, join_recv, row_send, row_recv, pass_send, pass_recv, back_send, back_recv, out_sem, save_sem,
+):
+    _, core, _, near, partner = relatives()
+    count = second_ref.shape[0]
+    half = count // 2
+    load = pltpu.make_async_copy(second_ref, held.at[0], load_sem.at[2])
+    load.start()
+    joins = []
+    for which in range(2):
+        src, dst = pieces_ref.at[:, which], weights.at[which, :, core]
+        joins.append(pltpu.make_async_copy(src, dst, load_sem.at[which]))
+        joins[-1].start()
+    greet(near[1:] + [partner])
+    for which in range(2):
+        src, dst = pieces_ref.at[:, which], weights.at[which, :, core]
+        joins.append(push(src, dst, join_send.at[which], join_recv.at[which], partner))
+        joins[-1].start()
+    rows = [
+        push(second_ref, held.at[step], row_send.at[step - 1], row_recv.at[step - 1], near[step])
+        for step in (1, 2)
+    ]
+    for copy in rows:
+        copy.start()
+    low, high = pl.ds(0, half), pl.ds(half, half)
+    passed = [
+        push(held.at[1, low], held.at[3, low], pass_send.at[0], pass_recv.at[0], near[2]),
+        push(held.at[2, high], held.at[3, high], pass_send.at[1], pass_recv.at[1], near[1]),
+    ]
+    backs = [pltpu.make_async_copy(made.at[0], back_out.at[0], save_sem.at[2])] + [
+        push(made.at[step], back_out.at[step], back_send.at[step - 1], back_recv.at[step - 1], near[step])
+        for step in (1, 2, 3)
+    ]
+    save_rows = pltpu.make_async_copy(held, rows_out, save_sem.at[0])
+    save_weights = pltpu.make_async_copy(weights, weights_out, save_sem.at[1])
+    load.wait()
+    for copy in joins:
+        copy.wait()
+    save_weights.start()
+
+    def outs(slot, step, turn):
+        place = pl.ds(pl.multiple_of(step * count, count), count)
+        return (
+            pltpu.make_async_copy(acts.at[slot], act_out.at[turn, place], out_sem.at[0, slot]),
+            pltpu.make_async_copy(slopes.at[slot], slope_out.at[turn, place], out_sem.at[1, slot]),
+        )
+
+    def chunk(step, carry):
+        @pl.when(step == 1)
+        def _():
+            for copy in rows:
+                copy.wait()
+            for copy in passed:
+                copy.start()
+
+        @pl.when(step == 3)
+        def _():
+            for copy in passed:
+                copy.wait()
+            save_rows.start()
+
+        def part(turn, carry):
+            slot = lax.rem(turn, 2)
+
+            @pl.when(step * 4 + turn >= 2)
+            def _():
+                for copy in outs(slot, step, turn):
+                    copy.wait()
+
+            for at in range(0, count, TILE):
+                tile = pl.ds(at, TILE)
+                act, slope = gelu_pair(nn(held[step, tile, :], weight_of(weights, 0, turn)))
+                act = act.astype(bf16)
+                acts[slot, tile, :] = act
+                slopes[slot, tile, :] = slope.astype(bf16)
+                product = nt(act, weight_of(weights, 1, turn))
+                total[tile, :] = jnp.where(turn == 0, product, total[tile, :] + product)
+            for copy in outs(slot, step, turn):
+                copy.start()
+            return carry
+
+        lax.fori_loop(0, 4, part, 0)
+        made[step] = total[...].astype(bf16)
+        for at in range(4):
+
+            @pl.when(step == at)
+            def _():
+                backs[at].start()
+
+        return carry
+
+    lax.fori_loop(0, 4, chunk, 0)
+    for slot in range(2):
+        for copy in outs(slot, 3, 2 + slot):
+            copy.wait()
+    save_rows.wait()
+    save_weights.wait()
+    for copy in backs:
+        copy.wait()
+
+
+def expert_rows(second, pieces):
+    count = second.shape[0]
+    block = (count, D)
+    weight_shape = (2, 16, 2, D // 8, D)
     return pl.pallas_call(
         expert_kernel,
-        grid=(groups, 4),
-        in_specs=[
-            pl.BlockSpec((1, count, D), lambda at, turn: (at, 0, 0)),
-            pl.BlockSpec((2, 4, D, D), lambda at, turn: (0, 0, 0, 0), pipeline_mode=pl.Buffered(1)),
+        in_specs=[ANY_SPEC, ANY_SPEC],
+        out_specs=(ANY_SPEC,) * 5,
+        out_shape=(
+            jax.ShapeDtypeStruct((4,) + block, bf16),
+            jax.ShapeDtypeStruct((4,) + block, bf16),
+            jax.ShapeDtypeStruct(weight_shape, bf16),
+            jax.ShapeDtypeStruct((4, 4 * count, D), bf16),
+            jax.ShapeDtypeStruct((4, 4 * count, D), bf16),
+        ),
+        scratch_shapes=[
+            pltpu.VMEM((4,) + block, bf16),
+            pltpu.VMEM(weight_shape, bf16),
+            pltpu.VMEM((4,) + block, bf16),
+            pltpu.VMEM((2,) + block, bf16),
+            pltpu.VMEM((2,) + block, bf16),
+            pltpu.VMEM(block, f32),
+            DMA((3,)), DMA((2,)), DMA((2,)), DMA((2,)), DMA((2,)), DMA((2,)), DMA((2,)),
+            DMA((3,)), DMA((3,)), DMA((2, 2)), DMA((3,)),
         ],
-        out_specs=(
-            pl.BlockSpec((1, count, D), lambda at, turn: (at, 0, 0)),
-            pl.BlockSpec((1, count, D), lambda at, turn: (turn, at, 0)),
-            pl.BlockSpec((1, count, D), lambda at, turn: (turn, at, 0)),
-        ),
-        out_shape=(
-            jax.ShapeDtypeStruct((groups, count, D), bf16),
-            jax.ShapeDtypeStruct((4, groups * count, D), bf16),
-            jax.ShapeDtypeStruct((4, groups * count, D), bf16),
-        ),
-        scratch_shapes=[pltpu.VMEM((count, D), f32)],
-        compiler_params=pltpu.CompilerParams(vmem_limit_bytes=VMEM_LIMIT),
+        compiler_params=comm_params(4),
         name="expert_rows",
-    )(rows, weights)
-
-
-def expert_pull_kernel(rows_ref, grad_ref, act_ref, slope_ref, weight_ref, out_ref, wgrad_ref, sum_sc, pre_sc):
-    step = pl.program_id(0)
-    groups, count, _ = rows_ref.shape
-    last = groups * 4
-
-    @pl.when(step < last)
-    def _():
-        at, turn = step // 4, step % 4
-        for place in range(0, count, TILE):
-            tile = pl.ds(place, TILE)
-            dact = nn(grad_ref[at, tile, :], weight_ref[1, turn])
-            dpre = (slope_ref[0, tile, :].astype(f32) * dact).astype(bf16)
-            pre_sc[turn, pl.ds(at * count + place, TILE), :] = dpre
-            part = nt(dpre, weight_ref[0, turn])
-            sum_sc[tile, :] = jnp.where(turn == 0, part, sum_sc[tile, :] + part)
-
-        @pl.when(turn == 3)
+    )(second, pieces)
+
+
+def expert_pull_kernel(
+    sent_ref, rows_ref, act_ref, slope_ref, weights_ref, moved_out, wgrad_out,
+    grads, rows, weights, pres, made, slopes, acts, total, halves, arrived,
+    load_sem, row_send, row_recv, back_send, back_recv, slope_sem, act_sem, chip_send, chip_recv, save_sem,
+):
+    _, core, _, near, partner = relatives()
+    count = sent_ref.shape[1]
+    own = pltpu.make_async_copy(sent_ref.at[0], grads.at[0], load_sem.at[0])
+    load_weights = pltpu.make_async_copy(weights_ref, weights, load_sem.at[1])
+    load_rows = pltpu.make_async_copy(rows_ref, rows, load_sem.at[2])
+
+    def slope_load(step, turn, slot):
+        place = pl.ds(pl.multiple_of(step * count, count), count)
+        return pltpu.make_async_copy(slope_ref.at[turn, place], slopes.at[slot], slope_sem.at[slot])
+
+    def act_load(turn, slot):
+        return pltpu.make_async_copy(act_ref.at[turn], acts.at[slot], act_sem.at[slot])
+
+    own.start()
+    load_weights.start()
+    for slot in range(2):
+        slope_load(0, slot, slot).start()
+    load_rows.start()
+    for slot in range(2):
+        act_load(slot, slot).start()
+    greet(near[1:] + [partner])
+    sends = [None] + [
+        push(sent_ref.at[step], grads.at[step], row_send.at[step - 1], row_recv.at[step - 1], near[step])
+        for step in (1, 2, 3)
+    ]
+    sends[1].start()
+    sends[2].start()
+    backs = [pltpu.make_async_copy(made.at[0], moved_out.at[0], load_sem.at[3])] + [
+        push(made.at[step], moved_out.at[step], back_send.at[step - 1], back_recv.at[step - 1], near[step])
+        for step in (1, 2, 3)
+    ]
+    own.wait()
+    load_weights.wait()
+
+    def chunk(step, carry):
+        @pl.when(step == 1)
         def _():
-            out_ref[0] = sum_sc[...].astype(bf16)
-
-    @pl.when(step >= last)
-    def _():
-        turn = step - last
-        rows = rows_ref[...].reshape(groups * count, D)
-        grads = grad_ref[...].reshape(groups * count, D)
-        wgrad_ref[0, 0] = tn(rows, pre_sc[turn]).astype(bf16)
-        wgrad_ref[1, 0] = tn(grads, act_ref[0]).astype(bf16)
-
-
-def expert_pull(rows, grads, act, slope, weights):
-    groups, count, _ = rows.shape
-    last = groups * 4
-    early = lambda step: jnp.minimum(step, last - 1)
-    late = lambda step: jnp.maximum(step - last, 0)
-    whole = lambda shape: pl.BlockSpec(
-        shape, lambda step: (0,) * len(shape), pipeline_mode=pl.Buffered(1)
-    )
+            sends[3].start()
+
+        for at in (1, 2, 3):
+
+            @pl.when(step == at)
+            def _():
+                sends[at].wait()
+
+        def part(turn, carry):
+            slot = lax.rem(turn, 2)
+            slope_load(step, turn, slot).wait()
+            for at in range(0, count, TILE):
+                tile = pl.ds(at, TILE)
+                dact = nn(grads[step, tile, :], weight_of(weights, 1, turn))
+                dpre = (slopes[slot, tile, :].astype(f32) * dact).astype(bf16)
+                pres[turn, step, tile, :] = dpre
+                product = nt(dpre, weight_of(weights, 0, turn))
+                total[tile, :] = jnp.where(turn == 0, product, total[tile, :] + product)
+
+            @pl.when(step * 4 + turn < 14)
+            def _():
+                after = step * 4 + turn + 2
+                slope_load(after // 4, after % 4, slot).start()
+
+            return carry
+
+        lax.fori_loop(0, 4, part, 0)
+        made[step] = total[...].astype(bf16)
+        for at in range(4):
+
+            @pl.when(step == at)
+            def _():
+                backs[at].start()
+
+        return carry
+
+    lax.fori_loop(0, 4, chunk, 0)
+    load_rows.wait()
+
+    def chip_copy(which, turn):
+        return push(
+            halves.at[which, turn, :, 1 - core], arrived.at[which, turn],
+            chip_send.at[which, turn], chip_recv.at[which, turn], partner,
+        )
+
+    def save(which, turn):
+        return pltpu.make_async_copy(arrived.at[which, turn], wgrad_out.at[turn, :, which], save_sem.at[which, turn])
+
+    def finish(turn):
+        for which in range(2):
+            chip_copy(which, turn).wait()
+            arrived[which, turn] = (
+                halves[which, turn, :, core].astype(f32) + arrived[which, turn].astype(f32)
+            ).astype(bf16)
+            save(which, turn).start()
+
+    def wgrad(turn, carry):
+        slot = lax.rem(turn, 2)
+        flat = (4 * count, D)
+        act_load(turn, slot).wait()
+        first = tn(rows[...].reshape(flat), pres[turn].reshape(flat))
+        halves[0, turn] = first.astype(bf16).reshape(4, 2, D // 8, D)
+        chip_copy(0, turn).start()
+        second = tn(grads[...].reshape(flat), acts[slot])
+        halves[1, turn] = second.astype(bf16).reshape(4, 2, D // 8, D)
+        chip_copy(1, turn).start()
+
+        @pl.when(turn < 2)
+        def _():
+            act_load(turn + 2, slot).start()
+
+        @pl.when(turn > 0)
+        def _():
+            finish(turn - 1)
+
+        return carry
+
+    lax.fori_loop(0, 4, wgrad, 0)
+    finish(3)
+    for turn in range(4):
+        for which in range(2):
+            save(which, turn).wait()
+    for copy in backs:
+        copy.wait()
+
+
+def expert_pull(sent, rows, act, slope, weights):
+    count = sent.shape[1]
+    block = (count, D)
+    slices = D // 8
     return pl.pallas_call(
         expert_pull_kernel,
-        grid=(last + 4,),
-        in_specs=[
-            whole((groups, count, D)),
-            whole((groups, count, D)),
-            pl.BlockSpec((1, groups * count, D), lambda step: (late(step), 0, 0)),
-            pl.BlockSpec((1, count, D), lambda step: (early(step) % 4, early(step) // 4, 0)),
-            whole((2, 4, D, D)),
-        ],
-        out_specs=(
-            pl.BlockSpec((1, count, D), lambda step: (early(step) // 4, 0, 0)),
-            pl.BlockSpec((2, 1, D, D), lambda step: (0, late(step), 0, 0)),
-        ),
+        in_specs=[ANY_SPEC] * 5,
+        out_specs=(ANY_SPEC, ANY_SPEC),
         out_shape=(
-            jax.ShapeDtypeStruct((groups, count, D), bf16),
-            jax.ShapeDtypeStruct((2, 4, D, D), bf16),
+            jax.ShapeDtypeStruct((4,) + block, bf16),
+            jax.ShapeDtypeStruct((4, 4, 2, slices, D), bf16),
         ),
         scratch_shapes=[
-            pltpu.VMEM((count, D), f32),
-            pltpu.VMEM((4, groups * count, D), bf16),
+            pltpu.VMEM((4,) + block, bf16),
+            pltpu.VMEM((4,) + block, bf16),
+            pltpu.VMEM(weights.shape, bf16),
+            pltpu.VMEM((4, 4) + block, bf16),
+            pltpu.VMEM((4,) + block, bf16),
+            pltpu.VMEM((2,) + block, bf16),
+            pltpu.VMEM((2, 4 * count, D), bf16),
+            pltpu.VMEM(block, f32),
+            pltpu.VMEM((2, 4, 4, 2, slices, D), bf16),
+            pltpu.VMEM((2, 4, 4, slices, D), bf16),
+            DMA((4,)), DMA((3,)), DMA((3,)), DMA((3,)), DMA((3,)), DMA((2,)), DMA((2,)),
+            DMA((2, 4)), DMA((2, 4)), DMA((2, 4)),
         ],
-        compiler_params=pltpu.CompilerParams(vmem_limit_bytes=VMEM_LIMIT),
+        compiler_params=comm_params(5),
         name="expert_pull",
-    )(rows, grads, act, slope, weights)
-
-
-def add_up(pieces, own):
-    return sum(pieces[at].astype(f32) for at in range(pieces.shape[0])).astype(own)
+    )(sent, rows, act, slope, weights)
 
 
 def per_device(
     tokens, counts, routes, norm_gain, norm_bias, w_router, w_qkv, w_out, w_in, w_back, cotangent
 ):
     dp, part = lax.axis_index("dp"), lax.axis_index("tensor")
-    core = dp % 2
+    place = dp // 2
     own_rows = tokens.shape[0]
     slices = D // 8
     row_ids = part * own_rows + jnp.arange(own_rows, dtype=jnp.int32)
     image_count = lax.dynamic_index_in_dim(counts, dp, keepdims=False)
     valid = ((row_ids // SEQ < image_count) & (row_ids % SEQ < LEN)).astype(f32)[:, None]
     my_routes = lax.dynamic_slice_in_dim(routes, part * own_rows, own_rows, axis=1)
-    chosen = (my_routes[:, :, :, None] == jnp.arange(EXPERTS)).any(axis=2)
-
-    pieces = []
-    for layer in range(LAYERS):
-        packed = jnp.stack([w_in[layer], w_back[layer]], axis=1)
-        arrived = swap(packed, "plane", False, 3)
-        pieces.append(lax.all_gather(arrived, "tensor", axis=0, tiled=True))
-
-    mixed_in = jnp.transpose(w_qkv, (0, 2, 1, 3)).reshape(LAYERS, slices, QKV)
-    attn_block = jnp.concatenate([mixed_in, jnp.transpose(w_out, (0, 2, 1))], axis=2)
+    row, col = place // 2, place % 2
+    served = jnp.stack([place, row * 2 + 1 - col, (1 - row) * 2 + col, (1 - row) * 2 + 1 - col])
+    expert_of = served[:, None] == jnp.arange(EXPERTS)[None, :]
+    chosen = (my_routes[:, :, :, None] == served).any(axis=2)
+
+    def by_place(table):
+        return jnp.sum(jnp.where(expert_of[None], table[:, None, :], 0.0), axis=-1)
+
+    attn_blocks = jnp.concatenate(
+        [
+            jnp.transpose(w_qkv, (0, 2, 1, 3)).reshape(LAYERS, slices, QKV),
+            jnp.transpose(w_out, (0, 2, 1)),
+        ],
+        axis=2,
+    )
     small = jnp.concatenate([norm_gain, norm_bias, w_router])
     small = jnp.pad(small, (0, 2048 - small.shape[0])).reshape(16, 128)
-    attn_all, small_all = spread(attn_block, small)
-    attn_all = attn_all.reshape(LAYERS, 4, D, D)
-    flat = jnp.transpose(small_all.reshape(4, 8, 2048), (1, 0, 2)).reshape(32, 2048)
+
+    def expert_pieces(layer, after):
+        packed = jnp.stack([w_in[layer], w_back[layer]], axis=1)
+        packed, _ = lax.optimization_barrier((packed, after))
+        arrived = swap(packed, "plane", False, 3)
+        return lax.all_gather(arrived, "tensor", axis=0, tiled=True)
+
+    pieces = [expert_pieces(0, small), None]
+    attn_first, small_all = spread(attn_blocks[0], small)
+    attn_later = [
+        lax.all_gather(attn_blocks[layer], ("dp", "tensor"), axis=0, tiled=False) for layer in range(1, LAYERS)
+    ]
+    attn_all = [attn_first] + [each.reshape(8, 4, slices, D) for each in attn_later]
+    flat = small_all.reshape(32, 2048)
     vec_count = LAYERS * 2 * D // 32
     gains = flat[:, :vec_count].reshape(LAYERS, 2, D).astype(f32)
     biases = flat[:, vec_count : 2 * vec_count].reshape(LAYERS, 2, D).astype(f32)
@@ -1045,12 +1290,11 @@
     stats = []
     for layer in range(LAYERS):
         resid, second, saved, table, logs = attend_rows(hidden, attn_all[layer], vecs[layer], routers[layer])
-        rows = swap(second, "plane", True, 4)
-        weights = join(pieces[layer]).reshape(2, 4, D, D)
-        made, act, slope = expert_rows(rows, weights)
-        back = swap(made, "plane", False, 5)
-        gates = jnp.where(chosen[layer], table[:, :EXPERTS], 0.0)
-        moe = sum(gates[:, e : e + 1] * back[e].astype(f32) for e in range(EXPERTS))
+        if layer + 1 < LAYERS:
+            pieces[layer + 1] = expert_pieces(layer + 1, second[:8, :128])
+        rows, back, weights, act, slope = expert_rows(second, pieces[layer])
+        gates = jnp.where(chosen[layer], by_place(table[:, :EXPERTS]), 0.0)
+        moe = sum(gates[:, at : at + 1] * back[at].astype(f32) for at in range(EXPERTS))
         result = resid + moe
         stats.append(
             jnp.stack(
@@ -1065,34 +1309,28 @@
         hidden = result
 
     grad = cotangent.astype(f32) * valid
-    attn_grads, expert_grads, small_grads, router_grads = [], [], [], []
+    attn_grads, owned, small_grads, router_grads = [], [], [], []
     for layer in reversed(range(LAYERS)):
         before, resid, saved, table, logs, rows, weights, act, slope, back, gates = kept[layer]
         low = grad.astype(bf16)
-        dgate = [jnp.sum(back[e].astype(f32) * low.astype(f32), axis=-1) for e in range(EXPERTS)]
-        dprob = jnp.where(chosen[layer], jnp.stack(dgate, axis=1), 0.0)
+        dgate = [jnp.sum(back[at].astype(f32) * low.astype(f32), axis=-1) for at in range(EXPERTS)]
+        dprob = by_place(jnp.where(chosen[layer], jnp.stack(dgate, axis=1), 0.0))
         dprob = jnp.pad(dprob, ((0, 0), (0, 128 - EXPERTS)))
-        sent = jnp.stack([(gates[:, e : e + 1] * low.astype(f32)).astype(bf16) for e in range(EXPERTS)])
-        arrived = swap(sent, "plane", False, 5)
-        drows, wgrad = expert_pull(rows, arrived, act, slope, weights)
-        moved = swap(drows, "plane", False, 5)
-        wgrad = wgrad.reshape(2, 4, 4, 2, slices, D)
-        halves = jnp.transpose(wgrad, (3, 1, 2, 0, 4, 5))
-        halves = add_up(swap(halves, "chip", False, 6), bf16)
-        summed = lax.psum_scatter(halves, "tensor", scatter_dimension=0, tiled=False)
-        expert_grads.append(summed)
+        sent = jnp.stack([(gates[:, at : at + 1] * low.astype(f32)).astype(bf16) for at in range(EXPERTS)])
+        moved, wgrad = expert_pull(sent, rows, act, slope, weights)
+        summed = lax.psum_scatter(wgrad, "tensor", scatter_dimension=0, tiled=False)
+        owned.append(summed)
         grad, attn_wgrad, small_grad, router_grad = attend_pull(
             grad, moved, before, resid, saved, table, logs, dprob, attn_all[layer], vecs[layer], routers[layer]
         )
-        attn_wgrad = jnp.transpose(attn_wgrad.reshape(4, 4, 2, slices, D), (2, 1, 0, 3, 4))
-        attn_wgrad = add_up(swap(attn_wgrad, "chip", False, 7), bf16)
-        attn_wgrad = add_up(swap(attn_wgrad, "plane", False, 8), bf16)
-        attn_wgrad = add_up(swap(attn_wgrad, "column", False, 9), f32)
+        if layer:
+            attn_wgrad = lax.psum_scatter(
+                attn_wgrad.reshape(32, slices, D), ("dp", "tensor"), scatter_dimension=0, tiled=False
+            ).astype(f32)
         attn_grads.append(attn_wgrad)
         small_grads.append(small_grad[:4])
         router_grads.append(router_grad[:, :EXPERTS])
-    owned = [swap(each, "plane", False, 10) for each in expert_grads]
-    for listed in (attn_grads, owned, small_grads, router_grads):
+    for listed in (small_grads, router_grads, owned):
         listed.reverse()
 
     vec_grads = jnp.stack(small_grads).reshape(LAYERS, 2, 2, D)
@@ -1105,17 +1343,19 @@
         ],
         axis=1,
     )
-    packed = jnp.pad(packed, ((0, 0), (0, 1024 - packed.shape[1]))).reshape(32, 8, 128)
-    total = jnp.sum(swap(packed, "all", False, 11), axis=0).reshape(-1)
+    packed = jnp.pad(packed, ((0, 0), (0, 1024 - packed.shape[1]))).reshape(4, 2, 4, 8, 128)
+    last, total = gather_sums(attn_grads.pop().reshape(4, 2, 4, slices, D), packed)
+    attn_grad = jnp.stack([last] + attn_grads)
+    total = total.reshape(-1)
     share = LAYERS * 2 * D // 32
     router_share = LAYERS * D * EXPERTS // 32
     at = 2 * share + router_share
     denom = jnp.sum(counts).astype(f32) * (LEN * D)
     rms = jnp.sqrt(total[at : at + 3 * LAYERS].reshape(LAYERS, 3) / denom)
-    attn_grad = jnp.stack(attn_grads)
     qkv_grad = jnp.transpose(attn_grad[:, :, :QKV].reshape(LAYERS, slices, 3, QKV // 3), (0, 2, 1, 3))
     out_grad = jnp.transpose(attn_grad[:, :, QKV:], (0, 2, 1))
-    expert_grad = jnp.stack(owned).astype(f32)
+    expert_grad = swap(jnp.stack(owned, axis=1), "plane", False, 6).astype(f32)
+    expert_grad = jnp.transpose(expert_grad, (2, 1, 0, 3, 4))
     return (
         hidden,
         grad,
@@ -1124,8 +1364,8 @@
         total[2 * share : at],
         qkv_grad,
         out_grad,
-        expert_grad[:, :, 0],
-        expert_grad[:, :, 1],
+        expert_grad[0],
+        expert_grad[1],
         rms,
     )
 

time: 1020 us -> 851 us (0.83)
  Pallas kernels: 879 us -> 573 us
  waiting for transfers between devices: 0.13 us -> 197 us
  local copies, waits for them, and re-layouts: 54.1 us -> 23.7 us
  other arithmetic: 61.5 us -> 38 us
    pallas_call x21 -> x3, Pallas kernels: 517 us -> 63.6 us  [swap(): pl.pallas_call(partial(swap_kernel, kind, same), out_shape=jax.ShapeDtype...]
    pallas_call x9 -> x8, Pallas kernels: 301 us -> 447 us  [the longest x2 158 us: expert_pull(): pl.pallas_call(expert_pull_kernel, in_specs=[ANY_SPEC] * 5, out_specs=(AN...]
    all_gather x2 -> x3, waiting for transfers between devices: 0.04 us -> 101 us  [the longest x2 96.7 us: expert_pieces(): return lax.all_gather(arrived, 'tensor', axis=0, tiled=True)]
    reduce_scatter x2 -> x3, waiting for transfers between devices: 0.02 us -> 95.5 us  [the longest x2 95.5 us: per_device(): summed = lax.psum_scatter(wgrad, 'tensor', scatter_dimension=0, tiled=False)]
    reshape x7 -> x1, local copies, waits for them, and re-layouts: 27.3 us -> 0.19 us  [per_device(): jnp.transpose(w_qkv, (0, 2, 1, 3)).reshape(LAYERS, slices, QKV)]
    convert_element_type x5 -> x1, other arithmetic: 25.9 us -> 0.93 us  [per_device(): attn_wgrad = lax.psum_scatter(attn_wgrad.reshape(32, slices, D), ('dp', '...]
  transfers between devices with their start and end apart: 4 -> 6, of which waited for: 0 -> 5; matrix products, arithmetic and copies ran while one was open for 8% -> 4% of each run, Pallas kernels for 65% -> 41%
where the time goes in v2:
time: 851 us; the launch traced here: 848 us
  Pallas kernels  573 us (67%)
  waiting for transfers between devices  197 us (23%)
  other arithmetic  38 us (4%)
  local copies, waits for them, and re-layouts  23.7 us (3%)
  between operations  15.6 us (2%)
    pallas_call x2, Pallas kernels, expert_pull(): pl.pallas_call(expert_pull_kernel, in_specs=[ANY_SPEC] * 5, out_specs=(AN...  158 us
    pallas_call x2, Pallas kernels, expert_rows(): pl.pallas_call(expert_kernel, in_specs=[ANY_SPEC, ANY_SPEC], out_specs=(A...  149 us
    all_gather x2, waiting for transfers between devices, expert_pieces(): return lax.all_gather(arrived, 'tensor', axis=0, tiled=True)  96.7 us
    reduce_scatter x2, waiting for transfers between devices, per_device(): summed = lax.psum_scatter(wgrad, 'tensor', scatter_dimension=0, tiled=False)  95.5 us
    pallas_call x1, Pallas kernels, gather_sums(): pl.pallas_call(gather_sums_kernel, out_shape=tuple((jax.ShapeDtypeStruct(...  67.9 us
    pallas_call x3, Pallas kernels, swap(): pl.pallas_call(partial(swap_kernel, kind, same), out_shape=jax.ShapeDtype...  63.6 us
    pallas_call x2, Pallas kernels, attend_pull(): pl.pallas_call(attend_pull_kernel, grid=(4,), in_specs=[whole((rows, D)),...  61.8 us
    pallas_call x1, Pallas kernels, spread(): pl.pallas_call(spread_kernel, out_shape=(jax.ShapeDtypeStruct((8, 4) + bl...  41.1 us
  transfers between devices with their start and end apart: 6, of which 5 were waited for; matrix products, arithmetic and copies ran while one was open for 4% of the time, Pallas kernels for 41%

profile of v2, /device:TPU:0, one launch (start us, length us, event | category | flops | bytes accessed | tf_op | source)
XLA Modules:
  0.0 847.6 jit_solution(18140968685563812880)
XLA Ops:
  11.8 18.0 %swap_plane_3.2 = bf16[4,2,96,768]{3,2,1,0:T(8,128)(2,1)} custom-call(bf16[4,2,96,768]{3,2,1,0:T(8,128)(2,1)} %get-tuple-element.52.in_ref), custom_call_target="tpu_custom_call" | custom-call | tf_op jit(solution)/shard_map/swap_plane_3/pallas_call | solution.py:513
  31.3 16.6 %swap_plane_3.3 = bf16[4,2,96,768]{3,2,1,0:T(8,128)(2,1)} custom-call(bf16[4,2,96,768]{3,2,1,0:T(8,128)(2,1)} %get-tuple-element.182.in_ref), custom_call_target="tpu_custom_call" | custom-call | tf_op jit(solution)/shard_map/swap_plane_3/pallas_call | solution.py:513
  48.0 41.1 %spread.1 = (bf16[8,4,96,768]{3,2,1,0:T(8,128)(2,1)}, bf16[8,4,16,128]{3,2,1,0:T(8,128)(2,1)}) custom-call(bf16[96,768]{1,0:T(8,128)(2,1)} %get-tuple-element.160.block_ref, bf16[16,128]{1,0:T(8,128)(2,1)} %fusion.47.small_ref), custom_call_target="tpu_custom_call" | custom-call | tf_op jit(solution)/shard_map/spread/pallas_call | solution.py:617
  92.4 15.6 %attend_rows.2 = (f32[512,768]{1,0:T(8,128)}, bf16[512,768]{1,0:T(8,128)(2,1)}, bf16[4,512,768]{2,1,0:T(8,128)(2,1)}, f32[512,128]{1,0:T(8,128)}, f32[4,512,128]{2,1,0:T(8,128)}) custom-call(bf16[512,768]{1,0:T(8,128)(2,1)} %hidden_ref.3, bf16[8,4,96,768]{3,2,1,0:T(8,128)(2,1)} %get-tuple-element.47.weight_ref, f32[8,768]{1,0:T(8,128)} %get-tuple-element.164.vec_ref, ...), custom_call_target="tpu_custom_call" | custom-call | tf_op jit(solution)/shard_map/attend_rows/pallas_call | solution.py:799
  110.7 22.6 %all-gather.4.cloned.1.call-done.pieces_ref = bf16[16,2,96,768]{3,2,1,0:T(8,128)(2,1)} async-done(((bf16[4,2,96,768]{3,2,1,0:T(8,128)(2,1)}), bf16[16,2,96,768]{3,2,1,0:T(8,128)(2,1)}) %all-gather.4.cloned.1.call-update) | async-done | bytes 4718608 | tf_op jit(solution)/shard_map/all_gather | solution.py:1270
  133.3 78.1 %expert_rows.2 = (bf16[4,512,768]{2,1,0:T(8,128)(2,1)}, bf16[4,512,768]{2,1,0:T(8,128)(2,1)}, bf16[2,16,2,96,768]{4,3,2,1,0:T(8,128)(2,1)}, bf16[4,2048,768]{2,1,0:T(8,128)(2,1)}, bf16[4,2048,768]{2,1,0:T(8,128)(2,1)}) custom-call(bf16[512,768]{1,0:T(8,128)(2,1)} %get-tuple-element.51.second_ref, bf16[16,2,96,768]{3,2,1,0:T(8,128)(2,1)} %all-gather.4.cloned.1.call-done.pieces_ref), custom_call_target="tpu_custom_call" | custom-call | tf_op jit(solution)/shard_map/expert_rows/pallas_call | solution.py:1052
  211.4 4.7 fusion.55
  216.1 4.6 all-gather.6.cloned.1.call-done
  220.7 15.4 %attend_rows.3 = (f32[512,768]{1,0:T(8,128)}, bf16[512,768]{1,0:T(8,128)(2,1)}, bf16[4,512,768]{2,1,0:T(8,128)(2,1)}, f32[512,128]{1,0:T(8,128)}, f32[4,512,128]{2,1,0:T(8,128)}) custom-call(f32[512,768]{1,0:T(8,128)} %get-tuple-element.140.hidden_ref, bf16[8,4,96,768]{3,2,1,0:T(8,128)(2,1)} %bitcast.159, f32[8,768]{1,0:T(8,128)} %get-tuple-element.163.vec_ref, ...), custom_call_target="tpu_custom_call" | custom-call | tf_op jit(solution)/shard_map/attend_rows/pallas_call | solution.py:799
  237.3 74.1 %all-gather.8.cloned.1.call-done.pieces_ref = bf16[16,2,96,768]{3,2,1,0:T(8,128)(2,1)} async-done(((bf16[4,2,96,768]{3,2,1,0:T(8,128)(2,1)}), bf16[16,2,96,768]{3,2,1,0:T(8,128)(2,1)}) %all-gather.8.cloned.1.call-update) | async-done | bytes 4718608 | tf_op jit(solution)/shard_map/all_gather | solution.py:1270
  311.4 71.4 %expert_rows.3 = (bf16[4,512,768]{2,1,0:T(8,128)(2,1)}, bf16[4,512,768]{2,1,0:T(8,128)(2,1)}, bf16[2,16,2,96,768]{4,3,2,1,0:T(8,128)(2,1)}, bf16[4,2048,768]{2,1,0:T(8,128)(2,1)}, bf16[4,2048,768]{2,1,0:T(8,128)(2,1)}) custom-call(bf16[512,768]{1,0:T(8,128)(2,1)} %get-tuple-element.56.second_ref, bf16[16,2,96,768]{3,2,1,0:T(8,128)(2,1)} %all-gather.8.cloned.1.call-done.pieces_ref), custom_call_target="tpu_custom_call" | custom-call | tf_op jit(solution)/shard_map/expert_rows/pallas_call | solution.py:1052
  382.8 6.7 fusion.14
  392.3 75.7 %expert_pull.2 = (bf16[4,512,768]{2,1,0:T(8,128)(2,1)}, bf16[4,4,2,96,768]{4,3,2,1,0:T(8,128)(2,1)}) custom-call(bf16[4,512,768]{2,1,0:T(8,128)(2,1)} %pad_maximum_fusion.sent_ref, bf16[4,512,768]{2,1,0:T(8,128)(2,1)} %get-tuple-element.58.rows_ref, bf16[4,2048,768]{2,1,0:T(8,128)(2,1)} %get-tuple-element.59.act_ref, ...), custom_call_target="tpu_custom_call" | custom-call | tf_op jit(solution)/shard_map/expert_pull/pallas_call | solution.py:1210
  468.0 30.8 %attend_pull.2 = (f32[512,768]{1,0:T(8,128)}, bf16[8,4,96,768]{3,2,1,0:T(8,128)(2,1)}, f32[8,768]{1,0:T(8,128)}, f32[768,128]{1,0:T(8,128)}) custom-call(f32[512,768]{1,0:T(8,128)} %get-tuple-element.152.grad_ref, bf16[4,512,768]{2,1,0:T(8,128)(2,1)} %get-tuple-element.62.moved_ref, f32[512,768]{1,0:T(8,128)} %get-tuple-element.140.hidden_ref, ...), custom_call_target="tpu_custom_call" | custom-call | tf_op jit(solution)/shard_map/attend_pull/pallas_call | solution.py:902
  500.7 2.1 fusion.22
  503.3 2.2 pad_maximum_fusion.1.sent_ref
  505.4 82.1 %expert_pull.3 = (bf16[4,512,768]{2,1,0:T(8,128)(2,1)}, bf16[4,4,2,96,768]{4,3,2,1,0:T(8,128)(2,1)}) custom-call(bf16[4,512,768]{2,1,0:T(8,128)(2,1)} %pad_maximum_fusion.1.sent_ref, bf16[4,512,768]{2,1,0:T(8,128)(2,1)} %get-tuple-element.66.rows_ref, bf16[4,2048,768]{2,1,0:T(8,128)(2,1)} %get-tuple-element.67.act_ref, ...), custom_call_target="tpu_custom_call" | custom-call | tf_op jit(solution)/shard_map/expert_pull/pallas_call | solution.py:1210
  591.4 31.1 %attend_pull.3 = (f32[512,768]{1,0:T(8,128)}, bf16[8,4,96,768]{3,2,1,0:T(8,128)(2,1)}, f32[8,768]{1,0:T(8,128)}, f32[768,128]{1,0:T(8,128)}) custom-call(f32[512,768]{1,0:T(8,128)} %get-tuple-element.65.grad_ref, bf16[4,512,768]{2,1,0:T(8,128)(2,1)} %get-tuple-element.70.moved_ref, bf16[512,768]{1,0:T(8,128)(2,1)} %hidden_ref.3, ...), custom_call_target="tpu_custom_call" | custom-call | tf_op jit(solution)/shard_map/attend_pull/pallas_call | solution.py:902
  630.8 67.9 %gather_sums.1 = (f32[96,768]{1,0:T(8,128)}, f32[8,128]{1,0:T(8,128)}) custom-call(bf16[4,2,4,96,768]{4,3,2,1,0:T(8,128)(2,1)} %bitcast.162, f32[4,2,4,8,128]{4,3,2,1,0:T(8,128)} %bitcast.171), custom_call_target="tpu_custom_call" | custom-call | tf_op jit(solution)/shard_map/gather_sums/pallas_call | solution.py:706
  707.0 5.7 reduce-scatter.8.cloned.1.call-done
  712.7 89.8 %reduce-scatter.6.cloned.1.call-done = bf16[1,4,2,96,768]{4,3,2,1,0:T(8,128)(2,1)} async-done(((bf16[4,4,2,96,768]{4,3,2,1,0:T(8,128)(2,1)}), bf16[1,4,2,96,768]{4,3,2,1,0:T(8,128)(2,1)}) %reduce-scatter.6.cloned.1.call-update) | async-done | bytes 1179664 | tf_op jit(solution)/shard_map/reduce_scatter | solution.py:1321
  802.5 3.2 pad_maximum_fusion.2.in_ref
  805.7 29.0 %swap_plane_6.1 = bf16[4,2,2,96,768]{4,3,2,1,0:T(8,128)(2,1)} custom-call(bf16[4,2,2,96,768]{4,3,2,1,0:T(8,128)(2,1)} %pad_maximum_fusion.2.in_ref), custom_call_target="tpu_custom_call" | custom-call | tf_op jit(solution)/shard_map/swap_plane_6/pallas_call | solution.py:513
  834.7 2.2 convert_bitcast_fusion
  (126 shorter events, 41.5 us)
Async XLA Ops:
  7.2 103.2 %copy-start = (s32[2,2048,2]{1,2,0:T(2,128)S(1)}, s32[2,2048,2]{1,2,0:T(2,128)}, u32[]{:S(2)}) copy-start(s32[2,2048,2]{1,2,0:T(2,128)} %param.13) | copy-start | bytes 98308
  7.2 1.6 copy-start.5
  7.2 126.1 %all-gather.4.cloned.1.call-start = ((), (), s32[]{:S(2)}) async-start(), calls=%async_computation.3 | async-start | bytes 5898240 | tf_op jit(solution)/shard_map/all_gather | solution.py:1270
  8.8 0.7 copy-start.12
  8.8 0.7 copy-start.13
  8.8 0.7 copy-start.14
  11.8 18.0 %copy-start.9 = (bf16[2,192,96]{2,1,0:T(8,128)(2,1)S(1)}, bf16[2,192,96]{2,1,0:T(8,128)(2,1)}, u32[]{:S(2)}) copy-start(bf16[2,192,96]{2,1,0:T(8,128)(2,1)} %param.18) | copy-start | bytes 221188
  11.8 18.2 %copy-start.8 = (bf16[2,3,96,192]{3,2,1,0:T(8,128)(2,1)S(1)}, bf16[2,3,96,192]{3,2,1,0:T(8,128)(2,1)}, u32[]{:S(2)}) copy-start(bf16[2,3,96,192]{3,2,1,0:T(8,128)(2,1)} %param.17) | copy-start | bytes 663556
  29.8 190.9 %all-gather.6.cloned.1.call-start = ((), (), s32[]{:S(2)}) async-start(), calls=%async_computation.4 | async-start | bytes 4866048 | tf_op jit(solution)/shard_map/all_gather | solution.py:1275
  31.2 280.2 %all-gather.8.cloned.1.call-start = ((), (), s32[]{:S(2)}) async-start(), calls=%async_computation.5 | async-start | bytes 5898240 | tf_op jit(solution)/shard_map/all_gather | solution.py:1270
  47.9 654.9 %reduce-scatter.4.cloned.1.call-start = ((), (), s32[]{:S(2)}) async-start(), calls=%async_computation.6 | async-start | bytes 4866048 | tf_op jit(solution)/shard_map/reduce_scatter | solution.py:1327
  92.4 16.6 %copy-start.15 = (s32[8]{0:T(128)S(1)}, s32[8]{0:T(128)}, u32[]{:S(2)}) copy-start(s32[8]{0:T(128)} %param.12) | copy-start | bytes 100
  498.7 213.9 %reduce-scatter.8.cloned.1.call-start = ((), (), s32[]{:S(2)}) async-start(), calls=%async_computation.8 | async-start | bytes 5898240 | tf_op jit(solution)/shard_map/reduce_scatter | solution.py:1321
  498.8 1.9 copy-start.2
  499.3 303.1 %reduce-scatter.6.cloned.1.call-start = ((), (), s32[]{:S(2)}) async-start(), calls=%async_computation.7 | async-start | bytes 5898240 | tf_op jit(solution)/shard_map/reduce_scatter | solution.py:1321
  587.5 1.3 copy-start.3
  591.4 31.1 %copy-start.7 = (f32[768,128]{1,0:T(8,128)S(1)}, f32[768,128]{1,0:T(8,128)}, u32[]{:S(2)}) copy-start(f32[768,128]{1,0:T(8,128)} %get-tuple-element.78) | copy-start | bytes 1179652
  622.5 1.6 copy-start.11
  622.5 1.6 copy-start.10
  622.5 1.9 copy-start.4
  703.7 2.4 copy-start.6
  838.9 1.6 copy-start.1
Sparse Core Ops, SparseCore 0:
  29.9 103.3 all-gather.3
  136.6 83.9 all-gather.5
  222.3 89.0 all-gather.7
  498.9 117.6 reduce-scatter.3
  618.7 93.9 reduce-scatter.7
  714.8 87.5 reduce-scatter.5

commit v3 on v2

--- a/solution.py
+++ b/solution.py
@@ -479,7 +479,7 @@
     pl.semaphore_wait(barrier, len(devices))
 
 
-def swap_kernel(kind, same, in_ref, out_ref, held, local_sem, send_sem, recv_sem):
+def swap_kernel(kind, same, in_ref, after_ref, out_ref, held, local_sem, send_sem, recv_sem):
     place, count, device = group_of(kind)
     others = [lax.rem(place + step, count) for step in range(1, count)]
     first = pltpu.make_async_copy(in_ref if same else in_ref.at[place], held, local_sem.at[0])
@@ -506,14 +506,14 @@
         copy.wait()
 
 
-def swap(array, kind, same, collective_id):
+def swap(array, kind, same, collective_id, after):
     count = {"plane": 4, "column": 4, "chip": 2, "all": 32}[kind]
     block = array.shape if same else array.shape[1:]
     any_spec = pl.BlockSpec(memory_space=pl.ANY)
     return pl.pallas_call(
         partial(swap_kernel, kind, same),
         out_shape=jax.ShapeDtypeStruct((count,) + block, array.dtype),
-        in_specs=[any_spec],
+        in_specs=[any_spec, any_spec],
         out_specs=any_spec,
         scratch_shapes=[
             pltpu.VMEM(block, array.dtype),
@@ -525,7 +525,7 @@
             collective_id=collective_id, has_side_effects=True, vmem_limit_bytes=VMEM_LIMIT
         ),
         name=f"swap_{kind}_{collective_id}",
-    )(array)
+    )(array, after)
 
 
 def relatives():
@@ -630,38 +630,48 @@
     )(block, small)
 
 
-def gather_sums_kernel(
-    large_ref, small_ref, large_out, small_out,
-    own_a, own_b, chip_a, chip_b, sum_a, sum_b, near_a, near_b, col_a, col_b, part_a, part_b,
-    local_sem, chip_send, chip_recv, near_send, near_recv, col_send, col_recv,
-):
+def gather_sums_kernel(count, *refs):
+    ins, moved_ref, refs = refs[:count], refs[count], refs[count + 1 :]
+    outs, swapped, refs = refs[:count], refs[count], refs[count + 1 :]
+    sets = [(ins[which],) + refs[6 * which : 6 * which + 6] for which in range(count)]
+    held, *sems = refs[6 * count :]
+    local_sem, chip_send, chip_recv, near_send, near_recv, col_send, col_recv, held_sem, swap_send, swap_recv = sems
     place, core, part, near, partner = relatives()
     dp = place * 2 + core
     columns = [lax.rem(part + step, 4) for step in range(1, 4)]
     spots = [place] + [near[step][0] // 2 for step in range(1, 4)]
     order = (3, 1, 2, 0)
-    sets = (
-        (large_ref, own_a, chip_a, sum_a, near_a, col_a, part_a),
-        (small_ref, own_b, chip_b, sum_b, near_b, col_b, part_b),
-    )
     loads = {}
-    for step in order:
-        for which, (src, own, *_) in enumerate(sets):
+    for which, (src, own, *_) in enumerate(sets):
+        for step in order:
             loads[which, step] = pltpu.make_async_copy(
                 src.at[spots[step], core], own.at[step], local_sem.at[which, step]
             )
             loads[which, step].start()
+    bring = pltpu.make_async_copy(moved_ref.at[place], held, held_sem.at[0])
+    bring.start()
     greet([(dp, other) for other in columns] + near[1:] + [partner])
     chips, nears, cols = {}, {}, {}
-    for step in order:
-        for which, (src, own, chip, *_) in enumerate(sets):
+    for which, (src, own, chip, *_) in enumerate(sets):
+        for step in order:
             chips[which, step] = push(
                 src.at[spots[step], 1 - core], chip.at[step],
                 chip_send.at[which, step], chip_recv.at[which, step], partner,
             )
             chips[which, step].start()
-    for step in order:
-        for which, (src, own, chip, total, arrived, *_) in enumerate(sets):
+    swaps = [
+        push(
+            moved_ref.at[spots[step]], swapped.at[place], swap_send.at[step - 1], swap_recv.at[step - 1], near[step]
+        )
+        for step in (1, 2, 3)
+    ]
+    for copy in swaps:
+        copy.start()
+    bring.wait()
+    keep = pltpu.make_async_copy(held, swapped.at[place], held_sem.at[1])
+    keep.start()
+    for which, (src, own, chip, total, arrived, *_) in enumerate(sets):
+        for step in order:
             loads[which, step].wait()
             chips[which, step].wait()
             total[step] = (own[step].astype(f32) + chip[step].astype(f32)).astype(total.dtype)
@@ -686,7 +696,7 @@
                 col_send.at[which, step], col_recv.at[which, step], (dp, other),
             )
             cols[which, step].start()
-    for which, out in enumerate((large_out, small_out)):
+    for which, out in enumerate(outs):
         _, _, _, _, _, column, partial_sum = sets[which]
         for step in range(3):
             cols[which, step].wait()
@@ -696,28 +706,31 @@
             + column[1].astype(f32)
             + column[2].astype(f32)
         )
-
-
-def gather_sums(large, small):
-    blocks = (large.shape[2:], small.shape[2:])
-    kinds = (large.dtype, small.dtype)
-    two = lambda lead: [pltpu.VMEM(lead(block), kind) for block, kind in zip(blocks, kinds)]
+    keep.wait()
+    for copy in swaps:
+        copy.wait()
+
+
+def gather_sums(arrays, moved):
+    count = len(arrays)
+    scratch = []
+    for array in arrays:
+        block = array.shape[2:]
+        for shape in ((4,) + block, (4,) + block, (4,) + block, (3,) + block, (3,) + block[1:], block):
+            scratch.append(pltpu.VMEM(shape, array.dtype))
     vmem_spec = pl.BlockSpec(memory_space=pltpu.VMEM)
     return pl.pallas_call(
-        gather_sums_kernel,
-        out_shape=tuple(jax.ShapeDtypeStruct(block[1:], f32) for block in blocks),
-        in_specs=[ANY_SPEC, ANY_SPEC],
-        out_specs=(vmem_spec, vmem_spec),
-        scratch_shapes=two(lambda block: (4,) + block)
-        + two(lambda block: (4,) + block)
-        + two(lambda block: (4,) + block)
-        + two(lambda block: (3,) + block)
-        + two(lambda block: (3,) + block[1:])
-        + two(lambda block: block)
-        + [DMA((2, 4)), DMA((2, 4)), DMA((2, 4)), DMA((2, 3)), DMA((2, 3)), DMA((2, 3)), DMA((2, 3))],
+        partial(gather_sums_kernel, count),
+        out_shape=tuple(jax.ShapeDtypeStruct(array.shape[3:], f32) for array in arrays)
+        + (jax.ShapeDtypeStruct(moved.shape, moved.dtype),),
+        in_specs=[ANY_SPEC] * (count + 1),
+        out_specs=(vmem_spec,) * count + (ANY_SPEC,),
+        scratch_shapes=scratch
+        + [pltpu.VMEM(moved.shape[1:], moved.dtype)]
+        + [DMA((count, 4))] * 3 + [DMA((count, 3))] * 4 + [DMA((2,)), DMA((3,)), DMA((3,))],
         compiler_params=comm_params(2),
         name="gather_sums",
-    )(large, small)
+    )(*arrays, moved)
 
 
 def standard(rows):
@@ -737,7 +750,11 @@
     return jnp.where(slots < LEN, scores, far_negative)
 
 
-WEIGHT_SPEC = pl.BlockSpec((8, 1, D // 8, D), lambda turn: (0, turn, 0, 0))
+WGRAD_SPEC = pl.BlockSpec((8, 1, D // 8, D), lambda turn: (0, turn, 0, 0))
+
+
+def weight_spec(layer):
+    return pl.BlockSpec((8, 1, 1, D // 8, D), lambda turn: (0, turn, layer, 0, 0))
 
 
 def attend_kernel(
@@ -746,7 +763,7 @@
 ):
     turn = pl.program_id(0)
     images = hidden_ref.shape[0] // SEQ
-    weight = weight_ref[:, 0].reshape(D, D)
+    weight = weight_ref[:, 0, 0].reshape(D, D)
 
     @pl.when(turn == 0)
     def _():
@@ -792,14 +809,14 @@
         table_ref[...] = lane_put(probs, EXPERTS, jnp.sum(attn * attn, axis=-1, keepdims=True))
 
 
-def attend_rows(hidden, weights, vecs, router):
+def attend_rows(hidden, weights, vecs, router, layer):
     rows = hidden.shape[0]
     whole = lambda shape: pl.BlockSpec(shape, lambda turn: (0,) * len(shape))
     by_part = lambda shape: pl.BlockSpec((1,) + shape, lambda turn: (turn, 0, 0))
     return pl.pallas_call(
         attend_kernel,
         grid=(4,),
-        in_specs=[whole((rows, D)), WEIGHT_SPEC, whole((8, D)), whole((D, 128))],
+        in_specs=[whole((rows, D)), weight_spec(layer), whole((8, D)), whole((D, 128))],
         out_specs=(
             whole((rows, D)), whole((rows, D)), by_part((rows, D)), whole((rows, 128)), by_part((rows, 128)),
         ),
@@ -832,7 +849,7 @@
     turn = pl.program_id(0)
     rows_all = grad_ref.shape[0]
     images = rows_all // SEQ
-    weight = weight_ref[:, 0].reshape(D, D)
+    weight = weight_ref[:, 0, 0].reshape(D, D)
     scale = HD ** (-0.5)
 
     @pl.when(turn == 0)
@@ -895,7 +912,7 @@
         out_ref[...] = grad_sc[...] + norm_pull(dfirst, normed, inv_std, vec_ref[0:1])
 
 
-def attend_pull(grad, moved, hidden, resid, saved, table, logs, dprob, weights, vecs, router):
+def attend_pull(grad, moved, hidden, resid, saved, table, logs, dprob, weights, vecs, router, layer):
     rows = grad.shape[0]
     whole = lambda shape: pl.BlockSpec(shape, lambda turn: (0,) * len(shape))
     by_part = lambda shape: pl.BlockSpec((1,) + shape, lambda turn: (turn, 0, 0))
@@ -905,9 +922,9 @@
         in_specs=[
             whole((rows, D)), whole((EXPERTS, rows, D)), whole((rows, D)), whole((rows, D)),
             by_part((rows, D)), whole((rows, 128)), by_part((rows, 128)), whole((rows, 128)),
-            WEIGHT_SPEC, whole((8, D)), whole((D, 128)),
+            weight_spec(layer), whole((8, D)), whole((D, 128)),
         ],
-        out_specs=(whole((rows, D)), WEIGHT_SPEC, whole((8, D)), whole((D, 128))),
+        out_specs=(whole((rows, D)), WGRAD_SPEC, whole((8, D)), whole((D, 128))),
         out_shape=(
             jax.ShapeDtypeStruct((rows, D), f32),
             jax.ShapeDtypeStruct((8, 4, D // 8, D), bf16),
@@ -943,7 +960,7 @@
 
 
 def expert_kernel(
-    second_ref, pieces_ref, rows_out, back_out, weights_out, act_out, slope_out,
+    second_ref, pieces_ref, after_ref, rows_out, back_out, weights_out, act_out, slope_out,
     held, weights, made, acts, slopes, total,
     load_sem, join_send, join_recv, row_send, row_recv, pass_send, pass_recv, back_send, back_recv, out_sem, save_sem,
 ):
@@ -1045,13 +1062,13 @@
         copy.wait()
 
 
-def expert_rows(second, pieces):
+def expert_rows(second, pieces, after):
     count = second.shape[0]
     block = (count, D)
     weight_shape = (2, 16, 2, D // 8, D)
     return pl.pallas_call(
         expert_kernel,
-        in_specs=[ANY_SPEC, ANY_SPEC],
+        in_specs=[ANY_SPEC] * 3,
         out_specs=(ANY_SPEC,) * 5,
         out_shape=(
             jax.ShapeDtypeStruct((4,) + block, bf16),
@@ -1072,7 +1089,7 @@
         ],
         compiler_params=comm_params(4),
         name="expert_rows",
-    )(second, pieces)
+    )(second, pieces, after)
 
 
 def expert_pull_kernel(
@@ -1265,16 +1282,11 @@
 
     def expert_pieces(layer, after):
         packed = jnp.stack([w_in[layer], w_back[layer]], axis=1)
-        packed, _ = lax.optimization_barrier((packed, after))
-        arrived = swap(packed, "plane", False, 3)
-        return lax.all_gather(arrived, "tensor", axis=0, tiled=True)
+        arrived = swap(packed, "plane", False, 3 + 4 * layer, after)
+        return arrived, lax.all_gather(arrived, "tensor", axis=0, tiled=True)
 
     pieces = [expert_pieces(0, small), None]
-    attn_first, small_all = spread(attn_blocks[0], small)
-    attn_later = [
-        lax.all_gather(attn_blocks[layer], ("dp", "tensor"), axis=0, tiled=False) for layer in range(1, LAYERS)
-    ]
-    attn_all = [attn_first] + [each.reshape(8, 4, slices, D) for each in attn_later]
+    attn_all, small_all = spread(attn_blocks, small)
     flat = small_all.reshape(32, 2048)
     vec_count = LAYERS * 2 * D // 32
     gains = flat[:, :vec_count].reshape(LAYERS, 2, D).astype(f32)
@@ -1289,10 +1301,11 @@
     kept = []
     stats = []
     for layer in range(LAYERS):
-        resid, second, saved, table, logs = attend_rows(hidden, attn_all[layer], vecs[layer], routers[layer])
+        resid, second, saved, table, logs = attend_rows(hidden, attn_all, vecs[layer], routers[layer], layer)
         if layer + 1 < LAYERS:
-            pieces[layer + 1] = expert_pieces(layer + 1, second[:8, :128])
-        rows, back, weights, act, slope = expert_rows(second, pieces[layer])
+            pieces[layer + 1] = expert_pieces(layer + 1, second)
+        after = pieces[min(layer + 1, LAYERS - 1)][0]
+        rows, back, weights, act, slope = expert_rows(second, pieces[layer][1], after)
         gates = jnp.where(chosen[layer], by_place(table[:, :EXPERTS]), 0.0)
         moe = sum(gates[:, at : at + 1] * back[at].astype(f32) for at in range(EXPERTS))
         result = resid + moe
@@ -1321,13 +1334,9 @@
         summed = lax.psum_scatter(wgrad, "tensor", scatter_dimension=0, tiled=False)
         owned.append(summed)
         grad, attn_wgrad, small_grad, router_grad = attend_pull(
-            grad, moved, before, resid, saved, table, logs, dprob, attn_all[layer], vecs[layer], routers[layer]
-        )
-        if layer:
-            attn_wgrad = lax.psum_scatter(
-                attn_wgrad.reshape(32, slices, D), ("dp", "tensor"), scatter_dimension=0, tiled=False
-            ).astype(f32)
-        attn_grads.append(attn_wgrad)
+            grad, moved, before, resid, saved, table, logs, dprob, attn_all, vecs[layer], routers[layer], layer
+        )
+        attn_grads.append(attn_wgrad.reshape(4, 2, 4, slices, D))
         small_grads.append(small_grad[:4])
         router_grads.append(router_grad[:, :EXPERTS])
     for listed in (small_grads, router_grads, owned):
@@ -1344,8 +1353,8 @@
         axis=1,
     )
     packed = jnp.pad(packed, ((0, 0), (0, 1024 - packed.shape[1]))).reshape(4, 2, 4, 8, 128)
-    last, total = gather_sums(attn_grads.pop().reshape(4, 2, 4, slices, D), packed)
-    attn_grad = jnp.stack([last] + attn_grads)
+    *attn_grads, total, moved_later = gather_sums(attn_grads + [packed], owned[1])
+    attn_grad = jnp.stack(attn_grads[::-1])
     total = total.reshape(-1)
     share = LAYERS * 2 * D // 32
     router_share = LAYERS * D * EXPERTS // 32
@@ -1354,7 +1363,8 @@
     rms = jnp.sqrt(total[at : at + 3 * LAYERS].reshape(LAYERS, 3) / denom)
     qkv_grad = jnp.transpose(attn_grad[:, :, :QKV].reshape(LAYERS, slices, 3, QKV // 3), (0, 2, 1, 3))
     out_grad = jnp.transpose(attn_grad[:, :, QKV:], (0, 2, 1))
-    expert_grad = swap(jnp.stack(owned, axis=1), "plane", False, 6).astype(f32)
+    moved_first = swap(owned[0], "plane", False, 6, moved_later)
+    expert_grad = jnp.stack([moved_first, moved_later], axis=1).astype(f32)
     expert_grad = jnp.transpose(expert_grad, (2, 1, 0, 3, 4))
     return (
         hidden,

time: 851 us -> 680 us (0.80)
  waiting for transfers between devices: 197 us -> 7.54 us
  Pallas kernels: 573 us -> 593 us
    reduce_scatter x2, waiting for transfers between devices: 95.5 us -> 0.01 us  [per_device(): summed = lax.psum_scatter(wgrad, 'tensor', scatter_dimension=0, tiled=False)]
    all_gather x3 -> x2, waiting for transfers between devices: 101 us -> 7.47 us  [expert_pieces(): return (arrived, lax.all_gather(arrived, 'tensor', axis=0, tiled=True))]
    pallas_call x1, Pallas kernels: 41.1 us -> 68.3 us  [spread(): pl.pallas_call(spread_kernel, out_shape=(jax.ShapeDtypeStruct((8, 4) + bl...]
    pallas_call x3, Pallas kernels: 63.6 us -> 49.5 us  [swap(): pl.pallas_call(partial(swap_kernel, kind, same), out_shape=jax.ShapeDtype...]
    pallas_call x5, Pallas kernels: 248 us -> 262 us  [the longest x2 142 us: expert_rows(): pl.pallas_call(expert_kernel, in_specs=[ANY_SPEC] * 3, out_specs=(ANY_SPE...]
  transfers between devices with their start and end apart: 6 -> 4, of which waited for: 5 -> 2; matrix products, arithmetic and copies ran while one was open for 4% -> 6% of each run, Pallas kernels for 41% -> 61%
where the time goes in v3:
time: 680 us; the launch traced here: 674 us
  Pallas kernels  593 us (87%)
  other arithmetic  36.5 us (5%)
  local copies, waits for them, and re-layouts  21.7 us (3%)
  between operations  15.1 us (2%)
  waiting for transfers between devices  7.54 us (1%)
    pallas_call x2, Pallas kernels, expert_pull(): pl.pallas_call(expert_pull_kernel, in_specs=[ANY_SPEC] * 5, out_specs=(AN...  152 us
    pallas_call x2, Pallas kernels, expert_rows(): pl.pallas_call(expert_kernel, in_specs=[ANY_SPEC] * 3, out_specs=(ANY_SPE...  142 us
    pallas_call x1, Pallas kernels, gather_sums(): pl.pallas_call(partial(gather_sums_kernel, count), out_shape=tuple((jax.S...  88.6 us
    pallas_call x1, Pallas kernels, spread(): pl.pallas_call(spread_kernel, out_shape=(jax.ShapeDtypeStruct((8, 4) + bl...  68.3 us
    pallas_call x2, Pallas kernels, attend_pull(): pl.pallas_call(attend_pull_kernel, grid=(4,), in_specs=[whole((rows, D)),...  61.2 us
    pallas_call x3, Pallas kernels, swap(): pl.pallas_call(partial(swap_kernel, kind, same), out_shape=jax.ShapeDtype...  49.5 us
    pallas_call x2, Pallas kernels, attend_rows(): pl.pallas_call(attend_kernel, grid=(4,), in_specs=[whole((rows, D)), weig...  30.7 us
  transfers between devices with their start and end apart: 4, of which 2 were waited for; matrix products, arithmetic and copies ran while one was open for 6% of the time, Pallas kernels for 61%

profile of v3, /device:TPU:0, one launch (start us, length us, event | category | flops | bytes accessed | tf_op | source)
XLA Modules:
  0.0 673.6 jit_solution(10576204209138421873)
XLA Ops:
  7.2 2.6 slice_bitcast_fusion.2
  11.6 18.0 %swap_plane_3.1 = bf16[4,2,96,768]{3,2,1,0:T(8,128)(2,1)} custom-call(bf16[4,2,96,768]{3,2,1,0:T(8,128)(2,1)} %pad_maximum_fusion.2.in_ref, bf16[16,128]{1,0:T(8,128)(2,1)} %fusion.45.small_ref.after_ref), custom_call_target="tpu_custom_call" | custom-call | tf_op jit(solution)/shard_map/swap_plane_3/pallas_call | solution.py:513
  31.9 68.3 %spread.1 = (bf16[8,4,2,96,768]{4,3,2,1,0:T(8,128)(2,1)}, bf16[8,4,16,128]{3,2,1,0:T(8,128)(2,1)}) custom-call(bf16[2,96,768]{2,1,0:T(8,128)(2,1)} %pad_maximum_fusion.5.block_ref, bf16[16,128]{1,0:T(8,128)(2,1)} %fusion.45.small_ref.after_ref), custom_call_target="tpu_custom_call" | custom-call | tf_op jit(solution)/shard_map/spread/pallas_call | solution.py:617
  103.4 15.2 %attend_rows.2 = (f32[512,768]{1,0:T(8,128)}, bf16[512,768]{1,0:T(8,128)(2,1)}, bf16[4,512,768]{2,1,0:T(8,128)(2,1)}, f32[512,128]{1,0:T(8,128)}, f32[4,512,128]{2,1,0:T(8,128)}) custom-call(bf16[512,768]{1,0:T(8,128)(2,1)} %hidden_ref.3, bf16[8,4,2,96,768]{4,3,2,1,0:T(8,128)(2,1)} %get-tuple-element.48.weight_ref, f32[8,768]{1,0:T(8,128)} %get-tuple-element.164.vec_ref, ...), custom_call_target="tpu_custom_call" | custom-call | tf_op jit(solution)/shard_map/attend_rows/pallas_call | solution.py:816
  118.7 2.2 pad_maximum_fusion.3.in_ref
  120.9 16.5 %swap_plane_7.1.after_ref = bf16[4,2,96,768]{3,2,1,0:T(8,128)(2,1)} custom-call(bf16[4,2,96,768]{3,2,1,0:T(8,128)(2,1)} %pad_maximum_fusion.3.in_ref, bf16[512,768]{1,0:T(8,128)(2,1)} %get-tuple-element.52.after_ref.second_ref), custom_call_target="tpu_custom_call" | custom-call | tf_op jit(solution)/shard_map/swap_plane_7/pallas_call | solution.py:513
  139.6 71.0 %expert_rows.2 = (bf16[4,512,768]{2,1,0:T(8,128)(2,1)}, bf16[4,512,768]{2,1,0:T(8,128)(2,1)}, bf16[2,16,2,96,768]{4,3,2,1,0:T(8,128)(2,1)}, bf16[4,2048,768]{2,1,0:T(8,128)(2,1)}, bf16[4,2048,768]{2,1,0:T(8,128)(2,1)}) custom-call(bf16[512,768]{1,0:T(8,128)(2,1)} %get-tuple-element.52.after_ref.second_ref, ...), custom_call_target="tpu_custom_call" | custom-call | tf_op jit(solution)/shard_map/expert_rows/pallas_call | solution.py:1069
  210.5 4.7 fusion.53
  215.2 15.5 %attend_rows.3 = (f32[512,768]{1,0:T(8,128)}, bf16[512,768]{1,0:T(8,128)(2,1)}, bf16[4,512,768]{2,1,0:T(8,128)(2,1)}, f32[512,128]{1,0:T(8,128)}, f32[4,512,128]{2,1,0:T(8,128)}) custom-call(f32[512,768]{1,0:T(8,128)} %get-tuple-element.142.hidden_ref, bf16[8,4,2,96,768]{4,3,2,1,0:T(8,128)(2,1)} %get-tuple-element.48.weight_ref, ...), custom_call_target="tpu_custom_call" | custom-call | tf_op jit(solution)/shard_map/attend_rows/pallas_call | solution.py:816
  231.9 7.3 %all-gather.5.cloned.1.call-done.pieces_ref = bf16[16,2,96,768]{3,2,1,0:T(8,128)(2,1)} async-done(((bf16[4,2,96,768]{3,2,1,0:T(8,128)(2,1)}), bf16[16,2,96,768]{3,2,1,0:T(8,128)(2,1)}) %all-gather.5.cloned.1.call-update) | async-done | bytes 4718608 | tf_op jit(solution)/shard_map/all_gather | solution.py:1286
  239.2 71.4 %expert_rows.3 = (bf16[4,512,768]{2,1,0:T(8,128)(2,1)}, bf16[4,512,768]{2,1,0:T(8,128)(2,1)}, bf16[2,16,2,96,768]{4,3,2,1,0:T(8,128)(2,1)}, bf16[4,2048,768]{2,1,0:T(8,128)(2,1)}, bf16[4,2048,768]{2,1,0:T(8,128)(2,1)}) custom-call(bf16[512,768]{1,0:T(8,128)(2,1)} %get-tuple-element.56.second_ref, ...), custom_call_target="tpu_custom_call" | custom-call | tf_op jit(solution)/shard_map/expert_rows/pallas_call | solution.py:1069
  310.5 6.7 fusion.14
  319.1 76.1 %expert_pull.2 = (bf16[4,512,768]{2,1,0:T(8,128)(2,1)}, bf16[4,4,2,96,768]{4,3,2,1,0:T(8,128)(2,1)}) custom-call(bf16[4,512,768]{2,1,0:T(8,128)(2,1)} %pad_maximum_fusion.sent_ref, bf16[4,512,768]{2,1,0:T(8,128)(2,1)} %get-tuple-element.58.rows_ref, bf16[4,2048,768]{2,1,0:T(8,128)(2,1)} %get-tuple-element.59.act_ref, ...), custom_call_target="tpu_custom_call" | custom-call | tf_op jit(solution)/shard_map/expert_pull/pallas_call | solution.py:1227
  396.2 30.5 %attend_pull.2 = (f32[512,768]{1,0:T(8,128)}, bf16[8,4,96,768]{3,2,1,0:T(8,128)(2,1)}, f32[8,768]{1,0:T(8,128)}, f32[768,128]{1,0:T(8,128)}) custom-call(f32[512,768]{1,0:T(8,128)} %get-tuple-element.154.grad_ref, bf16[4,512,768]{2,1,0:T(8,128)(2,1)} %get-tuple-element.62.moved_ref, f32[512,768]{1,0:T(8,128)} %get-tuple-element.142.hidden_ref, ...), custom_call_target="tpu_custom_call" | custom-call | tf_op jit(solution)/shard_map/attend_pull/pallas_call | solution.py:919
  426.8 3.2 fusion.22
  430.4 2.0 pad_maximum_fusion.1.sent_ref
  432.4 75.8 %expert_pull.3 = (bf16[4,512,768]{2,1,0:T(8,128)(2,1)}, bf16[4,4,2,96,768]{4,3,2,1,0:T(8,128)(2,1)}) custom-call(bf16[4,512,768]{2,1,0:T(8,128)(2,1)} %pad_maximum_fusion.1.sent_ref, bf16[4,512,768]{2,1,0:T(8,128)(2,1)} %get-tuple-element.66.rows_ref, bf16[4,2048,768]{2,1,0:T(8,128)(2,1)} %get-tuple-element.67.act_ref, ...), custom_call_target="tpu_custom_call" | custom-call | tf_op jit(solution)/shard_map/expert_pull/pallas_call | solution.py:1227
  512.1 30.7 %attend_pull.3 = (f32[512,768]{1,0:T(8,128)}, bf16[8,4,96,768]{3,2,1,0:T(8,128)(2,1)}, f32[8,768]{1,0:T(8,128)}, f32[768,128]{1,0:T(8,128)}) custom-call(f32[512,768]{1,0:T(8,128)} %get-tuple-element.65.grad_ref, bf16[4,512,768]{2,1,0:T(8,128)(2,1)} %get-tuple-element.70.moved_ref, bf16[512,768]{1,0:T(8,128)(2,1)} %hidden_ref.3, ...), custom_call_target="tpu_custom_call" | custom-call | tf_op jit(solution)/shard_map/attend_pull/pallas_call | solution.py:919
  546.3 2.0 maximum_bitcast_fusion.1
  548.3 2.0 maximum_bitcast_fusion
  551.2 88.6 %gather_sums.1 = (f32[96,768]{1,0:T(8,128)}, f32[96,768]{1,0:T(8,128)}, f32[8,128]{1,0:T(8,128)}, bf16[4,2,96,768]{3,2,1,0:T(8,128)(2,1)}) custom-call(bf16[4,2,4,96,768]{4,3,2,1,0:T(8,128)(2,1)} %bitcast.161, bf16[4,2,4,96,768]{4,3,2,1,0:T(8,128)(2,1)} %bitcast.162, f32[4,2,4,8,128]{4,3,2,1,0:T(8,128)} %bitcast.173, bf16[4,2,96,768]{3,2,1,0:T(8,128)(2,1)} %bitcast.172), custom_call_target="tpu_custom_call" | custom-call | tf_op jit(solution)/shard_map/gather_sums/pallas_call | solution.py:722
  645.9 15.0 %swap_plane_6.1 = bf16[4,2,96,768]{3,2,1,0:T(8,128)(2,1)} custom-call(bf16[4,2,96,768]{3,2,1,0:T(8,128)(2,1)} %bitcast.166, bf16[4,2,96,768]{3,2,1,0:T(8,128)(2,1)} %get-tuple-element.85.after_ref), custom_call_target="tpu_custom_call" | custom-call | tf_op jit(solution)/shard_map/swap_plane_6/pallas_call | solution.py:513
  660.9 1.9 convert_bitcast_fusion
  662.9 2.6 slice_bitcast_fusion
  (112 shorter events, 28.8 us)
Async XLA Ops:
  7.2 131.9 %copy-start = (s32[2,2048,2]{1,2,0:T(2,128)S(1)}, s32[2,2048,2]{1,2,0:T(2,128)}, u32[]{:S(2)}) copy-start(s32[2,2048,2]{1,2,0:T(2,128)} %param.13) | copy-start | bytes 98308
  7.2 132.4 %all-gather.3.cloned.1.call-start = ((), (), s32[]{:S(2)}) async-start(), calls=%async_computation.2 | async-start | bytes 5898240 | tf_op jit(solution)/shard_map/all_gather | solution.py:1286
  9.8 1.1 copy-start.10
  9.8 1.1 copy-start.11
  9.8 1.1 copy-start.12
  11.6 19.0 %copy-start.7 = (bf16[2,3,96,192]{3,2,1,0:T(8,128)(2,1)S(1)}, bf16[2,3,96,192]{3,2,1,0:T(8,128)(2,1)}, u32[]{:S(2)}) copy-start(bf16[2,3,96,192]{3,2,1,0:T(8,128)(2,1)} %param.17) | copy-start | bytes 663556
  29.6 209.6 %all-gather.5.cloned.1.call-start = ((), (), s32[]{:S(2)}) async-start(), calls=%async_computation.3 | async-start | bytes 5898240 | tf_op jit(solution)/shard_map/all_gather | solution.py:1286
  120.9 16.6 %copy-start.2 = (f32[512,128]{1,0:T(8,128)S(1)}, f32[512,128]{1,0:T(8,128)}, u32[]{:S(2)}) copy-start(f32[512,128]{1,0:T(8,128)} %get-tuple-element.51.table_ref) | copy-start | bytes 786436
  120.9 16.7 %copy-start.13 = (s32[8]{0:T(128)S(1)}, s32[8]{0:T(128)}, u32[]{:S(2)}) copy-start(s32[8]{0:T(128)} %param.12) | copy-start | bytes 100
  137.4 413.8 %reduce-scatter.3.cloned.1.call-start = ((), (), s32[]{:S(2)}) async-start(), calls=%async_computation.4 | async-start | bytes 5898240 | tf_op jit(solution)/shard_map/reduce_scatter | solution.py:1334
  395.2 250.7 %reduce-scatter.5.cloned.1.call-start = ((), (), s32[]{:S(2)}) async-start(), calls=%async_computation.5 | async-start | bytes 5898240 | tf_op jit(solution)/shard_map/reduce_scatter | solution.py:1334
  512.1 30.7 %copy-start.6 = (f32[768,128]{1,0:T(8,128)S(1)}, f32[768,128]{1,0:T(8,128)}, u32[]{:S(2)}) copy-start(f32[768,128]{1,0:T(8,128)} %get-tuple-element.79) | copy-start | bytes 1179652
  542.9 1.5 copy-start.9
  542.9 1.5 copy-start.8
  542.9 1.9 copy-start.3
  641.2 2.5 copy-start.4
  641.2 2.5 copy-start.5
  662.9 4.0 copy-start.1
Sparse Core Ops, SparseCore 0:
  29.7 109.7 all-gather.2
  141.1 98.0 all-gather.4
  395.3 88.5 reduce-scatter.2
  508.3 88.5 reduce-scatter.4

commit v4 on v3

--- a/solution.py
+++ b/solution.py
@@ -479,55 +479,6 @@
     pl.semaphore_wait(barrier, len(devices))
 
 
-def swap_kernel(kind, same, in_ref, after_ref, out_ref, held, local_sem, send_sem, recv_sem):
-    place, count, device = group_of(kind)
-    others = [lax.rem(place + step, count) for step in range(1, count)]
-    first = pltpu.make_async_copy(in_ref if same else in_ref.at[place], held, local_sem.at[0])
-    first.start()
-    greet([device(other) for other in others])
-    copies = []
-    for step, other in enumerate(others):
-        copies.append(
-            pltpu.make_async_remote_copy(
-                src_ref=in_ref if same else in_ref.at[other],
-                dst_ref=out_ref.at[place],
-                send_sem=send_sem.at[step],
-                recv_sem=recv_sem.at[step],
-                device_id=device(other),
-                device_id_type=MESH,
-            )
-        )
-        copies[-1].start()
-    first.wait()
-    second = pltpu.make_async_copy(held, out_ref.at[place], local_sem.at[1])
-    second.start()
-    second.wait()
-    for copy in copies:
-        copy.wait()
-
-
-def swap(array, kind, same, collective_id, after):
-    count = {"plane": 4, "column": 4, "chip": 2, "all": 32}[kind]
-    block = array.shape if same else array.shape[1:]
-    any_spec = pl.BlockSpec(memory_space=pl.ANY)
-    return pl.pallas_call(
-        partial(swap_kernel, kind, same),
-        out_shape=jax.ShapeDtypeStruct((count,) + block, array.dtype),
-        in_specs=[any_spec, any_spec],
-        out_specs=any_spec,
-        scratch_shapes=[
-            pltpu.VMEM(block, array.dtype),
-            pltpu.SemaphoreType.DMA((2,)),
-            pltpu.SemaphoreType.DMA((count - 1,)),
-            pltpu.SemaphoreType.DMA((count - 1,)),
-        ],
-        compiler_params=pltpu.CompilerParams(
-            collective_id=collective_id, has_side_effects=True, vmem_limit_bytes=VMEM_LIMIT
-        ),
-        name=f"swap_{kind}_{collective_id}",
-    )(array, after)
-
-
 def relatives():
     dp, part = lax.axis_index("dp"), lax.axis_index("tensor")
     place, core = dp // 2, dp % 2
@@ -552,185 +503,258 @@
 DMA = pltpu.SemaphoreType.DMA
 
 
-def spread_kernel(
-    block_ref, small_ref, out_ref, small_out, local_sem, za_send, za_recv, yx_send, yx_recv, cc_send, cc_recv
+def column_copies(src, column, send_sem, recv_sem):
+    dp, part = lax.axis_index("dp"), lax.axis_index("tensor")
+    others = [lax.rem(part + step, 4) for step in range(1, 4)]
+    return [
+        push(src.at[other], column.at[step], send_sem.at[step], recv_sem.at[step], (dp, other))
+        for step, other in enumerate(others)
+    ]
+
+
+def column_greets():
+    dp, part = lax.axis_index("dp"), lax.axis_index("tensor")
+    return [(dp, lax.rem(part + step, 4)) for step in range(1, 4)]
+
+
+def column_sum(src, column):
+    return (
+        src[lax.axis_index("tensor")].astype(f32)
+        + column[0].astype(f32)
+        + column[1].astype(f32)
+        + column[2].astype(f32)
+    )
+
+
+def plane_moves(src, dst, send_sem, recv_sem):
+    place, _, _, near, _ = relatives()
+    return [
+        push(src.at[near[step][0] // 2], dst.at[place], send_sem.at[step - 1], recv_sem.at[step - 1], near[step])
+        for step in (1, 2, 3)
+    ]
+
+
+def spread_column_kernel(
+    block_ref, small_ref, moved_ref, block_out, small_out, swapped,
+    held, local_sem, col_send, col_recv, held_sem, swap_send, swap_recv,
 ):
-    place, core, part, near, partner = relatives()
-    dp = place * 2 + core
-    columns = [lax.rem(part + step, 4) for step in range(1, 4)]
-    pairs = ((block_ref, out_ref), (small_ref, small_out))
+    place, _, part, near, _ = relatives()
+    bring = pltpu.make_async_copy(moved_ref.at[place], held, held_sem.at[0])
+    bring.start()
+    pairs = ((block_ref, block_out), (small_ref, small_out))
     locals_ = [
-        pltpu.make_async_copy(src, dst.at[dp, part], local_sem.at[which])
-        for which, (src, dst) in enumerate(pairs)
+        pltpu.make_async_copy(src, dst.at[part], local_sem.at[which]) for which, (src, dst) in enumerate(pairs)
     ]
     for copy in locals_:
         copy.start()
-    greet([(dp, other) for other in columns] + near[1:] + [partner])
-    first = [
+    greet(column_greets() + near[1:])
+    swaps = plane_moves(moved_ref, swapped, swap_send, swap_recv)
+    columns = [
+        push(src, dst.at[part], col_send.at[which, step], col_recv.at[which, step], other)
+        for which, (src, dst) in enumerate(pairs)
+        for step, other in enumerate(column_greets())
+    ]
+    for copy in swaps + columns:
+        copy.start()
+    bring.wait()
+    keep = pltpu.make_async_copy(held, swapped.at[place], held_sem.at[1])
+    keep.start()
+    for copy in locals_:
+        copy.wait()
+    keep.wait()
+    for copy in swaps + columns:
+        copy.wait()
+
+
+def spread_column(block, small, moved):
+    vmem_spec = pl.BlockSpec(memory_space=pltpu.VMEM)
+    return pl.pallas_call(
+        spread_column_kernel,
+        out_shape=(
+            jax.ShapeDtypeStruct((4,) + block.shape, block.dtype),
+            jax.ShapeDtypeStruct((4,) + small.shape, small.dtype),
+            jax.ShapeDtypeStruct(moved.shape, moved.dtype),
+        ),
+        in_specs=[vmem_spec, vmem_spec, ANY_SPEC],
+        out_specs=(ANY_SPEC,) * 3,
+        scratch_shapes=[
+            pltpu.VMEM(moved.shape[1:], moved.dtype),
+            DMA((2,)), DMA((2, 3)), DMA((2, 3)), DMA((2,)), DMA((3,)), DMA((3,)),
+        ],
+        compiler_params=comm_params(3),
+        name="spread_column",
+    )(block, small, moved)
+
+
+def spread_kernel(
+    block_ref, small_ref, moved_ref, block_out, small_out, swapped,
+    held, local_sem, near_send, near_recv, chip_send, chip_recv, held_sem, swap_send, swap_recv,
+):
+    place, core, _, near, partner = relatives()
+    dp = place * 2 + core
+    bring = pltpu.make_async_copy(moved_ref.at[place], held, held_sem.at[0])
+    bring.start()
+    pairs = ((block_ref, block_out), (small_ref, small_out))
+    locals_ = [
+        pltpu.make_async_copy(src, dst.at[dp], local_sem.at[which]) for which, (src, dst) in enumerate(pairs)
+    ]
+    for copy in locals_:
+        copy.start()
+    greet(near[1:] + [partner])
+    nears = [
         [
-            push(src, dst.at[dp, part], za_send.at[which, step], za_recv.at[which, step], (dp, other))
+            push(
+                src.at[at], dst.at[dp, at], near_send.at[at, which, step - 1], near_recv.at[at, which, step - 1],
+                near[step],
+            )
             for which, (src, dst) in enumerate(pairs)
+            for step in (1, 2, 3)
         ]
-        for step, other in enumerate(columns)
-    ]
-    for listed in first:
+        for at in range(4)
+    ]
+    chips = [
+        push(src.at[at], dst.at[dp, at], chip_send.at[at, which, 0], chip_recv.at[at, which, 0], partner)
+        for at in range(4)
+        for which, (src, dst) in enumerate(pairs)
+    ]
+    swaps = plane_moves(moved_ref, swapped, swap_send, swap_recv)
+    for listed in nears + [chips, swaps]:
         for copy in listed:
             copy.start()
+    bring.wait()
+    keep = pltpu.make_async_copy(held, swapped.at[place], held_sem.at[1])
+    keep.start()
+    for at in range(4):
+        for which, (_, dst) in enumerate(pairs):
+            for step in (1, 2, 3):
+                nears[at][which * 3 + step - 1].wait()
+                spot = dst.at[near[step][0], at]
+                chips.append(
+                    push(spot, spot, chip_send.at[at, which, step], chip_recv.at[at, which, step], partner)
+                )
+                chips[-1].start()
     for copy in locals_:
         copy.wait()
-    second = [[], [], [], []]
-    third = []
-
-    def start(listed, copy):
-        copy.start()
-        listed.append(copy)
-
-    for turn in range(4):
-        part_at = lax.rem(part + 4 - turn, 4)
-        if turn:
-            for copy in first[turn - 1]:
-                copy.wait()
-        for which, (_, dst) in enumerate(pairs):
-            spot = dst.at[dp, part_at]
-            for step in range(3):
-                start(
-                    second[turn],
-                    push(spot, spot, yx_send.at[turn, which, step], yx_recv.at[turn, which, step], near[step + 1]),
-                )
-            start(third, push(spot, spot, cc_send.at[turn, which, 0], cc_recv.at[turn, which, 0], partner))
-    for turn in range(4):
-        part_at = lax.rem(part + 4 - turn, 4)
-        for which, (_, dst) in enumerate(pairs):
-            for step in range(3):
-                second[turn][which * 3 + step].wait()
-                spot = dst.at[near[step + 1][0], part_at]
-                start(
-                    third,
-                    push(spot, spot, cc_send.at[turn, which, step + 1], cc_recv.at[turn, which, step + 1], partner),
-                )
-    for copy in third:
+    keep.wait()
+    for copy in chips + swaps:
         copy.wait()
 
 
-def spread(block, small):
+def spread(block, small, moved):
     vmem_spec = pl.BlockSpec(memory_space=pltpu.VMEM)
     return pl.pallas_call(
         spread_kernel,
         out_shape=(
-            jax.ShapeDtypeStruct((8, 4) + block.shape, block.dtype),
-            jax.ShapeDtypeStruct((8, 4) + small.shape, small.dtype),
+            jax.ShapeDtypeStruct((8,) + block.shape, block.dtype),
+            jax.ShapeDtypeStruct((8,) + small.shape, small.dtype),
+            jax.ShapeDtypeStruct(moved.shape, moved.dtype),
         ),
-        in_specs=[vmem_spec, vmem_spec],
-        out_specs=(ANY_SPEC, ANY_SPEC),
+        in_specs=[vmem_spec, vmem_spec, ANY_SPEC],
+        out_specs=(ANY_SPEC,) * 3,
         scratch_shapes=[
-            DMA((2,)), DMA((2, 3)), DMA((2, 3)), DMA((4, 2, 3)), DMA((4, 2, 3)), DMA((4, 2, 4)), DMA((4, 2, 4)),
+            pltpu.VMEM(moved.shape[1:], moved.dtype),
+            DMA((2,)), DMA((4, 2, 3)), DMA((4, 2, 3)), DMA((4, 2, 4)), DMA((4, 2, 4)), DMA((2,)), DMA((3,)), DMA((3,)),
         ],
         compiler_params=comm_params(1),
         name="spread",
-    )(block, small)
-
-
-def gather_sums_kernel(count, *refs):
-    ins, moved_ref, refs = refs[:count], refs[count], refs[count + 1 :]
-    outs, swapped, refs = refs[:count], refs[count], refs[count + 1 :]
-    sets = [(ins[which],) + refs[6 * which : 6 * which + 6] for which in range(count)]
-    held, *sems = refs[6 * count :]
-    local_sem, chip_send, chip_recv, near_send, near_recv, col_send, col_recv, held_sem, swap_send, swap_recv = sems
-    place, core, part, near, partner = relatives()
-    dp = place * 2 + core
-    columns = [lax.rem(part + step, 4) for step in range(1, 4)]
+    )(block, small, moved)
+
+
+def plane_sums_kernel(
+    src, moved_ref, out, swapped, own, chip, total, arrived, held,
+    local_sem, chip_send, chip_recv, near_send, near_recv, held_sem, swap_send, swap_recv,
+):
+    place, core, _, near, partner = relatives()
     spots = [place] + [near[step][0] // 2 for step in range(1, 4)]
-    order = (3, 1, 2, 0)
-    loads = {}
-    for which, (src, own, *_) in enumerate(sets):
-        for step in order:
-            loads[which, step] = pltpu.make_async_copy(
-                src.at[spots[step], core], own.at[step], local_sem.at[which, step]
-            )
-            loads[which, step].start()
+    load = pltpu.make_async_copy(src.at[:, core], own, local_sem.at[0])
+    load.start()
     bring = pltpu.make_async_copy(moved_ref.at[place], held, held_sem.at[0])
     bring.start()
-    greet([(dp, other) for other in columns] + near[1:] + [partner])
-    chips, nears, cols = {}, {}, {}
-    for which, (src, own, chip, *_) in enumerate(sets):
-        for step in order:
-            chips[which, step] = push(
-                src.at[spots[step], 1 - core], chip.at[step],
-                chip_send.at[which, step], chip_recv.at[which, step], partner,
-            )
-            chips[which, step].start()
-    swaps = [
-        push(
-            moved_ref.at[spots[step]], swapped.at[place], swap_send.at[step - 1], swap_recv.at[step - 1], near[step]
-        )
-        for step in (1, 2, 3)
-    ]
-    for copy in swaps:
+    greet(near[1:] + [partner])
+    across = push(src.at[:, 1 - core], chip, chip_send.at[0], chip_recv.at[0], partner)
+    across.start()
+    swaps = plane_moves(moved_ref, swapped, swap_send, swap_recv)
+    load.wait()
+    across.wait()
+    total[...] = own[...] + chip[...]
+    nears = [
+        push(total.at[spots[step]], arrived.at[step - 1], near_send.at[step - 1], near_recv.at[step - 1], near[step])
+        for step in (3, 1, 2)
+    ]
+    for copy in nears + swaps:
         copy.start()
     bring.wait()
     keep = pltpu.make_async_copy(held, swapped.at[place], held_sem.at[1])
     keep.start()
-    for which, (src, own, chip, total, arrived, *_) in enumerate(sets):
-        for step in order:
-            loads[which, step].wait()
-            chips[which, step].wait()
-            total[step] = (own[step].astype(f32) + chip[step].astype(f32)).astype(total.dtype)
-            if step:
-                nears[which, step] = push(
-                    total.at[step], arrived.at[step - 1],
-                    near_send.at[which, step - 1], near_recv.at[which, step - 1], near[step],
-                )
-                nears[which, step].start()
-    for which, (src, own, chip, total, arrived, column, partial_sum) in enumerate(sets):
-        for step in order[:3]:
-            nears[which, step].wait()
-        partial_sum[...] = (
-            total[0].astype(f32)
-            + arrived[0].astype(f32)
-            + arrived[1].astype(f32)
-            + arrived[2].astype(f32)
-        ).astype(partial_sum.dtype)
-        for step, other in enumerate(columns):
-            cols[which, step] = push(
-                partial_sum.at[other], column.at[step],
-                col_send.at[which, step], col_recv.at[which, step], (dp, other),
-            )
-            cols[which, step].start()
-    for which, out in enumerate(outs):
-        _, _, _, _, _, column, partial_sum = sets[which]
-        for step in range(3):
-            cols[which, step].wait()
-        out[...] = (
-            partial_sum[part].astype(f32)
-            + column[0].astype(f32)
-            + column[1].astype(f32)
-            + column[2].astype(f32)
-        )
+    for copy in nears:
+        copy.wait()
+    out[...] = total[place] + arrived[0] + arrived[1] + arrived[2]
     keep.wait()
     for copy in swaps:
         copy.wait()
 
 
-def gather_sums(arrays, moved):
-    count = len(arrays)
-    scratch = []
-    for array in arrays:
-        block = array.shape[2:]
-        for shape in ((4,) + block, (4,) + block, (4,) + block, (3,) + block, (3,) + block[1:], block):
-            scratch.append(pltpu.VMEM(shape, array.dtype))
+def plane_sums(array, moved):
+    block = array.shape[2:]
+    vmem = lambda lead: pltpu.VMEM((lead,) + block, f32)
+    return pl.pallas_call(
+        plane_sums_kernel,
+        out_shape=(jax.ShapeDtypeStruct(block, f32), jax.ShapeDtypeStruct(moved.shape, moved.dtype)),
+        in_specs=[ANY_SPEC] * 2,
+        out_specs=(pl.BlockSpec(memory_space=pltpu.VMEM), ANY_SPEC),
+        scratch_shapes=[
+            vmem(4), vmem(4), vmem(4), vmem(3), pltpu.VMEM(moved.shape[1:], moved.dtype),
+            DMA((1,)), DMA((1,)), DMA((1,)), DMA((3,)), DMA((3,)), DMA((2,)), DMA((3,)), DMA((3,)),
+        ],
+        compiler_params=comm_params(2),
+        name="plane_sums",
+    )(array, moved)
+
+
+def finish_kernel(count, *refs):
+    parts, moved_ref, sums, swapped = refs[:count], refs[count], refs[count + 1 : 2 * count + 1], refs[2 * count + 1]
+    columns, rest = refs[2 * count + 2 : 3 * count + 2], refs[3 * count + 2 :]
+    held, col_send, col_recv, held_sem, swap_send, swap_recv = rest
+    place, _, _, near, _ = relatives()
+    bring = pltpu.make_async_copy(moved_ref.at[place], held, held_sem.at[0])
+    bring.start()
+    greet(column_greets() + near[1:])
+    swaps = plane_moves(moved_ref, swapped, swap_send, swap_recv)
+    copies = [
+        column_copies(parts[which], columns[which], col_send.at[which], col_recv.at[which]) for which in range(count)
+    ]
+    for listed in [swaps] + copies:
+        for copy in listed:
+            copy.start()
+    bring.wait()
+    keep = pltpu.make_async_copy(held, swapped.at[place], held_sem.at[1])
+    keep.start()
+    for which in range(count):
+        for copy in copies[which]:
+            copy.wait()
+        sums[which][...] = column_sum(parts[which], columns[which])
+    keep.wait()
+    for copy in swaps:
+        copy.wait()
+
+
+def finish(parts, moved):
+    count = len(parts)
     vmem_spec = pl.BlockSpec(memory_space=pltpu.VMEM)
     return pl.pallas_call(
-        partial(gather_sums_kernel, count),
-        out_shape=tuple(jax.ShapeDtypeStruct(array.shape[3:], f32) for array in arrays)
+        partial(finish_kernel, count),
+        out_shape=tuple(jax.ShapeDtypeStruct(each.shape[1:], f32) for each in parts)
         + (jax.ShapeDtypeStruct(moved.shape, moved.dtype),),
-        in_specs=[ANY_SPEC] * (count + 1),
+        in_specs=[vmem_spec] * count + [ANY_SPEC],
         out_specs=(vmem_spec,) * count + (ANY_SPEC,),
-        scratch_shapes=scratch
-        + [pltpu.VMEM(moved.shape[1:], moved.dtype)]
-        + [DMA((count, 4))] * 3 + [DMA((count, 3))] * 4 + [DMA((2,)), DMA((3,)), DMA((3,))],
-        compiler_params=comm_params(2),
-        name="gather_sums",
-    )(*arrays, moved)
+        scratch_shapes=[pltpu.VMEM((3,) + each.shape[1:], each.dtype) for each in parts]
+        + [
+            pltpu.VMEM(moved.shape[1:], moved.dtype),
+            DMA((count, 3)), DMA((count, 3)), DMA((2,)), DMA((3,)), DMA((3,)),
+        ],
+        compiler_params=comm_params(6),
+        name="finish",
+    )(*parts, moved)
 
 
 def standard(rows):
@@ -748,9 +772,6 @@
     scores = nt(query, key) * (HD ** (-0.5))
     slots = lax.broadcasted_iota(jnp.int32, scores.shape, 1)
     return jnp.where(slots < LEN, scores, far_negative)
-
-
-WGRAD_SPEC = pl.BlockSpec((8, 1, D // 8, D), lambda turn: (0, turn, 0, 0))
 
 
 def weight_spec(layer):
@@ -843,10 +864,42 @@
 def attend_pull_kernel(
     grad_ref, moved_ref, hidden_ref, resid_ref, saved_ref, table_ref, logs_ref, dprob_ref,
     weight_ref, vec_ref, router_ref,
-    out_ref, wgrad_ref, small_ref, rgrad_ref,
+    out_ref, partial_ref, small_ref, rgrad_ref,
     first_sc, grad_sc, low_sc, back_sc,
+    mine, chip, total, arrived, chip_send, chip_recv, near_send, near_recv,
 ):
     turn = pl.program_id(0)
+    place, core, _, near, partner = relatives()
+    spots = [place] + [near[step][0] // 2 for step in range(1, 4)]
+
+    def chip_copy(at):
+        return push(mine.at[at, :, 1 - core], chip.at[at], chip_send.at[at], chip_recv.at[at], partner)
+
+    def near_copies(at):
+        return [
+            push(
+                total.at[at, spots[step]], arrived.at[at, step - 1],
+                near_send.at[at, step - 1], near_recv.at[at, step - 1], near[step],
+            )
+            for step in (3, 1, 2)
+        ]
+
+    def after_chip(at):
+        chip_copy(at).wait()
+        total[at] = mine[at, :, core] + chip[at]
+        for copy in near_copies(at):
+            copy.start()
+
+    def after_near(at):
+        for copy in near_copies(at):
+            copy.wait()
+        partial_ref[at] = (
+            total[at, place].astype(f32)
+            + arrived[at, 0].astype(f32)
+            + arrived[at, 1].astype(f32)
+            + arrived[at, 2].astype(f32)
+        ).astype(bf16)
+
     rows_all = grad_ref.shape[0]
     images = rows_all // SEQ
     weight = weight_ref[:, 0, 0].reshape(D, D)
@@ -854,6 +907,7 @@
 
     @pl.when(turn == 0)
     def _():
+        greet(near[1:] + [partner])
         normed, inv_std = standard(resid_ref[...])
         second = (normed * vec_ref[2:3] + vec_ref[3:4]).astype(bf16)
         lanes = lax.broadcasted_iota(jnp.int32, (rows_all, 128), 1)
@@ -898,22 +952,37 @@
         mixed = jnp.concatenate(pieces[0] + pieces[1] + pieces[2], axis=1)
         back_sc[rows, :] += nt(mixed, weight[:, :QKV])
         mixed_grads.append(mixed)
+        if image == 0:
+
+            @pl.when(turn > 0)
+            def _():
+                after_chip(turn - 1)
+
     mixed = jnp.concatenate(mixed_grads, axis=0)
     wgrad = jnp.concatenate([tn(first_sc[...], mixed), tn(low_sc[...], saved_ref[0, :, QKV:])], axis=1)
-    wgrad_ref[:, 0] = wgrad.astype(bf16).reshape(8, D // 8, D)
-
-    @pl.when(turn == pl.num_programs(0) - 1)
+    mine[turn] = wgrad.astype(bf16).reshape(4, 2, D // 8, D)
+    chip_copy(turn).start()
+
+    @pl.when(turn > 1)
     def _():
+        after_near(turn - 2)
+
+    @pl.when(turn == 3)
+    def _():
+        after_chip(3)
         dfirst = back_sc[...]
         normed, inv_std = standard(hidden_ref[...].astype(f32))
         small_ref[0:1] = jnp.sum(dfirst * normed, axis=0, keepdims=True)
         small_ref[1:2] = jnp.sum(dfirst, axis=0, keepdims=True)
         small_ref[4:8] = jnp.zeros((4, D), f32)
         out_ref[...] = grad_sc[...] + norm_pull(dfirst, normed, inv_std, vec_ref[0:1])
+        after_near(2)
+        after_near(3)
 
 
 def attend_pull(grad, moved, hidden, resid, saved, table, logs, dprob, weights, vecs, router, layer):
     rows = grad.shape[0]
+    block = (D // 8, D)
     whole = lambda shape: pl.BlockSpec(shape, lambda turn: (0,) * len(shape))
     by_part = lambda shape: pl.BlockSpec((1,) + shape, lambda turn: (turn, 0, 0))
     return pl.pallas_call(
@@ -924,18 +993,21 @@
             by_part((rows, D)), whole((rows, 128)), by_part((rows, 128)), whole((rows, 128)),
             weight_spec(layer), whole((8, D)), whole((D, 128)),
         ],
-        out_specs=(whole((rows, D)), WGRAD_SPEC, whole((8, D)), whole((D, 128))),
+        out_specs=(whole((rows, D)), whole((4,) + block), whole((8, D)), whole((D, 128))),
         out_shape=(
             jax.ShapeDtypeStruct((rows, D), f32),
-            jax.ShapeDtypeStruct((8, 4, D // 8, D), bf16),
+            jax.ShapeDtypeStruct((4,) + block, bf16),
             jax.ShapeDtypeStruct((8, D), f32),
             jax.ShapeDtypeStruct((D, 128), f32),
         ),
         scratch_shapes=[
             pltpu.VMEM((rows, D), bf16), pltpu.VMEM((rows, D), f32),
             pltpu.VMEM((rows, D), bf16), pltpu.VMEM((rows, D), f32),
+            pltpu.VMEM((4, 4, 2) + block, bf16), pltpu.VMEM((4, 4) + block, bf16),
+            pltpu.VMEM((4, 4) + block, bf16), pltpu.VMEM((4, 3) + block, bf16),
+            DMA((4,)), DMA((4,)), DMA((4, 3)), DMA((4, 3)),
         ],
-        compiler_params=pltpu.CompilerParams(vmem_limit_bytes=VMEM_LIMIT),
+        compiler_params=comm_params(8 + layer),
         name="attend_pull",
     )(grad, moved, hidden, resid, saved, table, logs, dprob, weights, vecs, router)
 
@@ -960,7 +1032,7 @@
 
 
 def expert_kernel(
-    second_ref, pieces_ref, after_ref, rows_out, back_out, weights_out, act_out, slope_out,
+    second_ref, pieces_ref, rows_out, back_out, weights_out, act_out, slope_out,
     held, weights, made, acts, slopes, total,
     load_sem, join_send, join_recv, row_send, row_recv, pass_send, pass_recv, back_send, back_recv, out_sem, save_sem,
 ):
@@ -1062,13 +1134,13 @@
         copy.wait()
 
 
-def expert_rows(second, pieces, after):
+def expert_rows(second, pieces):
     count = second.shape[0]
     block = (count, D)
     weight_shape = (2, 16, 2, D // 8, D)
     return pl.pallas_call(
         expert_kernel,
-        in_specs=[ANY_SPEC] * 3,
+        in_specs=[ANY_SPEC] * 2,
         out_specs=(ANY_SPEC,) * 5,
         out_shape=(
             jax.ShapeDtypeStruct((4,) + block, bf16),
@@ -1089,7 +1161,7 @@
         ],
         compiler_params=comm_params(4),
         name="expert_rows",
-    )(second, pieces, after)
+    )(second, pieces)
 
 
 def expert_pull_kernel(
@@ -1280,13 +1352,12 @@
     small = jnp.concatenate([norm_gain, norm_bias, w_router])
     small = jnp.pad(small, (0, 2048 - small.shape[0])).reshape(16, 128)
 
-    def expert_pieces(layer, after):
-        packed = jnp.stack([w_in[layer], w_back[layer]], axis=1)
-        arrived = swap(packed, "plane", False, 3 + 4 * layer, after)
-        return arrived, lax.all_gather(arrived, "tensor", axis=0, tiled=True)
-
-    pieces = [expert_pieces(0, small), None]
-    attn_all, small_all = spread(attn_blocks, small)
+    packed = [jnp.stack([w_in[layer], w_back[layer]], axis=1) for layer in range(LAYERS)]
+    blocks_column, small_column, swapped_first = spread_column(attn_blocks, small, packed[0])
+    attn_all, small_all, swapped_later = spread(blocks_column, small_column, packed[1])
+    pieces = [
+        lax.all_gather(swapped, "tensor", axis=0, tiled=True) for swapped in (swapped_first, swapped_later)
+    ]
     flat = small_all.reshape(32, 2048)
     vec_count = LAYERS * 2 * D // 32
     gains = flat[:, :vec_count].reshape(LAYERS, 2, D).astype(f32)
@@ -1302,10 +1373,7 @@
     stats = []
     for layer in range(LAYERS):
         resid, second, saved, table, logs = attend_rows(hidden, attn_all, vecs[layer], routers[layer], layer)
-        if layer + 1 < LAYERS:
-            pieces[layer + 1] = expert_pieces(layer + 1, second)
-        after = pieces[min(layer + 1, LAYERS - 1)][0]
-        rows, back, weights, act, slope = expert_rows(second, pieces[layer][1], after)
+        rows, back, weights, act, slope = expert_rows(second, pieces[layer])
         gates = jnp.where(chosen[layer], by_place(table[:, :EXPERTS]), 0.0)
         moe = sum(gates[:, at : at + 1] * back[at].astype(f32) for at in range(EXPERTS))
         result = resid + moe
@@ -1333,10 +1401,10 @@
         moved, wgrad = expert_pull(sent, rows, act, slope, weights)
         summed = lax.psum_scatter(wgrad, "tensor", scatter_dimension=0, tiled=False)
         owned.append(summed)
-        grad, attn_wgrad, small_grad, router_grad = attend_pull(
+        grad, attn_part, small_grad, router_grad = attend_pull(
             grad, moved, before, resid, saved, table, logs, dprob, attn_all, vecs[layer], routers[layer], layer
         )
-        attn_grads.append(attn_wgrad.reshape(4, 2, 4, slices, D))
+        attn_grads.append(attn_part)
         small_grads.append(small_grad[:4])
         router_grads.append(router_grad[:, :EXPERTS])
     for listed in (small_grads, router_grads, owned):
@@ -1353,8 +1421,9 @@
         axis=1,
     )
     packed = jnp.pad(packed, ((0, 0), (0, 1024 - packed.shape[1]))).reshape(4, 2, 4, 8, 128)
-    *attn_grads, total, moved_later = gather_sums(attn_grads + [packed], owned[1])
-    attn_grad = jnp.stack(attn_grads[::-1])
+    small_part, moved_later = plane_sums(packed, owned[1])
+    *attn_grads, total, moved_first = finish(attn_grads[::-1] + [small_part], owned[0])
+    attn_grad = jnp.stack(attn_grads)
     total = total.reshape(-1)
     share = LAYERS * 2 * D // 32
     router_share = LAYERS * D * EXPERTS // 32
@@ -1363,7 +1432,6 @@
     rms = jnp.sqrt(total[at : at + 3 * LAYERS].reshape(LAYERS, 3) / denom)
     qkv_grad = jnp.transpose(attn_grad[:, :, :QKV].reshape(LAYERS, slices, 3, QKV // 3), (0, 2, 1, 3))
     out_grad = jnp.transpose(attn_grad[:, :, QKV:], (0, 2, 1))
-    moved_first = swap(owned[0], "plane", False, 6, moved_later)
     expert_grad = jnp.stack([moved_first, moved_later], axis=1).astype(f32)
     expert_grad = jnp.transpose(expert_grad, (2, 1, 0, 3, 4))
     return (

time: 680 us -> 654 us (0.962)
  Pallas kernels: 593 us -> 571 us
    pallas_call x7 -> x6, Pallas kernels: 349 us -> 296 us  [the longest x2 140 us: expert_rows(): pl.pallas_call(expert_kernel, in_specs=[ANY_SPEC] * 2, out_specs=(ANY_SPE...]
    pallas_call x2, Pallas kernels: 61.2 us -> 92.5 us  [attend_pull(): pl.pallas_call(attend_pull_kernel, grid=(4,), in_specs=[whole((rows, D)),...]
    all_gather x2, waiting for transfers between devices: 7.47 us -> 0.04 us  [per_device(): lax.all_gather(swapped, 'tensor', axis=0, tiled=True)]
  transfers between devices with their start and end apart: 4 -> 4, of which waited for: 2 -> 1; matrix products, arithmetic and copies ran while one was open for 6% -> 5% of each run, Pallas kernels for 61% -> 55%
where the time goes in v4:
time: 654 us; the launch traced here: 651 us
  Pallas kernels  571 us (87%)
  other arithmetic  34.5 us (5%)
  local copies, waits for them, and re-layouts  24.3 us (4%)
  between operations  15.2 us (2%)
    pallas_call x2, Pallas kernels, expert_pull(): pl.pallas_call(expert_pull_kernel, in_specs=[ANY_SPEC] * 5, out_specs=(AN...  151 us
    pallas_call x2, Pallas kernels, expert_rows(): pl.pallas_call(expert_kernel, in_specs=[ANY_SPEC] * 2, out_specs=(ANY_SPE...  140 us
    pallas_call x2, Pallas kernels, attend_pull(): pl.pallas_call(attend_pull_kernel, grid=(4,), in_specs=[whole((rows, D)),...  92.5 us
    pallas_call x1, Pallas kernels, spread(): pl.pallas_call(spread_kernel, out_shape=(jax.ShapeDtypeStruct((8,) + bloc...  69.5 us
    pallas_call x1, Pallas kernels, spread_column(): pl.pallas_call(spread_column_kernel, out_shape=(jax.ShapeDtypeStruct((4,)...  33.8 us
    pallas_call x1, Pallas kernels, finish(): pl.pallas_call(partial(finish_kernel, count), out_shape=tuple((jax.ShapeD...  33.5 us
    pallas_call x2, Pallas kernels, attend_rows(): pl.pallas_call(attend_kernel, grid=(4,), in_specs=[whole((rows, D)), weig...  30.7 us
    pallas_call x1, Pallas kernels, plane_sums(): pl.pallas_call(plane_sums_kernel, out_shape=(jax.ShapeDtypeStruct(block,...  19.4 us
  transfers between devices with their start and end apart: 4, of which 1 were waited for; matrix products, arithmetic and copies ran while one was open for 5% of the time, Pallas kernels for 55%

profile of v4, /device:TPU:0, one launch (start us, length us, event | category | flops | bytes accessed | tf_op | source)
XLA Modules:
  0.0 650.9 jit_solution(779656759454974886)
XLA Ops:
  12.3 1.6 pad_maximum_fusion.2
  14.0 33.8 %spread_column.1 = (bf16[4,2,96,768]{3,2,1,0:T(8,128)(2,1)}, bf16[4,16,128]{2,1,0:T(8,128)(2,1)}, bf16[4,2,96,768]{3,2,1,0:T(8,128)(2,1)}) custom-call(bf16[2,96,768]{2,1,0:T(8,128)(2,1)} %pad_maximum_fusion.5.block_ref, bf16[16,128]{1,0:T(8,128)(2,1)} %fusion.45.small_ref, bf16[4,2,96,768]{3,2,1,0:T(8,128)(2,1)} %get-tuple-element.191.moved_ref), custom_call_target="tpu_custom_call" | custom-call | tf_op jit(solution)/shard_map/spread_column/pallas_call | solution.py:571
  47.9 69.5 %spread.1 = (bf16[8,4,2,96,768]{4,3,2,1,0:T(8,128)(2,1)}, bf16[8,4,16,128]{3,2,1,0:T(8,128)(2,1)}, bf16[4,2,96,768]{3,2,1,0:T(8,128)(2,1)}) custom-call(bf16[4,2,96,768]{3,2,1,0:T(8,128)(2,1)} %get-tuple-element.54.block_ref, bf16[4,16,128]{2,1,0:T(8,128)(2,1)} %get-tuple-element.55.small_ref, bf16[4,2,96,768]{3,2,1,0:T(8,128)(2,1)} %get-tuple-element.192.moved_ref), custom_call_target="tpu_custom_call" | custom-call | tf_op jit(solution)/shard_map/spread/pallas_call | solution.py:645
  120.9 15.2 %attend_rows.2 = (f32[512,768]{1,0:T(8,128)}, bf16[512,768]{1,0:T(8,128)(2,1)}, bf16[4,512,768]{2,1,0:T(8,128)(2,1)}, f32[512,128]{1,0:T(8,128)}, f32[4,512,128]{2,1,0:T(8,128)}) custom-call(bf16[512,768]{1,0:T(8,128)(2,1)} %hidden_ref.3, bf16[8,4,2,96,768]{4,3,2,1,0:T(8,128)(2,1)} %get-tuple-element.56.weight_ref, f32[8,768]{1,0:T(8,128)} %get-tuple-element.176.vec_ref, ...), custom_call_target="tpu_custom_call" | custom-call | tf_op jit(solution)/shard_map/attend_rows/pallas_call | solution.py:837
  139.0 70.4 %expert_rows.2 = (bf16[4,512,768]{2,1,0:T(8,128)(2,1)}, bf16[4,512,768]{2,1,0:T(8,128)(2,1)}, bf16[2,16,2,96,768]{4,3,2,1,0:T(8,128)(2,1)}, bf16[4,2048,768]{2,1,0:T(8,128)(2,1)}, bf16[4,2048,768]{2,1,0:T(8,128)(2,1)}) custom-call(bf16[512,768]{1,0:T(8,128)(2,1)} %get-tuple-element.60.second_ref, bf16[16,2,96,768]{3,2,1,0:T(8,128)(2,1)} %all-gather.3.cloned.1.call-done.pieces_ref), custom_call_target="tpu_custom_call" | custom-call | tf_op jit(solution)/shard_map/expert_rows/pallas_call | solution.py:1141
  209.4 4.7 fusion.53
  214.0 15.4 %attend_rows.3 = (f32[512,768]{1,0:T(8,128)}, bf16[512,768]{1,0:T(8,128)(2,1)}, bf16[4,512,768]{2,1,0:T(8,128)(2,1)}, f32[512,128]{1,0:T(8,128)}, f32[4,512,128]{2,1,0:T(8,128)}) custom-call(f32[512,768]{1,0:T(8,128)} %get-tuple-element.154.hidden_ref, bf16[8,4,2,96,768]{4,3,2,1,0:T(8,128)(2,1)} %get-tuple-element.56.weight_ref, ...), custom_call_target="tpu_custom_call" | custom-call | tf_op jit(solution)/shard_map/attend_rows/pallas_call | solution.py:837
  230.7 69.7 %expert_rows.3 = (bf16[4,512,768]{2,1,0:T(8,128)(2,1)}, bf16[4,512,768]{2,1,0:T(8,128)(2,1)}, bf16[2,16,2,96,768]{4,3,2,1,0:T(8,128)(2,1)}, bf16[4,2048,768]{2,1,0:T(8,128)(2,1)}, bf16[4,2048,768]{2,1,0:T(8,128)(2,1)}) custom-call(bf16[512,768]{1,0:T(8,128)(2,1)} %get-tuple-element.65.second_ref, bf16[16,2,96,768]{3,2,1,0:T(8,128)(2,1)} %all-gather.5.cloned.1.call-done.pieces_ref), custom_call_target="tpu_custom_call" | custom-call | tf_op jit(solution)/shard_map/expert_rows/pallas_call | solution.py:1141
  300.4 6.5 fusion.14
  306.9 1.8 pad_maximum_fusion.sent_ref
  308.7 75.7 %expert_pull.2 = (bf16[4,512,768]{2,1,0:T(8,128)(2,1)}, bf16[4,4,2,96,768]{4,3,2,1,0:T(8,128)(2,1)}) custom-call(bf16[4,512,768]{2,1,0:T(8,128)(2,1)} %pad_maximum_fusion.sent_ref, bf16[4,512,768]{2,1,0:T(8,128)(2,1)} %get-tuple-element.68.rows_ref, bf16[4,2048,768]{2,1,0:T(8,128)(2,1)} %get-tuple-element.69.act_ref, ...), custom_call_target="tpu_custom_call" | custom-call | tf_op jit(solution)/shard_map/expert_pull/pallas_call | solution.py:1299
  385.5 45.8 %attend_pull.2 = (f32[512,768]{1,0:T(8,128)}, bf16[4,96,768]{2,1,0:T(8,128)(2,1)}, f32[8,768]{1,0:T(8,128)}, f32[768,128]{1,0:T(8,128)}) custom-call(f32[512,768]{1,0:T(8,128)} %get-tuple-element.166.grad_ref, bf16[4,512,768]{2,1,0:T(8,128)(2,1)} %get-tuple-element.72.moved_ref, f32[512,768]{1,0:T(8,128)} %get-tuple-element.154.hidden_ref, ...), custom_call_target="tpu_custom_call" | custom-call | tf_op jit(solution)/shard_map/attend_pull/pallas_call | solution.py:988
  431.4 3.1 fusion.22
  434.9 2.0 pad_maximum_fusion.1.sent_ref
  436.9 75.7 %expert_pull.3 = (bf16[4,512,768]{2,1,0:T(8,128)(2,1)}, bf16[4,4,2,96,768]{4,3,2,1,0:T(8,128)(2,1)}) custom-call(bf16[4,512,768]{2,1,0:T(8,128)(2,1)} %pad_maximum_fusion.1.sent_ref, bf16[4,512,768]{2,1,0:T(8,128)(2,1)} %get-tuple-element.76.rows_ref, bf16[4,2048,768]{2,1,0:T(8,128)(2,1)} %get-tuple-element.77.act_ref, ...), custom_call_target="tpu_custom_call" | custom-call | tf_op jit(solution)/shard_map/expert_pull/pallas_call | solution.py:1299
  516.5 46.7 %attend_pull.3 = (f32[512,768]{1,0:T(8,128)}, bf16[4,96,768]{2,1,0:T(8,128)(2,1)}, f32[8,768]{1,0:T(8,128)}, f32[768,128]{1,0:T(8,128)}) custom-call(f32[512,768]{1,0:T(8,128)} %get-tuple-element.75.grad_ref, bf16[4,512,768]{2,1,0:T(8,128)(2,1)} %get-tuple-element.80.moved_ref, bf16[512,768]{1,0:T(8,128)(2,1)} %hidden_ref.3, ...), custom_call_target="tpu_custom_call" | custom-call | tf_op jit(solution)/shard_map/attend_pull/pallas_call | solution.py:988
  566.6 2.0 maximum_bitcast_fusion.1
  568.6 2.0 maximum_bitcast_fusion
  571.5 19.4 %plane_sums.1 = (f32[4,8,128]{2,1,0:T(8,128)}, bf16[4,2,96,768]{3,2,1,0:T(8,128)(2,1)}) custom-call(f32[4,2,4,8,128]{4,3,2,1,0:T(8,128)} %bitcast.169, bf16[4,2,96,768]{3,2,1,0:T(8,128)(2,1)} %bitcast.162), custom_call_target="tpu_custom_call" | custom-call | tf_op jit(solution)/shard_map/plane_sums/pallas_call | solution.py:700
  591.0 5.6 reduce-scatter.5.cloned.1.call-done
  596.5 33.5 %finish.1 = (f32[96,768]{1,0:T(8,128)}, f32[96,768]{1,0:T(8,128)}, f32[8,128]{1,0:T(8,128)}, bf16[4,2,96,768]{3,2,1,0:T(8,128)(2,1)}) custom-call(bf16[4,96,768]{2,1,0:T(8,128)(2,1)} %get-tuple-element.84.refs_0_, bf16[4,96,768]{2,1,0:T(8,128)(2,1)} %get-tuple-element.85.refs_1_, f32[4,8,128]{2,1,0:T(8,128)} %get-tuple-element.91.refs_2_, ...), custom_call_target="tpu_custom_call" | custom-call | tf_op jit(solution)/shard_map/finish/pallas_call | solution.py:744
  633.8 1.9 fusion.37
  637.0 1.7 copy.56
  639.1 2.6 slice_bitcast_fusion
  (119 shorter events, 29.3 us)
Async XLA Ops:
  7.2 131.4 %copy-start = (s32[2,2048,2]{1,2,0:T(2,128)S(1)}, s32[2,2048,2]{1,2,0:T(2,128)}, u32[]{:S(2)}) copy-start(s32[2,2048,2]{1,2,0:T(2,128)} %param.13) | copy-start | bytes 98308
  7.2 2.5 copy-start.7
  7.2 131.8 %all-gather.3.cloned.1.call-start = ((), (), s32[]{:S(2)}) async-start(), calls=%async_computation.2 | async-start | bytes 5898240 | tf_op jit(solution)/shard_map/all_gather | solution.py:1359
  9.5 1.3 copy-start.8
  10.8 0.9 copy-start.13
  10.8 0.9 copy-start.14
  10.8 0.9 copy-start.15
  47.8 182.9 %all-gather.5.cloned.1.call-start = ((), (), s32[]{:S(2)}) async-start(), calls=%async_computation.3 | async-start | bytes 5898240 | tf_op jit(solution)/shard_map/all_gather | solution.py:1359
  117.4 454.1 %reduce-scatter.3.cloned.1.call-start = ((), (), s32[]{:S(2)}) async-start(), calls=%async_computation.4 | async-start | bytes 5898240 | tf_op jit(solution)/shard_map/reduce_scatter | solution.py:1402
  120.9 16.3 %copy-start.16 = (s32[8]{0:T(128)S(1)}, s32[8]{0:T(128)}, u32[]{:S(2)}) copy-start(s32[8]{0:T(128)} %param.12) | copy-start | bytes 100
  230.7 69.7 %copy-start.9 = (bf16[512,768]{1,0:T(8,128)(2,1)S(1)}, bf16[512,768]{1,0:T(8,128)(2,1)}, u32[]{:S(2)}) copy-start(bf16[512,768]{1,0:T(8,128)(2,1)} %param.21) | copy-start | bytes 2359300
  384.5 212.1 %reduce-scatter.5.cloned.1.call-start = ((), (), s32[]{:S(2)}) async-start(), calls=%async_computation.5 | async-start | bytes 5898240 | tf_op jit(solution)/shard_map/reduce_scatter | solution.py:1402
  512.6 1.3 copy-start.2
  516.5 46.7 %copy-start.10 = (f32[768,128]{1,0:T(8,128)S(1)}, f32[768,128]{1,0:T(8,128)}, u32[]{:S(2)}) copy-start(f32[768,128]{1,0:T(8,128)} %get-tuple-element.89) | copy-start | bytes 1179652
  563.2 1.5 copy-start.12
  563.2 1.5 copy-start.11
  563.2 1.8 copy-start.3
  633.8 5.0 copy-start.5
  633.8 4.9 copy-start.6
  639.1 4.0 copy-start.4
  643.0 1.1 copy-start.1
Sparse Core Ops, SparseCore 0:
  47.9 88.5 all-gather.2
  138.1 87.7 all-gather.4
  384.6 83.9 reduce-scatter.2
  512.8 83.7 reduce-scatter.4
